TPU v7x, 256 devices: a whole 4x4x8 slice. The times are simulated.
256 devices in a mesh: seq: 16 (over x, y_hi, core), fsdp: 16 (over y_lo, z).
Axes of the slice: x: 4, y: 4 (y_hi: 2, y_lo: 2; y = y_hi * 2 + y_lo), z: 8, core: 2. Of those that a mesh axis runs over, the one named last changes fastest.
Arguments:
- tokens: bfloat16 [16384, 4096], P('seq', 'fsdp'), may hold values from -6 to 6
- norm_gain: bfloat16 [4096], replicated, may hold values from 0.25 to 1.75
- in_weight: bfloat16 [3, 4096, 4096], P(None, 'seq', 'fsdp'), may hold values from -0.09375 to 0.09375
- short_filter: bfloat16 [7, 3, 4096], P(None, None, 'fsdp'), may hold values from -2 to 2
- medium_filter: bfloat16 [128, 4096], P(None, 'fsdp'), may hold values from -0.5 to 0.5
- out_weight: bfloat16 [4096, 4096], P(None, ('fsdp', 'seq')), may hold values from -0.375 to 0.375
- genome_lengths: int32 [4], replicated, may hold values from 1 to 8192, 16384 in all
- block_at_slot: int32 [64], replicated, may hold values from 0 to 63, each once
Outputs:
- layer_out: bfloat16 [16384, 4096], P('seq', 'fsdp')
Inputs may be any that keep to these rules, and one draw needn't show every extreme that they name: `genome_lengths`: the lengths sum to 16384. `block_at_slot`: every block number appears exactly once.
All inputs are finite; a program needn't handle non-finite values.
Results may differ from a plain program's by a relative error of at most 0.0087.
Values may be sent and summed in bfloat16 or wider, within the bound.
No kernel may reach another device: no remote copies, remote signals or barrier semaphores. Data moves between devices by JAX's collectives and lax.ppermute only.
A program may use at most 64 MiB of HBM per device.

v0:
```python
import functools

import jax
import jax.numpy as jnp
from jax import lax
from jax.experimental import pallas as pl
from jax.experimental.pallas import tpu as pltpu
from jax.sharding import PartitionSpec as P


BLK = 256
SHORT = 7
MED = 128
LANES = 128
TAIL = 8
HALF = 512
PIECE = 256
D = 4096
HALO = MED + 3 * TAIL
AXES = ("seq", "fsdp")
epsilon = 1e-06


def linear(x, y, z, core):
    return (x * 4 + (y // 2) * 2 + core) * 16 + (y % 2) * 8 + z


def permutation(move):
    pairs = []
    for x in range(4):
        for y in range(4):
            for z in range(8):
                for core in range(2):
                    pairs.append((linear(x, y, z, core), linear(*move(x, y, z, core))))
    return pairs


def send(value, move):
    return lax.ppermute(value, AXES, permutation(move))


def along_x(step):
    return lambda x, y, z, core: ((x + step) % 4, y, z, core)


def along_y(step):
    return lambda x, y, z, core: (x, (y + step) % 4, z, core)


def swap_y(x, y, z, core):
    return (x, y ^ 1, z, core)


def swap_core(x, y, z, core):
    return (x, y, z, core ^ 1)


def gather_line(value):
    groups = [
        [linear(x, y, z, core) for z in range(8) for core in range(2)]
        for x in range(4)
        for y in range(4)
    ]
    return lax.all_gather(value, AXES, axis=0, axis_index_groups=groups)


def axis_of(chunk, along):
    return [chunk] + [send(chunk, along(-d)) for d in range(1, 4)]


def anywhere():
    return pl.BlockSpec(memory_space=pl.ANY)


def full():
    return pl.BlockSpec(memory_space=pltpu.VMEM)


def scalars():
    return pl.BlockSpec(memory_space=pltpu.SMEM)


def project_kernel(place_ref, line_ref, *refs):
    weights = refs[:8]
    out_ref, x_scratch, s_scratch, w_scratch, total, x_sems, s_sems, w_sems = refs[8:]
    x, y, core, y_low = place_ref[0], place_ref[1], place_ref[2], place_ref[3]

    def copies(i):
        made = []
        z, group = i // 2, lax.rem(i, 2)
        source = z * 2 + lax.rem(core + group, 2)
        rows = pl.ds(pl.multiple_of(group * HALF, HALF), HALF)
        for p in range(2):
            lanes = pl.ds(pl.multiple_of((z * 2 + p) * PIECE, PIECE), PIECE)
            made.append(
                pltpu.make_async_copy(
                    line_ref.at[source, p, pl.ds(0, HALF)], x_scratch.at[rows, lanes], x_sems.at[p, i]
                )
            )
            made.append(
                pltpu.make_async_copy(
                    line_ref.at[source, p, pl.ds(HALF, TAIL)], s_scratch.at[group, z * 2 + p],
                    s_sems.at[p, i],
                )
            )
        return made

    def start(i, carry):
        for copy in copies(i):
            copy.start()
        return carry

    def finish(i, carry):
        for copy in copies(i):
            copy.wait()
        return carry

    started = []
    for other in range(2):
        for a in range(4):
            for b in range(4):
                dx, dy = (b, a) if other == 0 else (a, b)
                to_x, to_y = lax.rem(x + dx, 4), lax.rem(y + dy, 4)
                owner = to_x * 4 + (to_y // 2) * 2 + lax.rem(core + other, 2)
                turn = lax.rem(owner, 8) * 2 + lax.rem(owner // 8 + y_low, 2)
                rows = pl.ds(pl.multiple_of(turn * PIECE, PIECE), PIECE)
                lanes = pl.ds(pl.multiple_of(lax.rem(to_y, 2) * LANES, LANES), LANES)
                started.append(
                    pltpu.make_async_copy(
                        weights[other * 4 + a].at[b],
                        w_scratch.at[:, rows, lanes],
                        w_sems.at[other, a, b],
                    )
                )
    for copy in started:
        copy.start()
    lax.fori_loop(0, 16, start, 0)
    for copy in started:
        copy.wait()

    def half(part, carry):
        lax.fori_loop(part * 8, part * 8 + 8, finish, 0)
        depth = pl.ds(pl.multiple_of(part * (D // 2), D // 2), D // 2)

        def step(i, carry):
            branch, group = i // 2, lax.rem(i, 2)
            rows = pl.ds(pl.multiple_of(group * HALF, HALF), HALF)
            product = jnp.dot(
                x_scratch[rows, depth], w_scratch[branch, depth, :],
                preferred_element_type=jnp.float32,
            )

            @pl.when(part == 0)
            def _():
                total[branch, rows, :] = product

            @pl.when(part == 1)
            def _():
                total[branch, rows, :] += product

            return carry

        return lax.fori_loop(0, 6, step, carry)

    lax.fori_loop(0, 2, half, 0)
    for group in range(2):
        square = jnp.sum(s_scratch[group].astype(jnp.float32), axis=0)
        for i in range(2):
            row = square[i : i + 1] + square[i + 2 : i + 3] + square[i + 4 : i + 5]
            scale = lax.rsqrt(row / D + epsilon)
            scale = jnp.transpose(jnp.broadcast_to(scale, (LANES, PIECE)))
            scale = jnp.concatenate([scale, scale], axis=1)
            block = group * 2 + i

            def write(branch, carry, block=block, scale=scale):
                value = total[branch, block * BLK : (block + 1) * BLK, :]
                out_ref[branch, block] = (value * scale).astype(jnp.bfloat16)
                return carry

            lax.fori_loop(0, 3, write, 0)


def project(place, line, weights):
    return pl.pallas_call(
        project_kernel,
        out_shape=jax.ShapeDtypeStruct((3, 4, BLK, 2 * LANES), jnp.bfloat16),
        in_specs=[scalars()] + [anywhere()] * 9,
        out_specs=full(),
        scratch_shapes=[
            pltpu.VMEM((2 * HALF, D), jnp.bfloat16),
            pltpu.VMEM((2, 16, TAIL, PIECE), jnp.bfloat16),
            pltpu.VMEM((3, D, 2 * LANES), jnp.bfloat16),
            pltpu.VMEM((3, 2 * HALF, 2 * LANES), jnp.float32),
            pltpu.SemaphoreType.DMA((2, 16)),
            pltpu.SemaphoreType.DMA((2, 16)),
            pltpu.SemaphoreType.DMA((2, 4, 4)),
        ],
        cost_estimate=pl.CostEstimate(
            flops=2 * 1024 * D * 768, bytes_accessed=16 << 20, transcendentals=0
        ),
        name="project",
    )(place, line, *weights)


def reach_of(start, rows, ends_ref):
    position = start + lax.broadcasted_iota(jnp.int32, (rows, LANES), 0)
    first = jnp.zeros((rows, LANES), jnp.int32)
    for g in range(3):
        end = ends_ref[g]
        first = jnp.maximum(first, jnp.where(position >= end, end, 0))
    return position - first


def split_by_genome(start, ends_ref):
    cut = False
    for g in range(3):
        cut = cut | ((ends_ref[g] > start) & (ends_ref[g] < start + BLK))
    return cut


def short_mix(window_ref, reach, taps_ref, branch, rows, lanes):
    total = jnp.zeros((rows, LANES), jnp.float32)
    for j in range(SHORT):
        part = window_ref[TAIL - j : TAIL - j + rows, :]
        if reach is not None:
            part = jnp.where(reach >= j, part, 0.0)
        total = total + part * taps_ref[j, branch : branch + 1, lanes].astype(jnp.float32)
    return total


def product_kernel(start_ref, ends_ref, proj_ref, taps_ref, out_ref, low_ref, high_ref, k, v):
    start = start_ref[pl.program_id(0)]
    cut = split_by_genome(start, ends_ref)
    for part, tail_ref in enumerate((low_ref, high_ref)):
        lanes = pl.ds(part * LANES, LANES)
        k[:TAIL, :] = jnp.zeros((TAIL, LANES), jnp.float32)
        v[:TAIL, :] = jnp.zeros((TAIL, LANES), jnp.float32)
        k[TAIL:, :] = proj_ref[1, 0, :, lanes].astype(jnp.float32)
        v[TAIL:, :] = proj_ref[2, 0, :, lanes].astype(jnp.float32)

        def store(reach):
            mixed = short_mix(k, reach, taps_ref, 1, BLK, lanes)
            product = mixed * short_mix(v, reach, taps_ref, 2, BLK, lanes)
            first = lax.broadcasted_iota(jnp.int32, (BLK, LANES), 0) >= SHORT - 1
            out_ref[0, :, lanes] = jnp.where(first, product, 0.0).astype(jnp.bfloat16)

        @pl.when(cut)
        def _():
            store(reach_of(start, BLK, ends_ref))

        @pl.when(jnp.logical_not(cut))
        def _():
            store(None)

        tail_ref[0, :MED, :] = out_ref[0, BLK - MED :, lanes]
        for branch in range(3):
            at = MED + branch * TAIL
            tail_ref[0, at : at + TAIL, :] = proj_ref[branch, 0, BLK - TAIL :, lanes]


def products(starts, ends, proj, taps):
    tail = jax.ShapeDtypeStruct((4, HALO, LANES), jnp.bfloat16)
    tail_spec = pl.BlockSpec((1, HALO, LANES), lambda i, *_: (i, 0, 0))
    return pl.pallas_call(
        product_kernel,
        grid_spec=pltpu.PrefetchScalarGridSpec(
            num_scalar_prefetch=2,
            grid=(4,),
            in_specs=[
                pl.BlockSpec((3, 1, BLK, 2 * LANES), lambda i, *_: (0, i, 0, 0)),
                pl.BlockSpec((SHORT, 3, 2 * LANES), lambda i, *_: (0, 0, 0)),
            ],
            out_specs=(
                pl.BlockSpec((1, BLK, 2 * LANES), lambda i, *_: (i, 0, 0)), tail_spec, tail_spec,
            ),
            scratch_shapes=[pltpu.VMEM((BLK + TAIL, LANES), jnp.float32)] * 2,
        ),
        out_shape=(jax.ShapeDtypeStruct((4, BLK, 2 * LANES), jnp.bfloat16), tail, tail),
        cost_estimate=pl.CostEstimate(
            flops=60 << 20, bytes_accessed=4 << 20, transcendentals=0
        ),
        name="products",
    )(starts, ends, proj, taps)


def taps_of(shifted, medium_ref, lanes, base, first, last, rows):
    def step(turn, total):
        at = pl.multiple_of(base - turn * TAIL, TAIL)
        weights = medium_ref[pl.ds(pl.multiple_of(turn * TAIL, TAIL), TAIL), lanes]
        for s in range(TAIL):
            total = total + shifted[s, pl.ds(at, rows), :] * weights[s : s + 1, :]
        return total

    return lax.fori_loop(first, last, step, jnp.zeros((rows, LANES), jnp.float32))


GROUP = 64


def inner_kernel(index, start_ref, ends_ref, product_ref, medium_ref, out_ref, shifted):
    start = start_ref[index * 2 + pl.program_id(0)]
    row = start + lax.broadcasted_iota(jnp.int32, (BLK, LANES), 0)
    cut = split_by_genome(start, ends_ref)

    for part in range(2):
        lanes = pl.ds(part * LANES, LANES)

        def run(low, high):
            value = product_ref[0, :, lanes].astype(jnp.float32)
            if low is not None:
                value = jnp.where(row >= low, value, 0.0)
            for s in range(TAIL):
                shifted[s, : GROUP + TAIL, :] = jnp.zeros((GROUP + TAIL, LANES), jnp.float32)
                shifted[s, GROUP + s : GROUP + BLK, :] = value[: BLK - s, :]
            for r in range(BLK // GROUP):
                last = min(MED // TAIL, (r + 1) * GROUP // TAIL)
                total = taps_of(
                    shifted, medium_ref, lanes, GROUP + r * GROUP, 0, last, GROUP
                )
                rows = pl.ds(r * GROUP, GROUP)
                if low is not None:
                    here = row[r * GROUP : (r + 1) * GROUP]
                    total = jnp.where((here >= low) & (here < high), total, out_ref[0, rows, lanes])
                out_ref[0, rows, lanes] = total

        @pl.when(jnp.logical_not(cut))
        def _():
            run(None, None)

        @pl.when(cut)
        def _():
            def genome(g, carry):
                low = jnp.where(g == 0, 0, ends_ref[jnp.maximum(g - 1, 0)])
                high = ends_ref[g]

                @pl.when((low < start + BLK) & (high > start))
                def _():
                    run(low, high)

                return carry

            lax.fori_loop(0, 4, genome, 0)


def inner(index, starts, ends, product, medium):
    return pl.pallas_call(
        functools.partial(inner_kernel, index),
        grid_spec=pltpu.PrefetchScalarGridSpec(
            num_scalar_prefetch=2,
            grid=(2,),
            in_specs=[
                pl.BlockSpec((1, BLK, 2 * LANES), lambda i, *_: (index * 2 + i, 0, 0)),
                pl.BlockSpec((MED, 2 * LANES), lambda i, *_: (0, 0)),
            ],
            out_specs=pl.BlockSpec((1, BLK, 2 * LANES), lambda i, *_: (i, 0, 0)),
            scratch_shapes=[pltpu.VMEM((TAIL, GROUP + BLK, LANES), jnp.float32)],
        ),
        out_shape=jax.ShapeDtypeStruct((2, BLK, 2 * LANES), jnp.float32),
        cost_estimate=pl.CostEstimate(
            flops=1024 * 256 * 128, bytes_accessed=1 << 20, transcendentals=0
        ),
        name="inner",
    )(starts, ends, product, medium)


def route_kernel(table_ref, *refs):
    ins, outs, every = refs[:8], refs[8:16], refs[16]
    for way in range(2):
        for d in range(4):
            every[d * 4 : (d + 1) * 4] = ins[way * 4 + d][...]
        for d in range(4):
            for j in range(4):
                outs[way * 4 + d][j] = every[table_ref[way, d, j]]


def route(table, ins):
    return pl.pallas_call(
        route_kernel,
        out_shape=(jax.ShapeDtypeStruct((4, HALO, LANES), jnp.bfloat16),) * 8,
        in_specs=[scalars()] + [full()] * 8,
        out_specs=(full(),) * 8,
        scratch_shapes=[pltpu.VMEM((16, HALO, LANES), jnp.bfloat16)],
        cost_estimate=pl.CostEstimate(flops=1 << 10, bytes_accessed=4 << 20, transcendentals=0),
        name="route",
    )(table, *ins)


def edge_kernel(
    start_ref, ends_ref, pick_ref, proj_ref, early_ref, late_ref, taps_ref, medium_ref, *refs
):
    halos, (out_ref, halo, window, small, prior, shifted, filtered) = refs[:8], refs[8:]
    block = pl.program_id(0)
    start = start_ref[block]
    cut = split_by_genome(start, ends_ref)
    near = MED + TAIL
    reach8 = reach_of(start, TAIL, ends_ref)
    row = start - MED + lax.broadcasted_iota(jnp.int32, (near, LANES), 0)
    out_row = start + lax.broadcasted_iota(jnp.int32, (near, LANES), 0)
    for part in range(2):
        lanes = pl.ds(part * LANES, LANES)
        for m in range(4):

            @pl.when(pick_ref[part, block] == m)
            def _(m=m):
                halo[...] = halos[part * 4 + m][0].astype(jnp.float32)

        mixes = []
        for branch in (1, 2):
            at = MED + branch * TAIL
            small[:TAIL, :] = halo[at : at + TAIL, :]
            small[TAIL:, :] = proj_ref[branch, 0, : 2 * TAIL, lanes][:TAIL].astype(jnp.float32)
            mixes.append(short_mix(small, reach8, taps_ref, branch, TAIL, lanes))
        first = lax.broadcasted_iota(jnp.int32, (TAIL, LANES), 0) < SHORT - 1
        early = (mixes[0] * mixes[1]).astype(jnp.bfloat16).astype(jnp.float32)
        prior[:MED, :] = halo[:MED, :]
        prior[MED:, :] = jnp.where(first, early, 0.0)

        @pl.when(block < 2)
        def _():
            filtered[...] = early_ref[0, :, lanes]

        @pl.when(block >= 2)
        def _():
            filtered[...] = late_ref[0, :, lanes]

        def genome(g, carry):
            low = jnp.where(g == 0, 0, ends_ref[jnp.maximum(g - 1, 0)])
            high = ends_ref[g]

            @pl.when((low < start + near) & (high > start))
            def _():
                value = jnp.where(row >= low, prior[...], 0.0)
                for s in range(TAIL):
                    shifted[s, TAIL : TAIL + TAIL, :] = jnp.zeros((TAIL, LANES), jnp.float32)
                    shifted[s, near + TAIL :, :] = jnp.zeros((GROUP, LANES), jnp.float32)
                    shifted[s, TAIL + s : TAIL + s + near, :] = value
                for at, rows, begin in ((0, GROUP, 0), (GROUP, GROUP, 7), (2 * GROUP, TAIL, 15)):
                    total = taps_of(
                        shifted, medium_ref, lanes, TAIL + MED + at, begin, MED // TAIL, rows
                    )
                    here = out_row[at : at + rows]
                    total = jnp.where((here >= low) & (here < high), total, 0.0)
                    filtered[at : at + rows, :] += total

            return carry

        lax.fori_loop(0, 4, genome, 0)
        window[:TAIL, :] = halo[MED : MED + TAIL, :]
        window[TAIL:, :] = proj_ref[0, 0, :, lanes].astype(jnp.float32)

        @pl.when(cut)
        def _():
            mixed = short_mix(window, reach_of(start, BLK, ends_ref), taps_ref, 0, BLK, lanes)
            out_ref[0, :, lanes] = (mixed * filtered[...]).astype(jnp.bfloat16)

        @pl.when(jnp.logical_not(cut))
        def _():
            head = short_mix(window, reach8, taps_ref, 0, TAIL, lanes)
            mixed = short_mix(window, None, taps_ref, 0, BLK, lanes)
            mixed = jnp.concatenate([head, mixed[TAIL:]], axis=0)
            out_ref[0, :, lanes] = (mixed * filtered[...]).astype(jnp.bfloat16)


def edges(starts, ends, picks, proj, partials, taps, medium, halos):
    return pl.pallas_call(
        edge_kernel,
        grid_spec=pltpu.PrefetchScalarGridSpec(
            num_scalar_prefetch=3,
            grid=(4,),
            in_specs=[
                pl.BlockSpec((3, 1, BLK, 2 * LANES), lambda i, *_: (0, i, 0, 0)),
                pl.BlockSpec((1, BLK, 2 * LANES), lambda i, *_: (jnp.minimum(i, 1), 0, 0)),
                pl.BlockSpec((1, BLK, 2 * LANES), lambda i, *_: (jnp.maximum(i - 2, 0), 0, 0)),
                pl.BlockSpec((SHORT, 3, 2 * LANES), lambda i, *_: (0, 0, 0)),
                pl.BlockSpec((MED, 2 * LANES), lambda i, *_: (0, 0)),
            ]
            + [pl.BlockSpec((1, HALO, LANES), lambda i, *_: (i, 0, 0))] * 8,
            out_specs=pl.BlockSpec((1, BLK, 2 * LANES), lambda i, *_: (i, 0, 0)),
            scratch_shapes=[
                pltpu.VMEM((HALO, LANES), jnp.float32),
                pltpu.VMEM((BLK + TAIL, LANES), jnp.float32),
                pltpu.VMEM((2 * TAIL, LANES), jnp.float32),
                pltpu.VMEM((MED + TAIL, LANES), jnp.float32),
                pltpu.VMEM((TAIL, MED + 2 * TAIL + GROUP, LANES), jnp.float32),
                pltpu.VMEM((BLK, LANES), jnp.float32),
            ],
        ),
        out_shape=jax.ShapeDtypeStruct((4, BLK, 2 * LANES), jnp.bfloat16),
        cost_estimate=pl.CostEstimate(
            flops=1024 * 256 * 64, bytes_accessed=3 << 20, transcendentals=0
        ),
        name="edges",
    )(starts, ends, picks, proj, *partials, taps, medium, *halos)


def assemble_kernel(place_ref, own_ref, other_ref, out_ref, sems):
    x, y, core = place_ref[0], place_ref[1], place_ref[2]
    started = []
    for other, ref in enumerate((own_ref, other_ref)):
        for dy in range(4):
            for dx in range(4):
                to_x, to_y = lax.rem(x + dx, 4), lax.rem(y + dy, 4)
                owner = to_x * 4 + (to_y // 2) * 2 + lax.rem(core + other, 2)
                rows = pl.ds(pl.multiple_of(owner * 16, 16), 16)
                started.append(
                    pltpu.make_async_copy(
                        ref.at[dy, dx], out_ref.at[lax.rem(to_y, 2), rows], sems.at[other, dy, dx]
                    )
                )
    for copy in started:
        copy.start()
    for copy in started:
        copy.wait()


def assemble(place, own, other):
    return pl.pallas_call(
        assemble_kernel,
        out_shape=jax.ShapeDtypeStruct((2, PIECE, D), jnp.bfloat16),
        in_specs=[scalars()] + [anywhere()] * 2,
        out_specs=full(),
        scratch_shapes=[pltpu.SemaphoreType.DMA((2, 4, 4))],
        cost_estimate=pl.CostEstimate(flops=1 << 10, bytes_accessed=8 << 20, transcendentals=0),
        name="assemble",
    )(place, own, other)


def output_kernel(side, place_ref, residual_ref, w_ref, gated_ref, out_ref, scratch, weights, total, sems, w_sem):
    core, y_low = place_ref[2], place_ref[3]
    load = pltpu.make_async_copy(w_ref.at[lax.rem(y_low + side, 2)], weights, w_sem)
    load.start()
    started = []
    for z in range(8):
        for owner in range(2):
            lanes = pl.ds((z * 2 + owner) * PIECE, PIECE)
            source = gated_ref.at[z * 2 + owner, lax.rem(core + owner, 2)]
            started.append(
                pltpu.make_async_copy(source, scratch.at[:, lanes], sems.at[z, owner])
            )
    for copy in started:
        copy.start()
    for copy in started:
        copy.wait()
    load.wait()
    total[...] = residual_ref[...].astype(jnp.float32)

    def step(i, carry):
        lanes = pl.ds(pl.multiple_of(i * 1024, 1024), 1024)
        total[...] += lax.dot_general(
            scratch[:, lanes], weights[:, lanes], (((1,), (1,)), ((), ())),
            preferred_element_type=jnp.float32,
        )
        return carry

    lax.fori_loop(0, 4, step, 0)
    out_ref[...] = total[...].astype(jnp.bfloat16)


def output(side, place, residual, weights, gated):
    return pl.pallas_call(
        functools.partial(output_kernel, side),
        out_shape=jax.ShapeDtypeStruct((HALF, PIECE), jnp.bfloat16),
        in_specs=[scalars(), full()] + [anywhere()] * 2,
        out_specs=full(),
        scratch_shapes=[
            pltpu.VMEM((HALF, D), jnp.bfloat16),
            pltpu.VMEM((PIECE, D), jnp.bfloat16),
            pltpu.VMEM((HALF, PIECE), jnp.float32),
            pltpu.SemaphoreType.DMA((8, 2)),
            pltpu.SemaphoreType.DMA,
        ],
        cost_estimate=pl.CostEstimate(
            flops=2 * HALF * D * PIECE, bytes_accessed=6 << 20, transcendentals=0
        ),
        name="output",
    )(place, residual, weights, gated)


def block(
    tokens,
    norm_gain,
    in_weight,
    short_filter,
    medium_filter,
    out_weight,
    genome_lengths,
    block_at_slot,
):
    seq, fsdp = lax.axis_index("seq"), lax.axis_index("fsdp")
    x, core, y_low, z = seq // 4, seq % 2, fsdp // 8, fsdp % 8
    y = ((seq // 2) % 2) * 2 + y_low

    values = tokens.astype(jnp.float32)
    gain = lax.dynamic_index_in_dim(norm_gain.reshape(16, 1, PIECE), fsdp, 0, keepdims=False)
    scaled = (values * gain.astype(jnp.float32)).astype(jnp.bfloat16)
    square = jnp.sum(values * values, axis=1)
    parts = []
    for _ in range(3):
        part = lax.reduce_precision(square, exponent_bits=8, mantissa_bits=7)
        parts.append(part.astype(jnp.bfloat16).reshape(2, 2, PIECE))
        square = square - part
    parts.append(jnp.zeros((2, 2, PIECE), jnp.bfloat16))
    packed = jnp.concatenate([scaled.reshape(2, HALF, PIECE)] + parts, axis=1)
    mine = jnp.where(y_low == 0, packed[0], packed[1])
    theirs = send(jnp.where(y_low == 0, packed[1], packed[0]), swap_y)
    pair = jnp.stack([mine, theirs])
    line = gather_line(pair)

    halves = in_weight.reshape(3, PIECE, 2, LANES)
    keep = jnp.where(core == 0, halves[:, :, 0], halves[:, :, 1])
    give = jnp.where(core == 0, halves[:, :, 1], halves[:, :, 0])
    other = send(give, swap_core)
    first = axis_of(keep, along_x)
    first, other = jnp.stack(first), jnp.stack(axis_of(other, along_y))
    weights = axis_of(first, along_y) + axis_of(other, along_x)

    place = jnp.stack([x, y, core, y_low, z]).astype(jnp.int32)

    columns = out_weight.reshape(2, 8, 2, LANES, 16).transpose(4, 1, 2, 0, 3).reshape(16, D)
    columns = axis_of(columns, along_x)
    columns = jnp.stack(columns)
    place, columns = lax.optimization_barrier((place, columns))
    proj = project(place, line, weights)

    both = jnp.concatenate([short_filter.reshape(SHORT * 3, PIECE), medium_filter], axis=0)
    both = jnp.where(core == 0, both[:, :LANES], both[:, LANES:])
    theirs = send(both, swap_y)
    both = jnp.concatenate(
        [jnp.where(y_low == 0, both, theirs), jnp.where(y_low == 0, theirs, both)], axis=1
    )
    taps = both[: SHORT * 3].reshape(SHORT, 3, 2 * LANES)
    medium = both[SHORT * 3 :].astype(jnp.float32)

    way = jnp.arange(2, dtype=jnp.int32).reshape(2, 1, 1, 1)
    ahead = jnp.arange(4, dtype=jnp.int32).reshape(1, 4, 1, 1)
    group = jnp.arange(2, dtype=jnp.int32).reshape(1, 1, 2, 1)
    index = jnp.arange(2, dtype=jnp.int32).reshape(1, 1, 1, 2)
    to_x, to_y = (x + way * ahead) % 4, (y + (1 - way) * ahead) % 4
    slots = (to_x * 4 + (to_y // 2) * 2 + (core + group) % 2) * 4 + (to_y % 2) * 2 + index
    slots = slots.reshape(32)
    all_slots = jnp.arange(block_at_slot.shape[0], dtype=jnp.int32)
    ids = jnp.sum(jnp.where(all_slots == slots[:, None], block_at_slot, 0), axis=1)
    previous = jnp.maximum(ids - 1, 0)
    before = jnp.sum(jnp.where(block_at_slot == previous[:, None], all_slots, 0), axis=1)
    before = before.reshape(2, 4, 4)
    from_x, from_y = before // 16, ((before // 8) % 2) * 2 + (before // 2) % 2
    local = ((before // 4 + core) % 2) * 2 + before % 2
    dx, dy = (from_x - x) % 4, (from_y - y) % 4
    table = jnp.stack(
        [jnp.where(dy[0] == 0, dx[0] * 4, 0) + local[0],
         jnp.where(dx[1] == 0, dy[1] * 4, 0) + local[1]]
    ).astype(jnp.int32)
    picks = jnp.stack([dy[0, 0], dx[1, 0]]).astype(jnp.int32)
    starts = (ids[:4] * BLK).astype(jnp.int32)
    ends = jnp.cumsum(genome_lengths).astype(jnp.int32)

    product, low, high = products(starts, ends, proj, taps)
    rows_x, rows_y = axis_of(low, along_x), axis_of(high, along_y)
    partials = [inner(i, starts, ends, product, medium) for i in range(2)]
    table, partials[0] = lax.optimization_barrier((table, partials[0]))
    routed = route(table, rows_x + rows_y)
    halos = [routed[0]] + [send(routed[4 - d], along_y(4 - d)) for d in range(1, 4)]
    halos += [routed[4]] + [send(routed[8 - d], along_x(4 - d)) for d in range(1, 4)]

    rows = tokens.reshape(2, HALF, PIECE)
    residual = send(jnp.where(y_low == 0, rows[1], rows[0]), swap_y)
    mine = jnp.where(y_low == 0, rows[0], rows[1])
    gated = edges(starts, ends, picks, proj, partials, taps, medium, halos)
    columns = lax.optimization_barrier((columns, gated))[0]
    gathered = gather_line(gated.reshape(2, HALF, 2 * LANES))
    columns = jnp.stack(axis_of(columns, along_y))
    columns = assemble(place, columns, send(columns, swap_core))
    theirs = output(1, place, residual, columns, gathered)
    place, theirs = lax.optimization_barrier((place, theirs))
    theirs = send(theirs, swap_y)
    ours = output(0, place, mine, columns, gathered)
    first = jnp.where(y_low == 0, ours, theirs)
    second = jnp.where(y_low == 0, theirs, ours)
    return jnp.concatenate([first, second], axis=0)


def solution(mesh):
    in_specs = (
        P("seq", "fsdp"),
        P(),
        P(None, "seq", "fsdp"),
        P(None, None, "fsdp"),
        P(None, "fsdp"),
        P(None, ("fsdp", "seq")),
        P(),
        P(),
    )
    out_specs = P("seq", "fsdp")
    return jax.shard_map(block, mesh=mesh, in_specs=in_specs, out_specs=out_specs, check_vma=False)
```

profile of v0, /device:TPU:32, one launch (start us, length us, event | category | flops | bytes accessed | tf_op | source)
XLA Modules:
  0.0 255.7 jit_solution(13049880859537472219)
XLA Ops:
  6.5 0.7 reshape.315
  7.3 1.3 fusion.1
  8.8 1.7 collective-permute-start.4
  10.5 6.6 %collective-permute-done.4 = bf16[520,256]{1,0:T(8,128)(2,1)S(1)} collective-permute-done((bf16[520,256]{1,0:T(8,128)(2,1)S(1)}, bf16[520,256]{1,0:T(8,128)(2,1)S(1)}, u32[]{:S(2)}, u32[]{:S(2)}) %collective-permute-start.4) | collective-permute-done | bytes 266272 | tf_op jit(solution)/shard_map/ppermute | solution.py:39
  17.0 0.9 pad_maximum_fusion.3
  18.6 2.8 %collective-permute-start.5 = (bf16[3,256,128]{2,1,0:T(8,128)(2,1)S(1)}, bf16[3,256,128]{2,1,0:T(8,128)(2,1)S(1)}, u32[]{:S(2)}, u32[]{:S(2)}) collective-permute-start(bf16[3,256,128]{2,1,0:T(8,128)(2,1)S(1)} %get-tuple-element.50), channel_id=1, source_target_pairs={{0,192},{16,208},{1,193},{17,209},{2,194},{18,210},{3,195},{19,211... | collective-permute-start | bytes 589832 | tf_op jit(solution)/shard_map/ppermute | solution.py:39
  21.5 0.8 collective-permute-start.6
  22.3 0.9 collective-permute-start.7
  23.4 2.4 collective-permute-start
  26.4 0.7 reduce-window.9
  27.3 2.4 collective-permute-done.5
  29.8 0.9 collective-permute-done.6
  30.6 2.1 collective-permute-done.7
  32.8 1.7 collective-permute-start.10
  34.7 0.7 stack.93.place_ref
  35.5 1.7 collective-permute-start.12
  37.2 2.0 collective-permute-start.13
  39.2 0.7 collective-permute-start.14
  40.4 3.0 %collective-permute-done.12 = bf16[3,256,128]{2,1,0:T(8,128)(2,1)S(1)} collective-permute-done((bf16[3,256,128]{2,1,0:T(8,128)(2,1)S(1)}, bf16[3,256,128]{2,1,0:T(8,128)(2,1)S(1)}, u32[]{:S(2)}, u32[]{:S(2)}) %collective-permute-start.12) | collective-permute-done | bytes 196640 | tf_op jit(solution)/shard_map/ppermute | solution.py:39
  43.4 0.8 collective-permute-start.1
  44.2 15.9 %collective-permute-done.13 = bf16[3,256,128]{2,1,0:T(8,128)(2,1)S(1)} collective-permute-done((bf16[3,256,128]{2,1,0:T(8,128)(2,1)S(1)}, bf16[3,256,128]{2,1,0:T(8,128)(2,1)S(1)}, u32[]{:S(2)}, u32[]{:S(2)}) %collective-permute-start.13) | collective-permute-done | bytes 196640 | tf_op jit(solution)/shard_map/ppermute | solution.py:39
  60.0 1.7 collective-permute-done.14
  62.2 3.5 %collective-permute-done.18 = bf16[149,128]{1,0:T(8,128)(2,1)S(1)} collective-permute-done((bf16[149,128]{1,0:T(8,128)(2,1)S(1)}, bf16[149,128]{1,0:T(8,128)(2,1)S(1)}, u32[]{:S(2)}, u32[]{:S(2)}) %collective-permute-start.18) | collective-permute-done | bytes 38176 | tf_op jit(solution)/shard_map/ppermute | solution.py:39
  65.7 1.8 collective-permute-start.8
  67.5 0.6 collective-permute-start.9
  68.1 1.2 collective-permute-start.15
  69.3 0.9 collective-permute-start.17
  70.3 0.6 reshape.319.taps_ref
  71.0 28.6 %collective-permute-done.8.refs_1_ = bf16[4,3,256,128]{3,2,1,0:T(8,128)(2,1)} collective-permute-done((bf16[4,3,256,128]{3,2,1,0:T(8,128)(2,1)S(1)}, bf16[4,3,256,128]{3,2,1,0:T(8,128)(2,1)}, u32[]{:S(2)}, u32[]{:S(2)}) %collective-permute-start.8) | collective-permute-done | bytes 786464 | tf_op jit(solution)/shard_map/ppermute | solution.py:39
  99.6 4.2 %collective-permute-done.17.refs_7_ = bf16[4,3,256,128]{3,2,1,0:T(8,128)(2,1)} collective-permute-done((bf16[4,3,256,128]{3,2,1,0:T(8,128)(2,1)S(1)}, bf16[4,3,256,128]{3,2,1,0:T(8,128)(2,1)}, u32[]{:S(2)}, u32[]{:S(2)}) %collective-permute-start.17) | collective-permute-done | bytes 786464 | tf_op jit(solution)/shard_map/ppermute | solution.py:39
  103.8 16.8 %project.1.proj_ref = bf16[3,4,256,256]{3,2,1,0:T(8,128)(2,1)} custom-call(s32[5]{0:T(128)} %stack.93.place_ref, bf16[16,2,520,256]{3,2,1,0:T(8,128)(2,1)} %bitcast.69, bf16[4,3,256,128]{3,2,1,0:T(8,128)(2,1)} %copy-done.2, bf16[4,3,256,128]{3,2,1,0:T(8,128)(2,1)} %collective-permute-done.8.refs_1_, bf16[4,3,256,128]{3,2,1,0:T(8,128)(2,1)} %collective-permute-done.9.refs_2_, ...), custom_call_target="tpu_custom_call" | custom-call | flops 6442450944 | bytes 16777216 | tf_op jit(solution)/shard_map/project/pallas_call | solution.py:184
  120.6 4.7 %products.1 = (bf16[4,256,256]{2,1,0:T(8,128)(2,1)}, bf16[4,152,128]{2,1,0:T(8,128)(2,1)}, bf16[4,152,128]{2,1,0:T(8,128)(2,1)}) custom-call(s32[4]{0:T(128)} %slice_multiply_fusion.2.start_ref, s32[4]{0:T(128)} %bitcast.64, bf16[3,4,256,256]{3,2,1,0:T(8,128)(2,1)} %project.1.proj_ref, bf16[7,3,256]{2,1,0:T(4,128)(2,1)} %reshape.319.taps_ref), custom_call_target="tpu_custom_call" | custom-call | flops 62914560 | bytes 4194304 | tf_op jit(solution)/shard_map/products/pallas_call | solution.py:264
  125.3 1.1 collective-permute-start.19
  126.4 1.0 collective-permute-start.21
  127.3 2.2 collective-permute-start.22
  129.6 0.9 collective-permute-start.23
  130.5 1.9 collective-permute-done.19.refs_1_
  132.4 0.9 collective-permute-start.24
  133.9 0.7 fusion.4.medium_ref
  134.5 7.9 %inner.2.early_ref = f32[2,256,256]{2,1,0:T(8,128)} custom-call(s32[4]{0:T(128)} %slice_multiply_fusion.2.start_ref, s32[4]{0:T(128)} %bitcast.65, bf16[4,256,256]{2,1,0:T(8,128)(2,1)} %get-tuple-element.25.product_ref, f32[128,256]{1,0:T(8,128)} %fusion.4.medium_ref), custom_call_target="tpu_custom_call" | custom-call | flops 33554432 | bytes 1048576 | tf_op jit(solution)/shard_map/inner/pallas_call | solution.py:346
  143.3 0.7 copy-done.17
  143.9 2.5 route.1
  146.4 2.3 collective-permute-start.25
  148.7 3.4 %collective-permute-start.26 = (bf16[4,152,128]{2,1,0:T(8,128)(2,1)}, bf16[4,152,128]{2,1,0:T(8,128)(2,1)S(1)}, u32[]{:S(2)}, u32[]{:S(2)}) collective-permute-start(bf16[4,152,128]{2,1,0:T(8,128)(2,1)} %get-tuple-element.32), channel_id=1, source_target_pairs={{0,32},{16,48},{1,33},{17,49},{2,34},{18,50},{3,35},{19,51},{4,36}... | collective-permute-start | bytes 466952 | tf_op jit(solution)/shard_map/ppermute | solution.py:39
  152.2 1.3 collective-permute-start.27
  153.5 1.6 collective-permute-start.29
  155.1 1.7 collective-permute-start.30
  157.5 7.9 %inner.3.late_ref = f32[2,256,256]{2,1,0:T(8,128)} custom-call(s32[4]{0:T(128)} %slice_multiply_fusion.2.start_ref, s32[4]{0:T(128)} %bitcast.66, bf16[4,256,256]{2,1,0:T(8,128)(2,1)} %get-tuple-element.25.product_ref, f32[128,256]{1,0:T(8,128)} %fusion.4.medium_ref), custom_call_target="tpu_custom_call" | custom-call | flops 33554432 | bytes 1048576 | tf_op jit(solution)/shard_map/inner/pallas_call | solution.py:346
  166.3 9.7 %edges.1 = bf16[4,256,256]{2,1,0:T(8,128)(2,1)} custom-call(s32[4]{0:T(128)} %slice_multiply_fusion.2.start_ref, s32[4]{0:T(128)} %bitcast.67, s32[2,4]{1,0:T(2,128)} %pad_add_fusion.1.pick_ref, bf16[3,4,256,256]{3,2,1,0:T(8,128)(2,1)} %project.1.proj_ref, f32[2,256,256]{2,1,0:T(8,128)} %inner.2.early_ref, f32[2,256,256]{2,1,0:T(8,128)} %inner.3.late_ref, ...), custom_call_target="tpu_custom_call" | custom-call | flops 16777216 | bytes 3145728 | tf_op jit(solution)/shard_map/edges/pallas_call | solution.py:465
  176.0 3.6 %collective-permute-start.31 = (bf16[4,16,4096]{2,1,0:T(8,128)(2,1)S(1)}, bf16[4,16,4096]{2,1,0:T(8,128)(2,1)S(1)}, u32[]{:S(2)}, u32[]{:S(2)}) collective-permute-start(bf16[4,16,4096]{2,1,0:T(8,128)(2,1)S(1)} %pad_maximum_fusion.4), channel_id=1, source_target_pairs={{0,40},{16,56},{1,41},{17,57},{2,42},{18,58},{3,43},{19,59},{4,44}... | collective-permute-start | bytes 1572872 | tf_op jit(solution)/shard_map/ppermute | solution.py:39
  179.7 1.0 collective-permute-start.33
  180.6 15.7 %collective-permute-done.31 = bf16[4,16,4096]{2,1,0:T(8,128)(2,1)S(1)} collective-permute-done((bf16[4,16,4096]{2,1,0:T(8,128)(2,1)S(1)}, bf16[4,16,4096]{2,1,0:T(8,128)(2,1)S(1)}, u32[]{:S(2)}, u32[]{:S(2)}) %collective-permute-start.31) | collective-permute-done | bytes 524320 | tf_op jit(solution)/shard_map/ppermute | solution.py:39
  196.3 4.5 %collective-permute-done.33 = bf16[4,16,4096]{2,1,0:T(8,128)(2,1)S(1)} collective-permute-done((bf16[4,16,4096]{2,1,0:T(8,128)(2,1)S(1)}, bf16[4,16,4096]{2,1,0:T(8,128)(2,1)S(1)}, u32[]{:S(2)}, u32[]{:S(2)}) %collective-permute-start.33) | collective-permute-done | bytes 524320 | tf_op jit(solution)/shard_map/ppermute | solution.py:39
  201.1 0.7 copy-done.1
  201.8 0.7 broadcast_select_fusion.3
  202.5 1.8 collective-permute-start.3
  204.3 1.5 collective-permute-done.34.other_ref
  205.8 5.4 %assemble.1.w_ref = bf16[2,256,4096]{2,1,0:T(8,128)(2,1)} custom-call(s32[5]{0:T(128)} %stack.93.place_ref, bf16[4,4,16,4096]{3,2,1,0:T(8,128)(2,1)} %copy-done, bf16[4,4,16,4096]{3,2,1,0:T(8,128)(2,1)} %collective-permute-done.34.other_ref), custom_call_target="tpu_custom_call" | custom-call | flops 1024 | bytes 8388608 | tf_op jit(solution)/shard_map/assemble/pallas_call | solution.py:517
  211.2 20.4 %all-gather.4.cloned.1.call-done.gated_ref = bf16[16,2,512,256]{3,2,1,0:T(8,128)(2,1)} async-done(((bf16[1,2,512,256]{3,2,1,0:T(8,128)(2,1)}), bf16[16,2,512,256]{3,2,1,0:T(8,128)(2,1)}) %all-gather.4.cloned.1.call-update) | async-done | bytes 8388624 | tf_op jit(solution)/shard_map/all_gather | solution.py:64
  231.6 6.6 %output.2 = bf16[512,256]{1,0:T(8,128)(2,1)} custom-call(s32[5]{0:T(128)} %stack.93.place_ref, bf16[512,256]{1,0:T(8,128)(2,1)} %copy-done.5, bf16[2,256,4096]{2,1,0:T(8,128)(2,1)} %assemble.1.w_ref, bf16[16,2,512,256]{3,2,1,0:T(8,128)(2,1)} %all-gather.4.cloned.1.call-done.gated_ref), custom_call_target="tpu_custom_call" | custom-call | flops 1073741824 | bytes 6291456 | tf_op jit(solution)/shard_map/output/pallas_call | solution.py:560
  238.3 1.6 collective-permute-start.35
  239.8 6.6 %output.3 = bf16[512,256]{1,0:T(8,128)(2,1)} custom-call(s32[5]{0:T(128)} %stack.93.place_ref, bf16[512,256]{1,0:T(8,128)(2,1)} %get-tuple-element.45.residual_ref, bf16[2,256,4096]{2,1,0:T(8,128)(2,1)} %assemble.1.w_ref, bf16[16,2,512,256]{3,2,1,0:T(8,128)(2,1)} %all-gather.4.cloned.1.call-done.gated_ref), custom_call_target="tpu_custom_call" | custom-call | flops 1073741824 | bytes 6291456 | tf_op jit(solution)/shard_map/output/pallas_call | solution.py:560
  247.0 1.0 broadcast_select_fusion.2
  248.0 0.8 pad_maximum_fusion.5
  (119 shorter events, 7.0 us)
Async XLA Ops:
  6.5 97.2 %all-gather.6.cloned.1.call-start = ((), (), s32[]{:S(2)}) async-start(), calls=%async_computation.1 | async-start | bytes 9052160 | tf_op jit(solution)/shard_map/all_gather | solution.py:64
  8.5 9.5 %copy-start.4 = (bf16[3,256,256]{2,1,0:T(8,128)(2,1)S(1)}, bf16[3,256,256]{2,1,0:T(8,128)(2,1)}, u32[]{:S(2)}) copy-start(bf16[3,256,256]{2,1,0:T(8,128)(2,1)} %param.10) | copy-start | bytes 1179652
  8.8 8.2 %collective-permute-start.4 = (bf16[520,256]{1,0:T(8,128)(2,1)S(1)}, bf16[520,256]{1,0:T(8,128)(2,1)S(1)}, u32[]{:S(2)}, u32[]{:S(2)}) collective-permute-start(bf16[520,256]{1,0:T(8,128)(2,1)S(1)} %get-tuple-element.42), channel_id=1, source_target_pairs={{0,8},{16,24},{1,9},{17,25},{2,10},{18,26},{3,11},{19,27},{4,12},{... | collective-permute-start | bytes 798728 | tf_op jit(solution)/shard_map/ppermute | solution.py:39
  17.9 5.3 %copy-start.18 = (bf16[4096,16]{0,1:T(8,128)(2,1)S(1)}, bf16[4096,16]{0,1:T(8,128)(2,1)}, u32[]{:S(2)}) copy-start(bf16[4096,16]{0,1:T(8,128)(2,1)} %param.13) | copy-start | bytes 393220
  17.9 213.7 %all-gather.4.cloned.1.call-start = ((), (), s32[]{:S(2)}) async-start(), calls=%async_computation | async-start | bytes 8912896 | tf_op jit(solution)/shard_map/all_gather | solution.py:64
  18.0 8.0 %copy-start.20 = (bf16[7,3,256]{2,0,1:T(8,128)(2,1)S(1)}, bf16[7,3,256]{2,0,1:T(8,128)(2,1)}, u32[]{:S(2)}) copy-start(bf16[7,3,256]{2,0,1:T(8,128)(2,1)} %param.11) | copy-start | bytes 32260
  18.0 8.4 %copy-start.21 = (s32[4]{0:T(128)S(1)}, s32[4]{0:T(128)}, u32[]{:S(2)}) copy-start(s32[4]{0:T(128)} %param.14) | copy-start | bytes 52
  18.0 9.1 %copy-start.22 = (s32[64]{0:T(128)S(1)}, s32[64]{0:T(128)}, u32[]{:S(2)}) copy-start(s32[64]{0:T(128)} %param.15) | copy-start | bytes 772
  18.4 17.0 %copy-start.19 = (bf16[128,256]{1,0:T(8,128)(2,1)S(1)}, bf16[128,256]{1,0:T(8,128)(2,1)}, u32[]{:S(2)}) copy-start(bf16[128,256]{1,0:T(8,128)(2,1)} %param.12) | copy-start | bytes 196612
  18.6 11.1 %collective-permute-start.5 = (bf16[3,256,128]{2,1,0:T(8,128)(2,1)S(1)}, bf16[3,256,128]{2,1,0:T(8,128)(2,1)S(1)}, u32[]{:S(2)}, u32[]{:S(2)}) collective-permute-start(bf16[3,256,128]{2,1,0:T(8,128)(2,1)S(1)} %get-tuple-element.50), channel_id=1, source_target_pairs={{0,192},{16,208},{1,193},{17,209},{2,194},{18,210},{3,195},{19,211... | collective-permute-start | bytes 589832 | tf_op jit(solution)/shard_map/ppermute | solution.py:39
  21.5 9.2 %collective-permute-start.6 = (bf16[3,256,128]{2,1,0:T(8,128)(2,1)S(1)}, bf16[3,256,128]{2,1,0:T(8,128)(2,1)S(1)}, u32[]{:S(2)}, u32[]{:S(2)}) collective-permute-start(bf16[3,256,128]{2,1,0:T(8,128)(2,1)S(1)} %get-tuple-element.50), channel_id=1, source_target_pairs={{0,128},{16,144},{1,129},{17,145},{2,130},{18,146},{3,131},{19,147... | collective-permute-start | bytes 589832 | tf_op jit(solution)/shard_map/ppermute | solution.py:39
  22.3 10.4 %collective-permute-start.7 = (bf16[3,256,128]{2,1,0:T(8,128)(2,1)S(1)}, bf16[3,256,128]{2,1,0:T(8,128)(2,1)S(1)}, u32[]{:S(2)}, u32[]{:S(2)}) collective-permute-start(bf16[3,256,128]{2,1,0:T(8,128)(2,1)S(1)} %get-tuple-element.50), channel_id=1, source_target_pairs={{0,64},{16,80},{1,65},{17,81},{2,66},{18,82},{3,67},{19,83},{4,68}... | collective-permute-start | bytes 589832 | tf_op jit(solution)/shard_map/ppermute | solution.py:39
  23.2 12.3 %collective-permute-start.11 = (bf16[3,256,128]{2,1,0:T(8,128)(2,1)S(1)}, bf16[3,256,128]{2,1,0:T(8,128)(2,1)S(1)}, u32[]{:S(2)}, u32[]{:S(2)}) collective-permute-start(bf16[3,256,128]{2,1,0:T(8,128)(2,1)S(1)} %get-tuple-element.49), channel_id=1, source_target_pairs={{0,16},{16,0},{1,17},{17,1},{2,18},{18,2},{3,19},{19,3},{4,20},{20... | collective-permute-start | bytes 589832 | tf_op jit(solution)/shard_map/ppermute | solution.py:39
  23.4 44.1 %collective-permute-start = (bf16[16,4096]{1,0:T(8,128)(2,1)S(1)}, bf16[16,4096]{1,0:T(8,128)(2,1)S(1)}, u32[]{:S(2)}, u32[]{:S(2)}) collective-permute-start(bf16[16,4096]{1,0:T(8,128)(2,1)S(1)} %reshape.311), channel_id=1, source_target_pairs={{0,192},{16,208},{1,193},{17,209},{2,194},{18,210},{3,195},{19,211... | collective-permute-start | bytes 393224 | tf_op jit(solution)/shard_map/ppermute | solution.py:39
  32.8 71.0 %copy-start.2 = (bf16[4,3,256,128]{3,2,1,0:T(8,128)(2,1)}, bf16[4,3,256,128]{3,2,1,0:T(8,128)(2,1)S(1)}, u32[]{:S(2)}) copy-start(bf16[4,3,256,128]{3,2,1,0:T(8,128)(2,1)S(1)} %pad_maximum_fusion.1.refs_0_) | copy-start | bytes 2359300
  32.8 36.5 %collective-permute-start.10 = (bf16[4,3,256,128]{3,2,1,0:T(8,128)(2,1)S(1)}, bf16[4,3,256,128]{3,2,1,0:T(8,128)(2,1)}, u32[]{:S(2)}, u32[]{:S(2)}) collective-permute-start(bf16[4,3,256,128]{3,2,1,0:T(8,128)(2,1)S(1)} %pad_maximum_fusion.1.refs_0_), channel_id=1, source_target_pairs={{0,8},{16,24},{1,9},{17,25},{2,10},{18,26},{3,11},{19,27},{4,12},{... | collective-permute-start | bytes 2359304 | tf_op jit(solution)/shard_map/ppermute | solution.py:39
  35.5 7.8 %collective-permute-start.12 = (bf16[3,256,128]{2,1,0:T(8,128)(2,1)S(1)}, bf16[3,256,128]{2,1,0:T(8,128)(2,1)S(1)}, u32[]{:S(2)}, u32[]{:S(2)}) collective-permute-start(bf16[3,256,128]{2,1,0:T(8,128)(2,1)S(1)} %collective-permute-done.11), channel_id=1, source_target_pairs={{0,40},{16,56},{1,41},{17,57},{2,42},{18,58},{3,43},{19,59},{4,44}... | collective-permute-start | bytes 589832 | tf_op jit(solution)/shard_map/ppermute | solution.py:39
  37.2 22.8 %collective-permute-start.13 = (bf16[3,256,128]{2,1,0:T(8,128)(2,1)S(1)}, bf16[3,256,128]{2,1,0:T(8,128)(2,1)S(1)}, u32[]{:S(2)}, u32[]{:S(2)}) collective-permute-start(bf16[3,256,128]{2,1,0:T(8,128)(2,1)S(1)} %collective-permute-done.11), channel_id=1, source_target_pairs={{0,32},{16,48},{1,33},{17,49},{2,34},{18,50},{3,35},{19,51},{4,36}... | collective-permute-start | bytes 589832 | tf_op jit(solution)/shard_map/ppermute | solution.py:39
  39.2 22.5 %collective-permute-start.14 = (bf16[3,256,128]{2,1,0:T(8,128)(2,1)S(1)}, bf16[3,256,128]{2,1,0:T(8,128)(2,1)S(1)}, u32[]{:S(2)}, u32[]{:S(2)}) collective-permute-start(bf16[3,256,128]{2,1,0:T(8,128)(2,1)S(1)} %collective-permute-done.11), channel_id=1, source_target_pairs={{0,8},{16,24},{1,9},{17,25},{2,10},{18,26},{3,11},{19,27},{4,12},{... | collective-permute-start | bytes 589832 | tf_op jit(solution)/shard_map/ppermute | solution.py:39
  43.4 24.8 %collective-permute-start.1 = (bf16[16,4096]{1,0:T(8,128)(2,1)S(1)}, bf16[16,4096]{1,0:T(8,128)(2,1)S(1)}, u32[]{:S(2)}, u32[]{:S(2)}) collective-permute-start(bf16[16,4096]{1,0:T(8,128)(2,1)S(1)} %reshape.311), channel_id=1, source_target_pairs={{0,128},{16,144},{1,129},{17,145},{2,130},{18,146},{3,131},{19,147... | collective-permute-start | bytes 393224 | tf_op jit(solution)/shard_map/ppermute | solution.py:39
  60.0 9.3 %collective-permute-start.2 = (bf16[16,4096]{1,0:T(8,128)(2,1)S(1)}, bf16[16,4096]{1,0:T(8,128)(2,1)S(1)}, u32[]{:S(2)}, u32[]{:S(2)}) collective-permute-start(bf16[16,4096]{1,0:T(8,128)(2,1)S(1)} %reshape.311), channel_id=1, source_target_pairs={{0,64},{16,80},{1,65},{17,81},{2,66},{18,82},{3,67},{19,83},{4,68}... | collective-permute-start | bytes 393224 | tf_op jit(solution)/shard_map/ppermute | solution.py:39
  61.7 4.0 %collective-permute-start.18 = (bf16[149,128]{1,0:T(8,128)(2,1)S(1)}, bf16[149,128]{1,0:T(8,128)(2,1)S(1)}, u32[]{:S(2)}, u32[]{:S(2)}) collective-permute-start(bf16[149,128]{1,0:T(8,128)(2,1)S(1)} %fusion.6), channel_id=1, source_target_pairs={{0,8},{16,24},{1,9},{17,25},{2,10},{18,26},{3,11},{19,27},{4,12},{... | collective-permute-start | bytes 114440 | tf_op jit(solution)/shard_map/ppermute | solution.py:39
  62.2 41.6 %copy-start.3 = (bf16[4,3,256,128]{3,2,1,0:T(8,128)(2,1)}, bf16[4,3,256,128]{3,2,1,0:T(8,128)(2,1)S(1)}, u32[]{:S(2)}) copy-start(bf16[4,3,256,128]{3,2,1,0:T(8,128)(2,1)S(1)} %pad_maximum_fusion.2.refs_4_) | copy-start | bytes 2359300
  65.7 33.8 %collective-permute-start.8 = (bf16[4,3,256,128]{3,2,1,0:T(8,128)(2,1)S(1)}, bf16[4,3,256,128]{3,2,1,0:T(8,128)(2,1)}, u32[]{:S(2)}, u32[]{:S(2)}) collective-permute-start(bf16[4,3,256,128]{3,2,1,0:T(8,128)(2,1)S(1)} %pad_maximum_fusion.1.refs_0_), channel_id=1, source_target_pairs={{0,40},{16,56},{1,41},{17,57},{2,42},{18,58},{3,43},{19,59},{4,44}... | collective-permute-start | bytes 2359304 | tf_op jit(solution)/shard_map/ppermute | solution.py:39
  67.5 32.0 %collective-permute-start.9 = (bf16[4,3,256,128]{3,2,1,0:T(8,128)(2,1)S(1)}, bf16[4,3,256,128]{3,2,1,0:T(8,128)(2,1)}, u32[]{:S(2)}, u32[]{:S(2)}) collective-permute-start(bf16[4,3,256,128]{3,2,1,0:T(8,128)(2,1)S(1)} %pad_maximum_fusion.1.refs_0_), channel_id=1, source_target_pairs={{0,32},{16,48},{1,33},{17,49},{2,34},{18,50},{3,35},{19,51},{4,36}... | collective-permute-start | bytes 2359304 | tf_op jit(solution)/shard_map/ppermute | solution.py:39
  68.1 31.4 %collective-permute-start.15 = (bf16[4,3,256,128]{3,2,1,0:T(8,128)(2,1)S(1)}, bf16[4,3,256,128]{3,2,1,0:T(8,128)(2,1)}, u32[]{:S(2)}, u32[]{:S(2)}) collective-permute-start(bf16[4,3,256,128]{3,2,1,0:T(8,128)(2,1)S(1)} %pad_maximum_fusion.2.refs_4_), channel_id=1, source_target_pairs={{0,192},{16,208},{1,193},{17,209},{2,194},{18,210},{3,195},{19,211... | collective-permute-start | bytes 2359304 | tf_op jit(solution)/shard_map/ppermute | solution.py:39
  69.3 30.2 %collective-permute-start.16 = (bf16[4,3,256,128]{3,2,1,0:T(8,128)(2,1)S(1)}, bf16[4,3,256,128]{3,2,1,0:T(8,128)(2,1)}, u32[]{:S(2)}, u32[]{:S(2)}) collective-permute-start(bf16[4,3,256,128]{3,2,1,0:T(8,128)(2,1)S(1)} %pad_maximum_fusion.2.refs_4_), channel_id=1, source_target_pairs={{0,128},{16,144},{1,129},{17,145},{2,130},{18,146},{3,131},{19,147... | collective-permute-start | bytes 2359304 | tf_op jit(solution)/shard_map/ppermute | solution.py:39
  69.3 34.4 %collective-permute-start.17 = (bf16[4,3,256,128]{3,2,1,0:T(8,128)(2,1)S(1)}, bf16[4,3,256,128]{3,2,1,0:T(8,128)(2,1)}, u32[]{:S(2)}, u32[]{:S(2)}) collective-permute-start(bf16[4,3,256,128]{3,2,1,0:T(8,128)(2,1)S(1)} %pad_maximum_fusion.2.refs_4_), channel_id=1, source_target_pairs={{0,64},{16,80},{1,65},{17,81},{2,66},{18,82},{3,67},{19,83},{4,68}... | collective-permute-start | bytes 2359304 | tf_op jit(solution)/shard_map/ppermute | solution.py:39
  125.3 7.1 %collective-permute-start.19 = (bf16[4,152,128]{2,1,0:T(8,128)(2,1)}, bf16[4,152,128]{2,1,0:T(8,128)(2,1)S(1)}, u32[]{:S(2)}, u32[]{:S(2)}) collective-permute-start(bf16[4,152,128]{2,1,0:T(8,128)(2,1)} %get-tuple-element.28.refs_0_), channel_id=1, source_target_pairs={{0,192},{16,208},{1,193},{17,209},{2,194},{18,210},{3,195},{19,211... | collective-permute-start | bytes 466952 | tf_op jit(solution)/shard_map/ppermute | solution.py:39
  126.4 16.1 %collective-permute-start.20 = (bf16[4,152,128]{2,1,0:T(8,128)(2,1)}, bf16[4,152,128]{2,1,0:T(8,128)(2,1)S(1)}, u32[]{:S(2)}, u32[]{:S(2)}) collective-permute-start(bf16[4,152,128]{2,1,0:T(8,128)(2,1)} %get-tuple-element.28.refs_0_), channel_id=1, source_target_pairs={{0,128},{16,144},{1,129},{17,145},{2,130},{18,146},{3,131},{19,147... | collective-permute-start | bytes 466952 | tf_op jit(solution)/shard_map/ppermute | solution.py:39
  126.4 16.1 %collective-permute-start.21 = (bf16[4,152,128]{2,1,0:T(8,128)(2,1)}, bf16[4,152,128]{2,1,0:T(8,128)(2,1)S(1)}, u32[]{:S(2)}, u32[]{:S(2)}) collective-permute-start(bf16[4,152,128]{2,1,0:T(8,128)(2,1)} %get-tuple-element.28.refs_0_), channel_id=1, source_target_pairs={{0,64},{16,80},{1,65},{17,81},{2,66},{18,82},{3,67},{19,83},{4,68}... | collective-permute-start | bytes 466952 | tf_op jit(solution)/shard_map/ppermute | solution.py:39
  127.3 15.2 %collective-permute-start.22 = (bf16[4,152,128]{2,1,0:T(8,128)(2,1)}, bf16[4,152,128]{2,1,0:T(8,128)(2,1)S(1)}, u32[]{:S(2)}, u32[]{:S(2)}) collective-permute-start(bf16[4,152,128]{2,1,0:T(8,128)(2,1)} %get-tuple-element.29.refs_4_), channel_id=1, source_target_pairs={{0,40},{16,56},{1,41},{17,57},{2,42},{18,58},{3,43},{19,59},{4,44}... | collective-permute-start | bytes 466952 | tf_op jit(solution)/shard_map/ppermute | solution.py:39
  129.6 12.9 %collective-permute-start.23 = (bf16[4,152,128]{2,1,0:T(8,128)(2,1)}, bf16[4,152,128]{2,1,0:T(8,128)(2,1)S(1)}, u32[]{:S(2)}, u32[]{:S(2)}) collective-permute-start(bf16[4,152,128]{2,1,0:T(8,128)(2,1)} %get-tuple-element.29.refs_4_), channel_id=1, source_target_pairs={{0,32},{16,48},{1,33},{17,49},{2,34},{18,50},{3,35},{19,51},{4,36}... | collective-permute-start | bytes 466952 | tf_op jit(solution)/shard_map/ppermute | solution.py:39
  132.4 10.2 %copy-start.12 = (bf16[4,152,128]{2,1,0:T(8,128)(2,1)}, bf16[4,152,128]{2,1,0:T(8,128)(2,1)S(1)}, u32[]{:S(2)}) copy-start(bf16[4,152,128]{2,1,0:T(8,128)(2,1)S(1)} %collective-permute-done.19.refs_1_) | copy-start | bytes 466948
  132.4 10.1 %collective-permute-start.24 = (bf16[4,152,128]{2,1,0:T(8,128)(2,1)}, bf16[4,152,128]{2,1,0:T(8,128)(2,1)S(1)}, u32[]{:S(2)}, u32[]{:S(2)}) collective-permute-start(bf16[4,152,128]{2,1,0:T(8,128)(2,1)} %get-tuple-element.29.refs_4_), channel_id=1, source_target_pairs={{0,8},{16,24},{1,9},{17,25},{2,10},{18,26},{3,11},{19,27},{4,12},{... | collective-permute-start | bytes 466952 | tf_op jit(solution)/shard_map/ppermute | solution.py:39
  142.5 0.7 copy-start.13
  142.5 0.7 copy-start.14
  142.5 0.7 copy-start.15
  142.5 0.8 copy-start.16
  143.3 0.7 copy-start.17
  146.4 8.7 %collective-permute-start.25 = (bf16[4,152,128]{2,1,0:T(8,128)(2,1)}, bf16[4,152,128]{2,1,0:T(8,128)(2,1)S(1)}, u32[]{:S(2)}, u32[]{:S(2)}) collective-permute-start(bf16[4,152,128]{2,1,0:T(8,128)(2,1)} %get-tuple-element.31), channel_id=1, source_target_pairs={{0,40},{16,56},{1,41},{17,57},{2,42},{18,58},{3,43},{19,59},{4,44}... | collective-permute-start | bytes 466952 | tf_op jit(solution)/shard_map/ppermute | solution.py:39
  148.7 16.6 %collective-permute-start.26 = (bf16[4,152,128]{2,1,0:T(8,128)(2,1)}, bf16[4,152,128]{2,1,0:T(8,128)(2,1)S(1)}, u32[]{:S(2)}, u32[]{:S(2)}) collective-permute-start(bf16[4,152,128]{2,1,0:T(8,128)(2,1)} %get-tuple-element.32), channel_id=1, source_target_pairs={{0,32},{16,48},{1,33},{17,49},{2,34},{18,50},{3,35},{19,51},{4,36}... | collective-permute-start | bytes 466952 | tf_op jit(solution)/shard_map/ppermute | solution.py:39
  152.2 13.2 %collective-permute-start.27 = (bf16[4,152,128]{2,1,0:T(8,128)(2,1)}, bf16[4,152,128]{2,1,0:T(8,128)(2,1)S(1)}, u32[]{:S(2)}, u32[]{:S(2)}) collective-permute-start(bf16[4,152,128]{2,1,0:T(8,128)(2,1)} %get-tuple-element.33), channel_id=1, source_target_pairs={{0,8},{16,24},{1,9},{17,25},{2,10},{18,26},{3,11},{19,27},{4,12},{... | collective-permute-start | bytes 466952 | tf_op jit(solution)/shard_map/ppermute | solution.py:39
  153.5 11.9 %collective-permute-start.28 = (bf16[4,152,128]{2,1,0:T(8,128)(2,1)}, bf16[4,152,128]{2,1,0:T(8,128)(2,1)S(1)}, u32[]{:S(2)}, u32[]{:S(2)}) collective-permute-start(bf16[4,152,128]{2,1,0:T(8,128)(2,1)} %get-tuple-element.35), channel_id=1, source_target_pairs={{0,192},{16,208},{1,193},{17,209},{2,194},{18,210},{3,195},{19,211... | collective-permute-start | bytes 466952 | tf_op jit(solution)/shard_map/ppermute | solution.py:39
  153.5 11.9 %collective-permute-start.29 = (bf16[4,152,128]{2,1,0:T(8,128)(2,1)}, bf16[4,152,128]{2,1,0:T(8,128)(2,1)S(1)}, u32[]{:S(2)}, u32[]{:S(2)}) collective-permute-start(bf16[4,152,128]{2,1,0:T(8,128)(2,1)} %get-tuple-element.36), channel_id=1, source_target_pairs={{0,128},{16,144},{1,129},{17,145},{2,130},{18,146},{3,131},{19,147... | collective-permute-start | bytes 466952 | tf_op jit(solution)/shard_map/ppermute | solution.py:39
  155.1 10.3 %copy-start.6 = (bf16[4,152,128]{2,1,0:T(8,128)(2,1)}, bf16[4,152,128]{2,1,0:T(8,128)(2,1)S(1)}, u32[]{:S(2)}) copy-start(bf16[4,152,128]{2,1,0:T(8,128)(2,1)S(1)} %collective-permute-done.25.refs_1_) | copy-start | bytes 466948
  155.1 10.3 %collective-permute-start.30 = (bf16[4,152,128]{2,1,0:T(8,128)(2,1)}, bf16[4,152,128]{2,1,0:T(8,128)(2,1)S(1)}, u32[]{:S(2)}, u32[]{:S(2)}) collective-permute-start(bf16[4,152,128]{2,1,0:T(8,128)(2,1)} %get-tuple-element.37), channel_id=1, source_target_pairs={{0,64},{16,80},{1,65},{17,81},{2,66},{18,82},{3,67},{19,83},{4,68}... | collective-permute-start | bytes 466952 | tf_op jit(solution)/shard_map/ppermute | solution.py:39
  165.4 0.7 copy-start.7
  165.4 0.7 copy-start.8
  165.4 0.8 copy-start.9
  165.4 0.8 copy-start.10
  165.4 0.8 copy-start.11
  176.0 20.2 %collective-permute-start.31 = (bf16[4,16,4096]{2,1,0:T(8,128)(2,1)S(1)}, bf16[4,16,4096]{2,1,0:T(8,128)(2,1)S(1)}, u32[]{:S(2)}, u32[]{:S(2)}) collective-permute-start(bf16[4,16,4096]{2,1,0:T(8,128)(2,1)S(1)} %pad_maximum_fusion.4), channel_id=1, source_target_pairs={{0,40},{16,56},{1,41},{17,57},{2,42},{18,58},{3,43},{19,59},{4,44}... | collective-permute-start | bytes 1572872 | tf_op jit(solution)/shard_map/ppermute | solution.py:39
  179.7 16.6 %collective-permute-start.32 = (bf16[4,16,4096]{2,1,0:T(8,128)(2,1)S(1)}, bf16[4,16,4096]{2,1,0:T(8,128)(2,1)S(1)}, u32[]{:S(2)}, u32[]{:S(2)}) collective-permute-start(bf16[4,16,4096]{2,1,0:T(8,128)(2,1)S(1)} %pad_maximum_fusion.4), channel_id=1, source_target_pairs={{0,32},{16,48},{1,33},{17,49},{2,34},{18,50},{3,35},{19,51},{4,36}... | collective-permute-start | bytes 1572872 | tf_op jit(solution)/shard_map/ppermute | solution.py:39
  179.7 21.1 %collective-permute-start.33 = (bf16[4,16,4096]{2,1,0:T(8,128)(2,1)S(1)}, bf16[4,16,4096]{2,1,0:T(8,128)(2,1)S(1)}, u32[]{:S(2)}, u32[]{:S(2)}) collective-permute-start(bf16[4,16,4096]{2,1,0:T(8,128)(2,1)S(1)} %pad_maximum_fusion.4), channel_id=1, source_target_pairs={{0,8},{16,24},{1,9},{17,25},{2,10},{18,26},{3,11},{19,27},{4,12},{... | collective-permute-start | bytes 1572872 | tf_op jit(solution)/shard_map/ppermute | solution.py:39
  200.7 1.0 copy-start.1
  201.0 4.9 %copy-start = (bf16[4,4,16,4096]{3,2,1,0:T(8,128)(2,1)}, bf16[4,4,16,4096]{3,2,1,0:T(8,128)(2,1)S(1)}, u32[]{:S(2)}) copy-start(bf16[4,4,16,4096]{3,2,1,0:T(8,128)(2,1)S(1)} %pad_maximum_fusion.own_ref) | copy-start | bytes 6291460
  201.0 4.8 %collective-permute-start.34 = (bf16[4,4,16,4096]{3,2,1,0:T(8,128)(2,1)S(1)}, bf16[4,4,16,4096]{3,2,1,0:T(8,128)(2,1)}, u32[]{:S(2)}, u32[]{:S(2)}) collective-permute-start(bf16[4,4,16,4096]{3,2,1,0:T(8,128)(2,1)S(1)} %pad_maximum_fusion.own_ref), channel_id=1, source_target_pairs={{0,16},{16,0},{1,17},{17,1},{2,18},{18,2},{3,19},{19,3},{4,20},{20... | collective-permute-start | bytes 6291464 | tf_op jit(solution)/shard_map/ppermute | solution.py:39
  202.5 8.7 %collective-permute-start.3 = (bf16[512,256]{1,0:T(8,128)(2,1)S(1)}, bf16[512,256]{1,0:T(8,128)(2,1)S(1)}, u32[]{:S(2)}, u32[]{:S(2)}) collective-permute-start(bf16[512,256]{1,0:T(8,128)(2,1)S(1)} %get-tuple-element.46), channel_id=1, source_target_pairs={{0,8},{16,24},{1,9},{17,25},{2,10},{18,26},{3,11},{19,27},{4,12},{... | collective-permute-start | bytes 786440 | tf_op jit(solution)/shard_map/ppermute | solution.py:39
  211.2 20.4 %copy-start.5 = (bf16[512,256]{1,0:T(8,128)(2,1)}, bf16[512,256]{1,0:T(8,128)(2,1)S(1)}, u32[]{:S(2)}) copy-start(bf16[512,256]{1,0:T(8,128)(2,1)S(1)} %collective-permute-done.3.residual_ref) | copy-start | bytes 786436
  238.3 8.7 %collective-permute-start.35 = (bf16[512,256]{1,0:T(8,128)(2,1)}, bf16[512,256]{1,0:T(8,128)(2,1)S(1)}, u32[]{:S(2)}, u32[]{:S(2)}) collective-permute-start(bf16[512,256]{1,0:T(8,128)(2,1)} %output.2), channel_id=1, source_target_pairs={{0,8},{16,24},{1,9},{17,25},{2,10},{18,26},{3,11},{19,27},{4,12},{... | collective-permute-start | bytes 786440 | tf_op jit(solution)/shard_map/ppermute | solution.py:39
Sparse Core Ops, SparseCore 0:
  18.0 57.2 all-gather.5
  176.1 55.4 all-gather.3
where the time goes:
time: 259 us; the launch traced here: 256 us
  waiting for transfers between devices  113 us (44%)
  Pallas kernels  68.1 us (26%)
  starting transfers between devices  45 us (17%)
  between operations  13.9 us (5%)
  other arithmetic  9.07 us (4%)
  local copies, waits for them, and re-layouts  6.22 us (2%)
    ppermute x36, waiting for transfers between devices, send(): return lax.ppermute(value, AXES, permutation(move))  92.8 us
    ppermute x36, starting transfers between devices, send(): return lax.ppermute(value, AXES, permutation(move))  45 us
    all_gather x2, waiting for transfers between devices, gather_line(): return lax.all_gather(value, AXES, axis=0, axis_index_groups=groups)  20.4 us
    pallas_call x1, Pallas kernels, project(): pl.pallas_call(project_kernel, out_shape=jax.ShapeDtypeStruct((3, 4, BLK,...  16.8 us
    pallas_call x2, Pallas kernels, inner(): pl.pallas_call(functools.partial(inner_kernel, index), grid_spec=pltpu.Pr...  15.8 us
    pallas_call x2, Pallas kernels, output(): pl.pallas_call(functools.partial(output_kernel, side), out_shape=jax.Shap...  13.3 us
    pallas_call x1, Pallas kernels, edges(): pl.pallas_call(edge_kernel, grid_spec=pltpu.PrefetchScalarGridSpec(num_sc...  9.73 us
    pallas_call x1, Pallas kernels, assemble(): pl.pallas_call(assemble_kernel, out_shape=jax.ShapeDtypeStruct((2, PIECE,...  5.37 us
  transfers between devices with their start and end apart: 38, of which 16 were waited for; matrix products, arithmetic and copies ran while one was open for 3% of the time, Pallas kernels for 11%

commit v1 on v0

--- a/solution.py
+++ b/solution.py
@@ -138,9 +138,9 @@
     for copy in started:
         copy.wait()
 
-    def half(part, carry):
-        lax.fori_loop(part * 8, part * 8 + 8, finish, 0)
-        depth = pl.ds(pl.multiple_of(part * (D // 2), D // 2), D // 2)
+    def quarter(part, carry):
+        lax.fori_loop(part * 4, part * 4 + 4, finish, 0)
+        depth = pl.ds(pl.multiple_of(part * 1024, 1024), 1024)
 
         def step(i, carry):
             branch, group = i // 2, lax.rem(i, 2)
@@ -154,7 +154,7 @@
             def _():
                 total[branch, rows, :] = product
 
-            @pl.when(part == 1)
+            @pl.when(part > 0)
             def _():
                 total[branch, rows, :] += product
 
@@ -162,7 +162,7 @@
 
         return lax.fori_loop(0, 6, step, carry)
 
-    lax.fori_loop(0, 2, half, 0)
+    lax.fori_loop(0, 4, quarter, 0)
     for group in range(2):
         square = jnp.sum(s_scratch[group].astype(jnp.float32), axis=0)
         for i in range(2):
@@ -283,63 +283,61 @@
     )(starts, ends, proj, taps)
 
 
-def taps_of(shifted, medium_ref, lanes, base, first, last, rows):
-    def step(turn, total):
-        at = pl.multiple_of(base - turn * TAIL, TAIL)
-        weights = medium_ref[pl.ds(pl.multiple_of(turn * TAIL, TAIL), TAIL), lanes]
-        for s in range(TAIL):
-            total = total + shifted[s, pl.ds(at, rows), :] * weights[s : s + 1, :]
-        return total
-
-    return lax.fori_loop(first, last, step, jnp.zeros((rows, LANES), jnp.float32))
-
-
-GROUP = 64
+def add_turn(total, shifted, weights, turn, at, first, last):
+    part = total[first:last]
+    for s in range(TAIL):
+        tap = turn * TAIL + s
+        part = part + shifted[s, at : at + last - first, :] * weights[tap : tap + 1, :]
+    pieces = [total[:first]] * (first > 0) + [part] + [total[last:]] * (last < total.shape[0])
+    return jnp.concatenate(pieces, axis=0) if len(pieces) > 1 else part
+
+
+def each_genome(ends_ref, start, rows, body):
+    def genome(g, carry):
+        low = jnp.where(g == 0, 0, ends_ref[jnp.maximum(g - 1, 0)])
+        high = ends_ref[g]
+
+        @pl.when((low < start + rows) & (high > start))
+        def _():
+            body(low, high)
+
+        return carry
+
+    lax.fori_loop(0, 4, genome, 0)
+
+
+def lanes_of(part):
+    return pl.ds(pl.multiple_of(part * LANES, LANES), LANES)
 
 
 def inner_kernel(index, start_ref, ends_ref, product_ref, medium_ref, out_ref, shifted):
     start = start_ref[index * 2 + pl.program_id(0)]
     row = start + lax.broadcasted_iota(jnp.int32, (BLK, LANES), 0)
-    cut = split_by_genome(start, ends_ref)
-
-    for part in range(2):
-        lanes = pl.ds(part * LANES, LANES)
+
+    def segment(part, carry):
+        lanes = lanes_of(part)
 
         def run(low, high):
-            value = product_ref[0, :, lanes].astype(jnp.float32)
-            if low is not None:
-                value = jnp.where(row >= low, value, 0.0)
+            value = jnp.where(row >= low, product_ref[0, :, lanes].astype(jnp.float32), 0.0)
             for s in range(TAIL):
-                shifted[s, : GROUP + TAIL, :] = jnp.zeros((GROUP + TAIL, LANES), jnp.float32)
-                shifted[s, GROUP + s : GROUP + BLK, :] = value[: BLK - s, :]
-            for r in range(BLK // GROUP):
-                last = min(MED // TAIL, (r + 1) * GROUP // TAIL)
-                total = taps_of(
-                    shifted, medium_ref, lanes, GROUP + r * GROUP, 0, last, GROUP
-                )
-                rows = pl.ds(r * GROUP, GROUP)
-                if low is not None:
-                    here = row[r * GROUP : (r + 1) * GROUP]
-                    total = jnp.where((here >= low) & (here < high), total, out_ref[0, rows, lanes])
-                out_ref[0, rows, lanes] = total
-
-        @pl.when(jnp.logical_not(cut))
-        def _():
-            run(None, None)
-
-        @pl.when(cut)
-        def _():
-            def genome(g, carry):
-                low = jnp.where(g == 0, 0, ends_ref[jnp.maximum(g - 1, 0)])
-                high = ends_ref[g]
-
-                @pl.when((low < start + BLK) & (high > start))
-                def _():
-                    run(low, high)
-
-                return carry
-
-            lax.fori_loop(0, 4, genome, 0)
+                shifted[s, :TAIL, :] = jnp.zeros((TAIL, LANES), jnp.float32)
+                shifted[s, s:BLK, :] = value[: BLK - s, :]
+            weights = medium_ref.at[:, lanes]
+            for begin in (0, MED):
+                total = jnp.zeros((MED, LANES), jnp.float32)
+                for turn in range(MED // TAIL):
+                    first = max(0, turn * TAIL - begin)
+                    at = begin + first - turn * TAIL
+                    total = add_turn(total, shifted, weights, turn, at, first, MED)
+                rows = pl.ds(begin, MED)
+                here = row[begin : begin + MED]
+                inside = (here >= low) & (here < high)
+                out_ref[0, rows, lanes] = jnp.where(inside, total, out_ref[0, rows, lanes])
+
+        each_genome(ends_ref, start, BLK, run)
+        return carry
+
+    lax.fori_loop(0, 2, segment, 0)
 
 
 def inner(index, starts, ends, product, medium):
@@ -353,7 +351,7 @@
                 pl.BlockSpec((MED, 2 * LANES), lambda i, *_: (0, 0)),
             ],
             out_specs=pl.BlockSpec((1, BLK, 2 * LANES), lambda i, *_: (i, 0, 0)),
-            scratch_shapes=[pltpu.VMEM((TAIL, GROUP + BLK, LANES), jnp.float32)],
+            scratch_shapes=[pltpu.VMEM((TAIL, BLK, LANES), jnp.float32)],
         ),
         out_shape=jax.ShapeDtypeStruct((2, BLK, 2 * LANES), jnp.float32),
         cost_estimate=pl.CostEstimate(
@@ -397,68 +395,67 @@
     row = start - MED + lax.broadcasted_iota(jnp.int32, (near, LANES), 0)
     out_row = start + lax.broadcasted_iota(jnp.int32, (near, LANES), 0)
     for part in range(2):
-        lanes = pl.ds(part * LANES, LANES)
         for m in range(4):
 
             @pl.when(pick_ref[part, block] == m)
-            def _(m=m):
-                halo[...] = halos[part * 4 + m][0].astype(jnp.float32)
-
+            def _(part=part, m=m):
+                halo[part] = halos[part * 4 + m][0].astype(jnp.float32)
+
+    @pl.when(block < 2)
+    def _():
+        filtered[...] = early_ref[0]
+
+    @pl.when(block >= 2)
+    def _():
+        filtered[...] = late_ref[0]
+
+    def segment(part, carry):
+        lanes = lanes_of(part)
+        taps = taps_ref.at[:, :, lanes]
         mixes = []
         for branch in (1, 2):
             at = MED + branch * TAIL
-            small[:TAIL, :] = halo[at : at + TAIL, :]
+            small[:TAIL, :] = halo[part, at : at + TAIL, :]
             small[TAIL:, :] = proj_ref[branch, 0, : 2 * TAIL, lanes][:TAIL].astype(jnp.float32)
-            mixes.append(short_mix(small, reach8, taps_ref, branch, TAIL, lanes))
+            mixes.append(short_mix(small, reach8, taps, branch, TAIL, slice(None)))
         first = lax.broadcasted_iota(jnp.int32, (TAIL, LANES), 0) < SHORT - 1
         early = (mixes[0] * mixes[1]).astype(jnp.bfloat16).astype(jnp.float32)
-        prior[:MED, :] = halo[:MED, :]
+        prior[:MED, :] = halo[part, :MED, :]
         prior[MED:, :] = jnp.where(first, early, 0.0)
 
-        @pl.when(block < 2)
-        def _():
-            filtered[...] = early_ref[0, :, lanes]
-
-        @pl.when(block >= 2)
-        def _():
-            filtered[...] = late_ref[0, :, lanes]
-
-        def genome(g, carry):
-            low = jnp.where(g == 0, 0, ends_ref[jnp.maximum(g - 1, 0)])
-            high = ends_ref[g]
-
-            @pl.when((low < start + near) & (high > start))
-            def _():
-                value = jnp.where(row >= low, prior[...], 0.0)
-                for s in range(TAIL):
-                    shifted[s, TAIL : TAIL + TAIL, :] = jnp.zeros((TAIL, LANES), jnp.float32)
-                    shifted[s, near + TAIL :, :] = jnp.zeros((GROUP, LANES), jnp.float32)
-                    shifted[s, TAIL + s : TAIL + s + near, :] = value
-                for at, rows, begin in ((0, GROUP, 0), (GROUP, GROUP, 7), (2 * GROUP, TAIL, 15)):
-                    total = taps_of(
-                        shifted, medium_ref, lanes, TAIL + MED + at, begin, MED // TAIL, rows
-                    )
-                    here = out_row[at : at + rows]
-                    total = jnp.where((here >= low) & (here < high), total, 0.0)
-                    filtered[at : at + rows, :] += total
-
-            return carry
-
-        lax.fori_loop(0, 4, genome, 0)
-        window[:TAIL, :] = halo[MED : MED + TAIL, :]
+        def run(low, high):
+            value = jnp.where(row >= low, prior[...], 0.0)
+            for s in range(TAIL):
+                shifted[s, near : near + TAIL, :] = jnp.zeros((TAIL, LANES), jnp.float32)
+                shifted[s, s : s + near, :] = value
+            weights = medium_ref.at[:, lanes]
+            total = jnp.zeros((near, LANES), jnp.float32)
+            for turn in range(MED // TAIL):
+                last = min((turn + 2) * TAIL, near)
+                at = MED - turn * TAIL
+                total = add_turn(total, shifted, weights, turn, at, 0, last)
+            inside = (out_row >= low) & (out_row < high)
+            filtered[:near, lanes] += jnp.where(inside, total, 0.0)
+
+        each_genome(ends_ref, start, near, run)
+        window[:TAIL, :] = halo[part, MED : MED + TAIL, :]
         window[TAIL:, :] = proj_ref[0, 0, :, lanes].astype(jnp.float32)
 
         @pl.when(cut)
         def _():
-            mixed = short_mix(window, reach_of(start, BLK, ends_ref), taps_ref, 0, BLK, lanes)
-            out_ref[0, :, lanes] = (mixed * filtered[...]).astype(jnp.bfloat16)
+            mixed = short_mix(window, reach_of(start, BLK, ends_ref), taps, 0, BLK, slice(None))
+            out_ref[0, :, lanes] = (mixed * filtered[:, lanes]).astype(jnp.bfloat16)
 
         @pl.when(jnp.logical_not(cut))
         def _():
-            head = short_mix(window, reach8, taps_ref, 0, TAIL, lanes)
-            mixed = short_mix(window, None, taps_ref, 0, BLK, lanes)
+            head = short_mix(window, reach8, taps, 0, TAIL, slice(None))
+            mixed = short_mix(window, None, taps, 0, BLK, slice(None))
             mixed = jnp.concatenate([head, mixed[TAIL:]], axis=0)
-            out_ref[0, :, lanes] = (mixed * filtered[...]).astype(jnp.bfloat16)
+            out_ref[0, :, lanes] = (mixed * filtered[:, lanes]).astype(jnp.bfloat16)
+
+        return carry
+
+    lax.fori_loop(0, 2, segment, 0)
 
 
 def edges(starts, ends, picks, proj, partials, taps, medium, halos):
@@ -477,12 +474,12 @@
             + [pl.BlockSpec((1, HALO, LANES), lambda i, *_: (i, 0, 0))] * 8,
             out_specs=pl.BlockSpec((1, BLK, 2 * LANES), lambda i, *_: (i, 0, 0)),
             scratch_shapes=[
-                pltpu.VMEM((HALO, LANES), jnp.float32),
+                pltpu.VMEM((2, HALO, LANES), jnp.float32),
                 pltpu.VMEM((BLK + TAIL, LANES), jnp.float32),
                 pltpu.VMEM((2 * TAIL, LANES), jnp.float32),
                 pltpu.VMEM((MED + TAIL, LANES), jnp.float32),
-                pltpu.VMEM((TAIL, MED + 2 * TAIL + GROUP, LANES), jnp.float32),
-                pltpu.VMEM((BLK, LANES), jnp.float32),
+                pltpu.VMEM((TAIL, MED + 2 * TAIL, LANES), jnp.float32),
+                pltpu.VMEM((BLK, 2 * LANES), jnp.float32),
             ],
         ),
         out_shape=jax.ShapeDtypeStruct((4, BLK, 2 * LANES), jnp.bfloat16),
@@ -525,26 +522,32 @@
     )(place, own, other)
 
 
-def output_kernel(side, place_ref, residual_ref, w_ref, gated_ref, out_ref, scratch, weights, total, sems, w_sem):
+def output_kernel(
+    side, place_ref, residual_ref, w_ref, gated_ref, out_ref, scratch, weights, total, sems, w_sems
+):
     core, y_low = place_ref[2], place_ref[3]
-    load = pltpu.make_async_copy(w_ref.at[lax.rem(y_low + side, 2)], weights, w_sem)
-    load.start()
-    started = []
-    for z in range(8):
-        for owner in range(2):
-            lanes = pl.ds((z * 2 + owner) * PIECE, PIECE)
-            source = gated_ref.at[z * 2 + owner, lax.rem(core + owner, 2)]
-            started.append(
-                pltpu.make_async_copy(source, scratch.at[:, lanes], sems.at[z, owner])
-            )
-    for copy in started:
-        copy.start()
-    for copy in started:
-        copy.wait()
-    load.wait()
+    column = lax.rem(y_low + side, 2)
+
+    def copies(i):
+        lanes = pl.ds(pl.multiple_of(i * 1024, 1024), 1024)
+        made = [pltpu.make_async_copy(w_ref.at[column, :, lanes], weights.at[:, lanes], w_sems.at[i])]
+        for k in range(4):
+            lanes = pl.ds(pl.multiple_of((i * 4 + k) * PIECE, PIECE), PIECE)
+            source = gated_ref.at[i * 4 + k, lax.rem(core + k, 2)]
+            made.append(pltpu.make_async_copy(source, scratch.at[:, lanes], sems.at[i, k]))
+        return made
+
+    def start(i, carry):
+        for copy in copies(i):
+            copy.start()
+        return carry
+
+    lax.fori_loop(0, 4, start, 0)
     total[...] = residual_ref[...].astype(jnp.float32)
 
     def step(i, carry):
+        for copy in copies(i):
+            copy.wait()
         lanes = pl.ds(pl.multiple_of(i * 1024, 1024), 1024)
         total[...] += lax.dot_general(
             scratch[:, lanes], weights[:, lanes], (((1,), (1,)), ((), ())),
@@ -566,8 +569,8 @@
             pltpu.VMEM((HALF, D), jnp.bfloat16),
             pltpu.VMEM((PIECE, D), jnp.bfloat16),
             pltpu.VMEM((HALF, PIECE), jnp.float32),
-            pltpu.SemaphoreType.DMA((8, 2)),
-            pltpu.SemaphoreType.DMA,
+            pltpu.SemaphoreType.DMA((4, 4)),
+            pltpu.SemaphoreType.DMA((4,)),
         ],
         cost_estimate=pl.CostEstimate(
             flops=2 * HALF * D * PIECE, bytes_accessed=6 << 20, transcendentals=0
@@ -619,7 +622,6 @@
     columns = out_weight.reshape(2, 8, 2, LANES, 16).transpose(4, 1, 2, 0, 3).reshape(16, D)
     columns = axis_of(columns, along_x)
     columns = jnp.stack(columns)
-    place, columns = lax.optimization_barrier((place, columns))
     proj = project(place, line, weights)
 
     both = jnp.concatenate([short_filter.reshape(SHORT * 3, PIECE), medium_filter], axis=0)
@@ -654,6 +656,7 @@
     starts = (ids[:4] * BLK).astype(jnp.int32)
     ends = jnp.cumsum(genome_lengths).astype(jnp.int32)
 
+    starts, columns = lax.optimization_barrier((starts, columns))
     product, low, high = products(starts, ends, proj, taps)
     rows_x, rows_y = axis_of(low, along_x), axis_of(high, along_y)
     partials = [inner(i, starts, ends, product, medium) for i in range(2)]

time: 259 us -> 253 us (0.977)
  Pallas kernels: 68.1 us -> 62.4 us
  waiting for transfers between devices: 113 us -> 116 us
    ppermute x36, waiting for transfers between devices: 92.8 us -> 96.5 us  [send(): return lax.ppermute(value, AXES, permutation(move))]
    pallas_call x2, Pallas kernels: 13.3 us -> 10.3 us  [output(): pl.pallas_call(functools.partial(output_kernel, side), out_shape=jax.Shap...]
    pallas_call x2, Pallas kernels: 15.8 us -> 12.8 us  [inner(): pl.pallas_call(functools.partial(inner_kernel, index), grid_spec=pltpu.Pr...]
  transfers between devices with their start and end apart: 38 -> 38, of which waited for: 16 -> 16; matrix products, arithmetic and copies ran while one was open for 3% -> 3% of each run, Pallas kernels for 11% -> 9%
where the time goes in v1:
time: 253 us; the launch traced here: 250 us
  waiting for transfers between devices  116 us (46%)
  Pallas kernels  62.4 us (25%)
  starting transfers between devices  42.6 us (17%)
  between operations  13.9 us (5%)
  other arithmetic  9.07 us (4%)
  local copies, waits for them, and re-layouts  6.23 us (2%)
    ppermute x36, waiting for transfers between devices, send(): return lax.ppermute(value, AXES, permutation(move))  96.5 us
    ppermute x36, starting transfers between devices, send(): return lax.ppermute(value, AXES, permutation(move))  42.5 us
    all_gather x2, waiting for transfers between devices, gather_line(): return lax.all_gather(value, AXES, axis=0, axis_index_groups=groups)  19.6 us
    pallas_call x1, Pallas kernels, project(): pl.pallas_call(project_kernel, out_shape=jax.ShapeDtypeStruct((3, 4, BLK,...  18.8 us
    pallas_call x2, Pallas kernels, inner(): pl.pallas_call(functools.partial(inner_kernel, index), grid_spec=pltpu.Pr...  12.8 us
    pallas_call x2, Pallas kernels, output(): pl.pallas_call(functools.partial(output_kernel, side), out_shape=jax.Shap...  10.3 us
    pallas_call x1, Pallas kernels, edges(): pl.pallas_call(edge_kernel, grid_spec=pltpu.PrefetchScalarGridSpec(num_sc...  7.92 us
    pallas_call x1, Pallas kernels, assemble(): pl.pallas_call(assemble_kernel, out_shape=jax.ShapeDtypeStruct((2, PIECE,...  5.37 us
  transfers between devices with their start and end apart: 38, of which 16 were waited for; matrix products, arithmetic and copies ran while one was open for 3% of the time, Pallas kernels for 9%

profile of v1, /device:TPU:32, one launch (start us, length us, event | category | flops | bytes accessed | tf_op | source)
XLA Modules:
  0.0 250.4 jit_solution(10378229815668597147)
XLA Ops:
  6.5 0.7 reshape.315
  7.3 1.3 fusion.1
  8.8 1.7 collective-permute-start.4
  10.5 6.6 %collective-permute-done.4 = bf16[520,256]{1,0:T(8,128)(2,1)S(1)} collective-permute-done((bf16[520,256]{1,0:T(8,128)(2,1)S(1)}, bf16[520,256]{1,0:T(8,128)(2,1)S(1)}, u32[]{:S(2)}, u32[]{:S(2)}) %collective-permute-start.4) | collective-permute-done | bytes 266272 | tf_op jit(solution)/shard_map/ppermute | solution.py:39
  17.0 0.9 pad_maximum_fusion.3
  18.6 2.8 %collective-permute-start.5 = (bf16[3,256,128]{2,1,0:T(8,128)(2,1)S(1)}, bf16[3,256,128]{2,1,0:T(8,128)(2,1)S(1)}, u32[]{:S(2)}, u32[]{:S(2)}) collective-permute-start(bf16[3,256,128]{2,1,0:T(8,128)(2,1)S(1)} %get-tuple-element.50), channel_id=1, source_target_pairs={{0,192},{16,208},{1,193},{17,209},{2,194},{18,210},{3,195},{19,211... | collective-permute-start | bytes 589832 | tf_op jit(solution)/shard_map/ppermute | solution.py:39
  21.5 0.8 collective-permute-start.6
  22.3 0.9 collective-permute-start.7
  23.4 2.4 collective-permute-start.1
  26.4 0.7 reduce-window.9
  27.3 2.4 collective-permute-done.5
  29.8 0.9 collective-permute-done.6
  30.6 2.1 collective-permute-done.7
  32.8 1.7 collective-permute-start.10
  34.7 0.7 stack.93.place_ref
  35.5 1.7 collective-permute-start.12
  37.2 2.0 collective-permute-start.13
  39.2 0.7 collective-permute-start.14
  40.4 3.0 %collective-permute-done.12 = bf16[3,256,128]{2,1,0:T(8,128)(2,1)S(1)} collective-permute-done((bf16[3,256,128]{2,1,0:T(8,128)(2,1)S(1)}, bf16[3,256,128]{2,1,0:T(8,128)(2,1)S(1)}, u32[]{:S(2)}, u32[]{:S(2)}) %collective-permute-start.12) | collective-permute-done | bytes 196640 | tf_op jit(solution)/shard_map/ppermute | solution.py:39
  43.4 0.8 collective-permute-start.2
  44.2 15.9 %collective-permute-done.13 = bf16[3,256,128]{2,1,0:T(8,128)(2,1)S(1)} collective-permute-done((bf16[3,256,128]{2,1,0:T(8,128)(2,1)S(1)}, bf16[3,256,128]{2,1,0:T(8,128)(2,1)S(1)}, u32[]{:S(2)}, u32[]{:S(2)}) %collective-permute-start.13) | collective-permute-done | bytes 196640 | tf_op jit(solution)/shard_map/ppermute | solution.py:39
  60.0 1.7 collective-permute-done.14
  62.2 3.5 %collective-permute-done.18 = bf16[149,128]{1,0:T(8,128)(2,1)S(1)} collective-permute-done((bf16[149,128]{1,0:T(8,128)(2,1)S(1)}, bf16[149,128]{1,0:T(8,128)(2,1)S(1)}, u32[]{:S(2)}, u32[]{:S(2)}) %collective-permute-start.18) | collective-permute-done | bytes 38176 | tf_op jit(solution)/shard_map/ppermute | solution.py:39
  65.7 1.8 collective-permute-start.8
  67.5 0.6 collective-permute-start.9
  68.1 1.2 collective-permute-start.15
  69.3 0.9 collective-permute-start.17
  70.3 0.6 reshape.319.taps_ref
  71.0 28.6 %collective-permute-done.8.refs_1_ = bf16[4,3,256,128]{3,2,1,0:T(8,128)(2,1)} collective-permute-done((bf16[4,3,256,128]{3,2,1,0:T(8,128)(2,1)S(1)}, bf16[4,3,256,128]{3,2,1,0:T(8,128)(2,1)}, u32[]{:S(2)}, u32[]{:S(2)}) %collective-permute-start.8) | collective-permute-done | bytes 786464 | tf_op jit(solution)/shard_map/ppermute | solution.py:39
  99.6 4.2 %collective-permute-done.17.refs_7_ = bf16[4,3,256,128]{3,2,1,0:T(8,128)(2,1)} collective-permute-done((bf16[4,3,256,128]{3,2,1,0:T(8,128)(2,1)S(1)}, bf16[4,3,256,128]{3,2,1,0:T(8,128)(2,1)}, u32[]{:S(2)}, u32[]{:S(2)}) %collective-permute-start.17) | collective-permute-done | bytes 786464 | tf_op jit(solution)/shard_map/ppermute | solution.py:39
  103.8 18.8 %project.1.proj_ref = bf16[3,4,256,256]{3,2,1,0:T(8,128)(2,1)} custom-call(s32[5]{0:T(128)} %stack.93.place_ref, bf16[16,2,520,256]{3,2,1,0:T(8,128)(2,1)} %bitcast.69, bf16[4,3,256,128]{3,2,1,0:T(8,128)(2,1)} %copy-done.2, bf16[4,3,256,128]{3,2,1,0:T(8,128)(2,1)} %collective-permute-done.8.refs_1_, bf16[4,3,256,128]{3,2,1,0:T(8,128)(2,1)} %collective-permute-done.9.refs_2_, ...), custom_call_target="tpu_custom_call" | custom-call | flops 6442450944 | bytes 16777216 | tf_op jit(solution)/shard_map/project/pallas_call | solution.py:184
  122.6 4.7 %products.1 = (bf16[4,256,256]{2,1,0:T(8,128)(2,1)}, bf16[4,152,128]{2,1,0:T(8,128)(2,1)}, bf16[4,152,128]{2,1,0:T(8,128)(2,1)}) custom-call(s32[4]{0:T(128)} %slice_multiply_fusion.2.start_ref, s32[4]{0:T(128)} %bitcast.64, bf16[3,4,256,256]{3,2,1,0:T(8,128)(2,1)} %project.1.proj_ref, bf16[7,3,256]{2,1,0:T(4,128)(2,1)} %reshape.319.taps_ref), custom_call_target="tpu_custom_call" | custom-call | flops 62914560 | bytes 4194304 | tf_op jit(solution)/shard_map/products/pallas_call | solution.py:264
  127.3 1.1 collective-permute-start.19
  128.4 1.0 collective-permute-start.21
  129.4 2.2 collective-permute-start.22
  131.6 0.9 collective-permute-start.23
  132.5 1.9 collective-permute-done.19.refs_1_
  134.4 0.9 collective-permute-start.24
  135.9 0.7 fusion.4.medium_ref
  136.6 6.4 %inner.2.early_ref = f32[2,256,256]{2,1,0:T(8,128)} custom-call(s32[4]{0:T(128)} %slice_multiply_fusion.2.start_ref, s32[4]{0:T(128)} %bitcast.65, bf16[4,256,256]{2,1,0:T(8,128)(2,1)} %get-tuple-element.25.product_ref, f32[128,256]{1,0:T(8,128)} %fusion.4.medium_ref), custom_call_target="tpu_custom_call" | custom-call | flops 33554432 | bytes 1048576 | tf_op jit(solution)/shard_map/inner/pallas_call | solution.py:344
  143.8 0.7 copy-done.17
  144.5 2.5 route.1
  147.0 2.3 collective-permute-start.25
  149.3 2.4 collective-permute-start.26
  151.7 1.3 collective-permute-start.27
  153.0 1.6 collective-permute-start.29
  154.6 1.7 collective-permute-start.30
  157.0 6.4 %inner.3.late_ref = f32[2,256,256]{2,1,0:T(8,128)} custom-call(s32[4]{0:T(128)} %slice_multiply_fusion.2.start_ref, s32[4]{0:T(128)} %bitcast.66, bf16[4,256,256]{2,1,0:T(8,128)(2,1)} %get-tuple-element.25.product_ref, f32[128,256]{1,0:T(8,128)} %fusion.4.medium_ref), custom_call_target="tpu_custom_call" | custom-call | flops 33554432 | bytes 1048576 | tf_op jit(solution)/shard_map/inner/pallas_call | solution.py:344
  164.3 7.9 %edges.1 = bf16[4,256,256]{2,1,0:T(8,128)(2,1)} custom-call(s32[4]{0:T(128)} %slice_multiply_fusion.2.start_ref, s32[4]{0:T(128)} %bitcast.67, s32[2,4]{1,0:T(2,128)} %pad_add_fusion.1.pick_ref, bf16[3,4,256,256]{3,2,1,0:T(8,128)(2,1)} %project.1.proj_ref, f32[2,256,256]{2,1,0:T(8,128)} %inner.2.early_ref, f32[2,256,256]{2,1,0:T(8,128)} %inner.3.late_ref, ...), custom_call_target="tpu_custom_call" | custom-call | flops 16777216 | bytes 3145728 | tf_op jit(solution)/shard_map/edges/pallas_call | solution.py:462
  172.2 3.6 %collective-permute-start.31 = (bf16[4,16,4096]{2,1,0:T(8,128)(2,1)S(1)}, bf16[4,16,4096]{2,1,0:T(8,128)(2,1)S(1)}, u32[]{:S(2)}, u32[]{:S(2)}) collective-permute-start(bf16[4,16,4096]{2,1,0:T(8,128)(2,1)S(1)} %pad_maximum_fusion.4), channel_id=1, source_target_pairs={{0,40},{16,56},{1,41},{17,57},{2,42},{18,58},{3,43},{19,59},{4,44}... | collective-permute-start | bytes 1572872 | tf_op jit(solution)/shard_map/ppermute | solution.py:39
  175.9 1.0 collective-permute-start.33
  176.8 17.1 %collective-permute-done.31 = bf16[4,16,4096]{2,1,0:T(8,128)(2,1)S(1)} collective-permute-done((bf16[4,16,4096]{2,1,0:T(8,128)(2,1)S(1)}, bf16[4,16,4096]{2,1,0:T(8,128)(2,1)S(1)}, u32[]{:S(2)}, u32[]{:S(2)}) %collective-permute-start.31) | collective-permute-done | bytes 524320 | tf_op jit(solution)/shard_map/ppermute | solution.py:39
  194.0 3.7 %collective-permute-done.33 = bf16[4,16,4096]{2,1,0:T(8,128)(2,1)S(1)} collective-permute-done((bf16[4,16,4096]{2,1,0:T(8,128)(2,1)S(1)}, bf16[4,16,4096]{2,1,0:T(8,128)(2,1)S(1)}, u32[]{:S(2)}, u32[]{:S(2)}) %collective-permute-start.33) | collective-permute-done | bytes 524320 | tf_op jit(solution)/shard_map/ppermute | solution.py:39
  198.0 0.7 copy-done.1
  198.7 0.7 broadcast_select_fusion.3
  199.8 3.0 %collective-permute-done.34.other_ref = bf16[4,4,16,4096]{3,2,1,0:T(8,128)(2,1)} collective-permute-done((bf16[4,4,16,4096]{3,2,1,0:T(8,128)(2,1)S(1)}, bf16[4,4,16,4096]{3,2,1,0:T(8,128)(2,1)}, u32[]{:S(2)}, u32[]{:S(2)}) %collective-permute-start.34) | collective-permute-done | bytes 2097184 | tf_op jit(solution)/shard_map/ppermute | solution.py:39
  202.8 5.4 %assemble.1.w_ref = bf16[2,256,4096]{2,1,0:T(8,128)(2,1)} custom-call(s32[5]{0:T(128)} %stack.93.place_ref, bf16[4,4,16,4096]{3,2,1,0:T(8,128)(2,1)} %copy-done, bf16[4,4,16,4096]{3,2,1,0:T(8,128)(2,1)} %collective-permute-done.34.other_ref), custom_call_target="tpu_custom_call" | custom-call | flops 1024 | bytes 8388608 | tf_op jit(solution)/shard_map/assemble/pallas_call | solution.py:514
  208.2 19.6 %all-gather.4.cloned.1.call-done.gated_ref = bf16[16,2,512,256]{3,2,1,0:T(8,128)(2,1)} async-done(((bf16[1,2,512,256]{3,2,1,0:T(8,128)(2,1)}), bf16[16,2,512,256]{3,2,1,0:T(8,128)(2,1)}) %all-gather.4.cloned.1.call-update) | async-done | bytes 8388624 | tf_op jit(solution)/shard_map/all_gather | solution.py:64
  227.8 5.1 %output.2 = bf16[512,256]{1,0:T(8,128)(2,1)} custom-call(s32[5]{0:T(128)} %stack.93.place_ref, bf16[512,256]{1,0:T(8,128)(2,1)} %copy-done.5, bf16[2,256,4096]{2,1,0:T(8,128)(2,1)} %assemble.1.w_ref, bf16[16,2,512,256]{3,2,1,0:T(8,128)(2,1)} %all-gather.4.cloned.1.call-done.gated_ref), custom_call_target="tpu_custom_call" | custom-call | flops 1073741824 | bytes 6291456 | tf_op jit(solution)/shard_map/output/pallas_call | solution.py:563
  233.0 1.6 collective-permute-start.35
  234.5 5.1 %output.3 = bf16[512,256]{1,0:T(8,128)(2,1)} custom-call(s32[5]{0:T(128)} %stack.93.place_ref, bf16[512,256]{1,0:T(8,128)(2,1)} %get-tuple-element.45.residual_ref, bf16[2,256,4096]{2,1,0:T(8,128)(2,1)} %assemble.1.w_ref, bf16[16,2,512,256]{3,2,1,0:T(8,128)(2,1)} %all-gather.4.cloned.1.call-done.gated_ref), custom_call_target="tpu_custom_call" | custom-call | flops 1073741824 | bytes 6291456 | tf_op jit(solution)/shard_map/output/pallas_call | solution.py:563
  239.7 2.0 collective-permute-done.35
  241.7 1.0 broadcast_select_fusion.2
  242.7 0.8 pad_maximum_fusion.5
  (119 shorter events, 6.9 us)
Async XLA Ops:
  6.5 97.2 %all-gather.6.cloned.1.call-start = ((), (), s32[]{:S(2)}) async-start(), calls=%async_computation.1 | async-start | bytes 9052160 | tf_op jit(solution)/shard_map/all_gather | solution.py:64
  8.5 9.5 %copy-start.4 = (bf16[3,256,256]{2,1,0:T(8,128)(2,1)S(1)}, bf16[3,256,256]{2,1,0:T(8,128)(2,1)}, u32[]{:S(2)}) copy-start(bf16[3,256,256]{2,1,0:T(8,128)(2,1)} %param.10) | copy-start | bytes 1179652
  8.8 8.2 %collective-permute-start.4 = (bf16[520,256]{1,0:T(8,128)(2,1)S(1)}, bf16[520,256]{1,0:T(8,128)(2,1)S(1)}, u32[]{:S(2)}, u32[]{:S(2)}) collective-permute-start(bf16[520,256]{1,0:T(8,128)(2,1)S(1)} %get-tuple-element.42), channel_id=1, source_target_pairs={{0,8},{16,24},{1,9},{17,25},{2,10},{18,26},{3,11},{19,27},{4,12},{... | collective-permute-start | bytes 798728 | tf_op jit(solution)/shard_map/ppermute | solution.py:39
  17.9 5.3 %copy-start.18 = (bf16[4096,16]{0,1:T(8,128)(2,1)S(1)}, bf16[4096,16]{0,1:T(8,128)(2,1)}, u32[]{:S(2)}) copy-start(bf16[4096,16]{0,1:T(8,128)(2,1)} %param.13) | copy-start | bytes 393220
  17.9 209.9 %all-gather.4.cloned.1.call-start = ((), (), s32[]{:S(2)}) async-start(), calls=%async_computation | async-start | bytes 8912896 | tf_op jit(solution)/shard_map/all_gather | solution.py:64
  18.0 8.4 %copy-start.20 = (bf16[7,3,256]{2,0,1:T(8,128)(2,1)S(1)}, bf16[7,3,256]{2,0,1:T(8,128)(2,1)}, u32[]{:S(2)}) copy-start(bf16[7,3,256]{2,0,1:T(8,128)(2,1)} %param.11) | copy-start | bytes 32260
  18.0 8.4 %copy-start.21 = (s32[4]{0:T(128)S(1)}, s32[4]{0:T(128)}, u32[]{:S(2)}) copy-start(s32[4]{0:T(128)} %param.14) | copy-start | bytes 52
  18.0 9.1 %copy-start.22 = (s32[64]{0:T(128)S(1)}, s32[64]{0:T(128)}, u32[]{:S(2)}) copy-start(s32[64]{0:T(128)} %param.15) | copy-start | bytes 772
  18.4 17.0 %copy-start.19 = (bf16[128,256]{1,0:T(8,128)(2,1)S(1)}, bf16[128,256]{1,0:T(8,128)(2,1)}, u32[]{:S(2)}) copy-start(bf16[128,256]{1,0:T(8,128)(2,1)} %param.12) | copy-start | bytes 196612
  18.6 11.1 %collective-permute-start.5 = (bf16[3,256,128]{2,1,0:T(8,128)(2,1)S(1)}, bf16[3,256,128]{2,1,0:T(8,128)(2,1)S(1)}, u32[]{:S(2)}, u32[]{:S(2)}) collective-permute-start(bf16[3,256,128]{2,1,0:T(8,128)(2,1)S(1)} %get-tuple-element.50), channel_id=1, source_target_pairs={{0,192},{16,208},{1,193},{17,209},{2,194},{18,210},{3,195},{19,211... | collective-permute-start | bytes 589832 | tf_op jit(solution)/shard_map/ppermute | solution.py:39
  21.5 9.2 %collective-permute-start.6 = (bf16[3,256,128]{2,1,0:T(8,128)(2,1)S(1)}, bf16[3,256,128]{2,1,0:T(8,128)(2,1)S(1)}, u32[]{:S(2)}, u32[]{:S(2)}) collective-permute-start(bf16[3,256,128]{2,1,0:T(8,128)(2,1)S(1)} %get-tuple-element.50), channel_id=1, source_target_pairs={{0,128},{16,144},{1,129},{17,145},{2,130},{18,146},{3,131},{19,147... | collective-permute-start | bytes 589832 | tf_op jit(solution)/shard_map/ppermute | solution.py:39
  22.3 10.4 %collective-permute-start.7 = (bf16[3,256,128]{2,1,0:T(8,128)(2,1)S(1)}, bf16[3,256,128]{2,1,0:T(8,128)(2,1)S(1)}, u32[]{:S(2)}, u32[]{:S(2)}) collective-permute-start(bf16[3,256,128]{2,1,0:T(8,128)(2,1)S(1)} %get-tuple-element.50), channel_id=1, source_target_pairs={{0,64},{16,80},{1,65},{17,81},{2,66},{18,82},{3,67},{19,83},{4,68}... | collective-permute-start | bytes 589832 | tf_op jit(solution)/shard_map/ppermute | solution.py:39
  23.2 12.3 %collective-permute-start.11 = (bf16[3,256,128]{2,1,0:T(8,128)(2,1)S(1)}, bf16[3,256,128]{2,1,0:T(8,128)(2,1)S(1)}, u32[]{:S(2)}, u32[]{:S(2)}) collective-permute-start(bf16[3,256,128]{2,1,0:T(8,128)(2,1)S(1)} %get-tuple-element.49), channel_id=1, source_target_pairs={{0,16},{16,0},{1,17},{17,1},{2,18},{18,2},{3,19},{19,3},{4,20},{20... | collective-permute-start | bytes 589832 | tf_op jit(solution)/shard_map/ppermute | solution.py:39
  23.4 44.1 %collective-permute-start.1 = (bf16[16,4096]{1,0:T(8,128)(2,1)S(1)}, bf16[16,4096]{1,0:T(8,128)(2,1)S(1)}, u32[]{:S(2)}, u32[]{:S(2)}) collective-permute-start(bf16[16,4096]{1,0:T(8,128)(2,1)S(1)} %reshape.311), channel_id=1, source_target_pairs={{0,192},{16,208},{1,193},{17,209},{2,194},{18,210},{3,195},{19,211... | collective-permute-start | bytes 393224 | tf_op jit(solution)/shard_map/ppermute | solution.py:39
  32.8 71.0 %copy-start.2 = (bf16[4,3,256,128]{3,2,1,0:T(8,128)(2,1)}, bf16[4,3,256,128]{3,2,1,0:T(8,128)(2,1)S(1)}, u32[]{:S(2)}) copy-start(bf16[4,3,256,128]{3,2,1,0:T(8,128)(2,1)S(1)} %pad_maximum_fusion.1.refs_0_) | copy-start | bytes 2359300
  32.8 36.5 %collective-permute-start.10 = (bf16[4,3,256,128]{3,2,1,0:T(8,128)(2,1)S(1)}, bf16[4,3,256,128]{3,2,1,0:T(8,128)(2,1)}, u32[]{:S(2)}, u32[]{:S(2)}) collective-permute-start(bf16[4,3,256,128]{3,2,1,0:T(8,128)(2,1)S(1)} %pad_maximum_fusion.1.refs_0_), channel_id=1, source_target_pairs={{0,8},{16,24},{1,9},{17,25},{2,10},{18,26},{3,11},{19,27},{4,12},{... | collective-permute-start | bytes 2359304 | tf_op jit(solution)/shard_map/ppermute | solution.py:39
  35.5 7.8 %collective-permute-start.12 = (bf16[3,256,128]{2,1,0:T(8,128)(2,1)S(1)}, bf16[3,256,128]{2,1,0:T(8,128)(2,1)S(1)}, u32[]{:S(2)}, u32[]{:S(2)}) collective-permute-start(bf16[3,256,128]{2,1,0:T(8,128)(2,1)S(1)} %collective-permute-done.11), channel_id=1, source_target_pairs={{0,40},{16,56},{1,41},{17,57},{2,42},{18,58},{3,43},{19,59},{4,44}... | collective-permute-start | bytes 589832 | tf_op jit(solution)/shard_map/ppermute | solution.py:39
  37.2 22.8 %collective-permute-start.13 = (bf16[3,256,128]{2,1,0:T(8,128)(2,1)S(1)}, bf16[3,256,128]{2,1,0:T(8,128)(2,1)S(1)}, u32[]{:S(2)}, u32[]{:S(2)}) collective-permute-start(bf16[3,256,128]{2,1,0:T(8,128)(2,1)S(1)} %collective-permute-done.11), channel_id=1, source_target_pairs={{0,32},{16,48},{1,33},{17,49},{2,34},{18,50},{3,35},{19,51},{4,36}... | collective-permute-start | bytes 589832 | tf_op jit(solution)/shard_map/ppermute | solution.py:39
  39.2 22.5 %collective-permute-start.14 = (bf16[3,256,128]{2,1,0:T(8,128)(2,1)S(1)}, bf16[3,256,128]{2,1,0:T(8,128)(2,1)S(1)}, u32[]{:S(2)}, u32[]{:S(2)}) collective-permute-start(bf16[3,256,128]{2,1,0:T(8,128)(2,1)S(1)} %collective-permute-done.11), channel_id=1, source_target_pairs={{0,8},{16,24},{1,9},{17,25},{2,10},{18,26},{3,11},{19,27},{4,12},{... | collective-permute-start | bytes 589832 | tf_op jit(solution)/shard_map/ppermute | solution.py:39
  43.4 24.8 %collective-permute-start.2 = (bf16[16,4096]{1,0:T(8,128)(2,1)S(1)}, bf16[16,4096]{1,0:T(8,128)(2,1)S(1)}, u32[]{:S(2)}, u32[]{:S(2)}) collective-permute-start(bf16[16,4096]{1,0:T(8,128)(2,1)S(1)} %reshape.311), channel_id=1, source_target_pairs={{0,128},{16,144},{1,129},{17,145},{2,130},{18,146},{3,131},{19,147... | collective-permute-start | bytes 393224 | tf_op jit(solution)/shard_map/ppermute | solution.py:39
  60.0 9.3 %collective-permute-start.3 = (bf16[16,4096]{1,0:T(8,128)(2,1)S(1)}, bf16[16,4096]{1,0:T(8,128)(2,1)S(1)}, u32[]{:S(2)}, u32[]{:S(2)}) collective-permute-start(bf16[16,4096]{1,0:T(8,128)(2,1)S(1)} %reshape.311), channel_id=1, source_target_pairs={{0,64},{16,80},{1,65},{17,81},{2,66},{18,82},{3,67},{19,83},{4,68}... | collective-permute-start | bytes 393224 | tf_op jit(solution)/shard_map/ppermute | solution.py:39
  61.7 4.0 %collective-permute-start.18 = (bf16[149,128]{1,0:T(8,128)(2,1)S(1)}, bf16[149,128]{1,0:T(8,128)(2,1)S(1)}, u32[]{:S(2)}, u32[]{:S(2)}) collective-permute-start(bf16[149,128]{1,0:T(8,128)(2,1)S(1)} %fusion.6), channel_id=1, source_target_pairs={{0,8},{16,24},{1,9},{17,25},{2,10},{18,26},{3,11},{19,27},{4,12},{... | collective-permute-start | bytes 114440 | tf_op jit(solution)/shard_map/ppermute | solution.py:39
  62.2 41.6 %copy-start.3 = (bf16[4,3,256,128]{3,2,1,0:T(8,128)(2,1)}, bf16[4,3,256,128]{3,2,1,0:T(8,128)(2,1)S(1)}, u32[]{:S(2)}) copy-start(bf16[4,3,256,128]{3,2,1,0:T(8,128)(2,1)S(1)} %pad_maximum_fusion.2.refs_4_) | copy-start | bytes 2359300
  65.7 33.8 %collective-permute-start.8 = (bf16[4,3,256,128]{3,2,1,0:T(8,128)(2,1)S(1)}, bf16[4,3,256,128]{3,2,1,0:T(8,128)(2,1)}, u32[]{:S(2)}, u32[]{:S(2)}) collective-permute-start(bf16[4,3,256,128]{3,2,1,0:T(8,128)(2,1)S(1)} %pad_maximum_fusion.1.refs_0_), channel_id=1, source_target_pairs={{0,40},{16,56},{1,41},{17,57},{2,42},{18,58},{3,43},{19,59},{4,44}... | collective-permute-start | bytes 2359304 | tf_op jit(solution)/shard_map/ppermute | solution.py:39
  67.5 32.0 %collective-permute-start.9 = (bf16[4,3,256,128]{3,2,1,0:T(8,128)(2,1)S(1)}, bf16[4,3,256,128]{3,2,1,0:T(8,128)(2,1)}, u32[]{:S(2)}, u32[]{:S(2)}) collective-permute-start(bf16[4,3,256,128]{3,2,1,0:T(8,128)(2,1)S(1)} %pad_maximum_fusion.1.refs_0_), channel_id=1, source_target_pairs={{0,32},{16,48},{1,33},{17,49},{2,34},{18,50},{3,35},{19,51},{4,36}... | collective-permute-start | bytes 2359304 | tf_op jit(solution)/shard_map/ppermute | solution.py:39
  68.1 31.4 %collective-permute-start.15 = (bf16[4,3,256,128]{3,2,1,0:T(8,128)(2,1)S(1)}, bf16[4,3,256,128]{3,2,1,0:T(8,128)(2,1)}, u32[]{:S(2)}, u32[]{:S(2)}) collective-permute-start(bf16[4,3,256,128]{3,2,1,0:T(8,128)(2,1)S(1)} %pad_maximum_fusion.2.refs_4_), channel_id=1, source_target_pairs={{0,192},{16,208},{1,193},{17,209},{2,194},{18,210},{3,195},{19,211... | collective-permute-start | bytes 2359304 | tf_op jit(solution)/shard_map/ppermute | solution.py:39
  69.3 30.2 %collective-permute-start.16 = (bf16[4,3,256,128]{3,2,1,0:T(8,128)(2,1)S(1)}, bf16[4,3,256,128]{3,2,1,0:T(8,128)(2,1)}, u32[]{:S(2)}, u32[]{:S(2)}) collective-permute-start(bf16[4,3,256,128]{3,2,1,0:T(8,128)(2,1)S(1)} %pad_maximum_fusion.2.refs_4_), channel_id=1, source_target_pairs={{0,128},{16,144},{1,129},{17,145},{2,130},{18,146},{3,131},{19,147... | collective-permute-start | bytes 2359304 | tf_op jit(solution)/shard_map/ppermute | solution.py:39
  69.3 34.4 %collective-permute-start.17 = (bf16[4,3,256,128]{3,2,1,0:T(8,128)(2,1)S(1)}, bf16[4,3,256,128]{3,2,1,0:T(8,128)(2,1)}, u32[]{:S(2)}, u32[]{:S(2)}) collective-permute-start(bf16[4,3,256,128]{3,2,1,0:T(8,128)(2,1)S(1)} %pad_maximum_fusion.2.refs_4_), channel_id=1, source_target_pairs={{0,64},{16,80},{1,65},{17,81},{2,66},{18,82},{3,67},{19,83},{4,68}... | collective-permute-start | bytes 2359304 | tf_op jit(solution)/shard_map/ppermute | solution.py:39
  127.3 7.1 %collective-permute-start.19 = (bf16[4,152,128]{2,1,0:T(8,128)(2,1)}, bf16[4,152,128]{2,1,0:T(8,128)(2,1)S(1)}, u32[]{:S(2)}, u32[]{:S(2)}) collective-permute-start(bf16[4,152,128]{2,1,0:T(8,128)(2,1)} %get-tuple-element.28.refs_0_), channel_id=1, source_target_pairs={{0,192},{16,208},{1,193},{17,209},{2,194},{18,210},{3,195},{19,211... | collective-permute-start | bytes 466952 | tf_op jit(solution)/shard_map/ppermute | solution.py:39
  128.4 14.6 %collective-permute-start.20 = (bf16[4,152,128]{2,1,0:T(8,128)(2,1)}, bf16[4,152,128]{2,1,0:T(8,128)(2,1)S(1)}, u32[]{:S(2)}, u32[]{:S(2)}) collective-permute-start(bf16[4,152,128]{2,1,0:T(8,128)(2,1)} %get-tuple-element.28.refs_0_), channel_id=1, source_target_pairs={{0,128},{16,144},{1,129},{17,145},{2,130},{18,146},{3,131},{19,147... | collective-permute-start | bytes 466952 | tf_op jit(solution)/shard_map/ppermute | solution.py:39
  128.4 14.6 %collective-permute-start.21 = (bf16[4,152,128]{2,1,0:T(8,128)(2,1)}, bf16[4,152,128]{2,1,0:T(8,128)(2,1)S(1)}, u32[]{:S(2)}, u32[]{:S(2)}) collective-permute-start(bf16[4,152,128]{2,1,0:T(8,128)(2,1)} %get-tuple-element.28.refs_0_), channel_id=1, source_target_pairs={{0,64},{16,80},{1,65},{17,81},{2,66},{18,82},{3,67},{19,83},{4,68}... | collective-permute-start | bytes 466952 | tf_op jit(solution)/shard_map/ppermute | solution.py:39
  129.4 13.7 %collective-permute-start.22 = (bf16[4,152,128]{2,1,0:T(8,128)(2,1)}, bf16[4,152,128]{2,1,0:T(8,128)(2,1)S(1)}, u32[]{:S(2)}, u32[]{:S(2)}) collective-permute-start(bf16[4,152,128]{2,1,0:T(8,128)(2,1)} %get-tuple-element.29.refs_4_), channel_id=1, source_target_pairs={{0,40},{16,56},{1,41},{17,57},{2,42},{18,58},{3,43},{19,59},{4,44}... | collective-permute-start | bytes 466952 | tf_op jit(solution)/shard_map/ppermute | solution.py:39
  131.6 11.5 %collective-permute-start.23 = (bf16[4,152,128]{2,1,0:T(8,128)(2,1)}, bf16[4,152,128]{2,1,0:T(8,128)(2,1)S(1)}, u32[]{:S(2)}, u32[]{:S(2)}) collective-permute-start(bf16[4,152,128]{2,1,0:T(8,128)(2,1)} %get-tuple-element.29.refs_4_), channel_id=1, source_target_pairs={{0,32},{16,48},{1,33},{17,49},{2,34},{18,50},{3,35},{19,51},{4,36}... | collective-permute-start | bytes 466952 | tf_op jit(solution)/shard_map/ppermute | solution.py:39
  134.4 8.7 %copy-start.12 = (bf16[4,152,128]{2,1,0:T(8,128)(2,1)}, bf16[4,152,128]{2,1,0:T(8,128)(2,1)S(1)}, u32[]{:S(2)}) copy-start(bf16[4,152,128]{2,1,0:T(8,128)(2,1)S(1)} %collective-permute-done.19.refs_1_) | copy-start | bytes 466948
  134.4 8.7 %collective-permute-start.24 = (bf16[4,152,128]{2,1,0:T(8,128)(2,1)}, bf16[4,152,128]{2,1,0:T(8,128)(2,1)S(1)}, u32[]{:S(2)}, u32[]{:S(2)}) collective-permute-start(bf16[4,152,128]{2,1,0:T(8,128)(2,1)} %get-tuple-element.29.refs_4_), channel_id=1, source_target_pairs={{0,8},{16,24},{1,9},{17,25},{2,10},{18,26},{3,11},{19,27},{4,12},{... | collective-permute-start | bytes 466952 | tf_op jit(solution)/shard_map/ppermute | solution.py:39
  143.0 0.7 copy-start.13
  143.0 0.7 copy-start.14
  143.0 0.7 copy-start.15
  143.1 0.8 copy-start.16
  143.8 0.7 copy-start.17
  147.0 7.7 %collective-permute-start.25 = (bf16[4,152,128]{2,1,0:T(8,128)(2,1)}, bf16[4,152,128]{2,1,0:T(8,128)(2,1)S(1)}, u32[]{:S(2)}, u32[]{:S(2)}) collective-permute-start(bf16[4,152,128]{2,1,0:T(8,128)(2,1)} %get-tuple-element.31), channel_id=1, source_target_pairs={{0,40},{16,56},{1,41},{17,57},{2,42},{18,58},{3,43},{19,59},{4,44}... | collective-permute-start | bytes 466952 | tf_op jit(solution)/shard_map/ppermute | solution.py:39
  149.3 14.1 %collective-permute-start.26 = (bf16[4,152,128]{2,1,0:T(8,128)(2,1)}, bf16[4,152,128]{2,1,0:T(8,128)(2,1)S(1)}, u32[]{:S(2)}, u32[]{:S(2)}) collective-permute-start(bf16[4,152,128]{2,1,0:T(8,128)(2,1)} %get-tuple-element.32), channel_id=1, source_target_pairs={{0,32},{16,48},{1,33},{17,49},{2,34},{18,50},{3,35},{19,51},{4,36}... | collective-permute-start | bytes 466952 | tf_op jit(solution)/shard_map/ppermute | solution.py:39
  151.7 11.7 %collective-permute-start.27 = (bf16[4,152,128]{2,1,0:T(8,128)(2,1)}, bf16[4,152,128]{2,1,0:T(8,128)(2,1)S(1)}, u32[]{:S(2)}, u32[]{:S(2)}) collective-permute-start(bf16[4,152,128]{2,1,0:T(8,128)(2,1)} %get-tuple-element.33), channel_id=1, source_target_pairs={{0,8},{16,24},{1,9},{17,25},{2,10},{18,26},{3,11},{19,27},{4,12},{... | collective-permute-start | bytes 466952 | tf_op jit(solution)/shard_map/ppermute | solution.py:39
  153.0 10.4 %collective-permute-start.28 = (bf16[4,152,128]{2,1,0:T(8,128)(2,1)}, bf16[4,152,128]{2,1,0:T(8,128)(2,1)S(1)}, u32[]{:S(2)}, u32[]{:S(2)}) collective-permute-start(bf16[4,152,128]{2,1,0:T(8,128)(2,1)} %get-tuple-element.35), channel_id=1, source_target_pairs={{0,192},{16,208},{1,193},{17,209},{2,194},{18,210},{3,195},{19,211... | collective-permute-start | bytes 466952 | tf_op jit(solution)/shard_map/ppermute | solution.py:39
  153.0 10.4 %collective-permute-start.29 = (bf16[4,152,128]{2,1,0:T(8,128)(2,1)}, bf16[4,152,128]{2,1,0:T(8,128)(2,1)S(1)}, u32[]{:S(2)}, u32[]{:S(2)}) collective-permute-start(bf16[4,152,128]{2,1,0:T(8,128)(2,1)} %get-tuple-element.36), channel_id=1, source_target_pairs={{0,128},{16,144},{1,129},{17,145},{2,130},{18,146},{3,131},{19,147... | collective-permute-start | bytes 466952 | tf_op jit(solution)/shard_map/ppermute | solution.py:39
  154.6 8.8 %copy-start.6 = (bf16[4,152,128]{2,1,0:T(8,128)(2,1)}, bf16[4,152,128]{2,1,0:T(8,128)(2,1)S(1)}, u32[]{:S(2)}) copy-start(bf16[4,152,128]{2,1,0:T(8,128)(2,1)S(1)} %collective-permute-done.25.refs_1_) | copy-start | bytes 466948
  154.6 8.8 %collective-permute-start.30 = (bf16[4,152,128]{2,1,0:T(8,128)(2,1)}, bf16[4,152,128]{2,1,0:T(8,128)(2,1)S(1)}, u32[]{:S(2)}, u32[]{:S(2)}) collective-permute-start(bf16[4,152,128]{2,1,0:T(8,128)(2,1)} %get-tuple-element.37), channel_id=1, source_target_pairs={{0,64},{16,80},{1,65},{17,81},{2,66},{18,82},{3,67},{19,83},{4,68}... | collective-permute-start | bytes 466952 | tf_op jit(solution)/shard_map/ppermute | solution.py:39
  163.4 0.7 copy-start.7
  163.4 0.7 copy-start.8
  163.4 0.8 copy-start.9
  163.4 0.8 copy-start.10
  163.5 0.8 copy-start.11
  172.2 21.7 %collective-permute-start.31 = (bf16[4,16,4096]{2,1,0:T(8,128)(2,1)S(1)}, bf16[4,16,4096]{2,1,0:T(8,128)(2,1)S(1)}, u32[]{:S(2)}, u32[]{:S(2)}) collective-permute-start(bf16[4,16,4096]{2,1,0:T(8,128)(2,1)S(1)} %pad_maximum_fusion.4), channel_id=1, source_target_pairs={{0,40},{16,56},{1,41},{17,57},{2,42},{18,58},{3,43},{19,59},{4,44}... | collective-permute-start | bytes 1572872 | tf_op jit(solution)/shard_map/ppermute | solution.py:39
  175.9 18.1 %collective-permute-start.32 = (bf16[4,16,4096]{2,1,0:T(8,128)(2,1)S(1)}, bf16[4,16,4096]{2,1,0:T(8,128)(2,1)S(1)}, u32[]{:S(2)}, u32[]{:S(2)}) collective-permute-start(bf16[4,16,4096]{2,1,0:T(8,128)(2,1)S(1)} %pad_maximum_fusion.4), channel_id=1, source_target_pairs={{0,32},{16,48},{1,33},{17,49},{2,34},{18,50},{3,35},{19,51},{4,36}... | collective-permute-start | bytes 1572872 | tf_op jit(solution)/shard_map/ppermute | solution.py:39
  175.9 21.8 %collective-permute-start.33 = (bf16[4,16,4096]{2,1,0:T(8,128)(2,1)S(1)}, bf16[4,16,4096]{2,1,0:T(8,128)(2,1)S(1)}, u32[]{:S(2)}, u32[]{:S(2)}) collective-permute-start(bf16[4,16,4096]{2,1,0:T(8,128)(2,1)S(1)} %pad_maximum_fusion.4), channel_id=1, source_target_pairs={{0,8},{16,24},{1,9},{17,25},{2,10},{18,26},{3,11},{19,27},{4,12},{... | collective-permute-start | bytes 1572872 | tf_op jit(solution)/shard_map/ppermute | solution.py:39
  197.7 1.1 copy-start.1
  197.9 4.9 %copy-start = (bf16[4,4,16,4096]{3,2,1,0:T(8,128)(2,1)}, bf16[4,4,16,4096]{3,2,1,0:T(8,128)(2,1)S(1)}, u32[]{:S(2)}) copy-start(bf16[4,4,16,4096]{3,2,1,0:T(8,128)(2,1)S(1)} %pad_maximum_fusion.own_ref) | copy-start | bytes 6291460
  197.9 4.8 %collective-permute-start.34 = (bf16[4,4,16,4096]{3,2,1,0:T(8,128)(2,1)S(1)}, bf16[4,4,16,4096]{3,2,1,0:T(8,128)(2,1)}, u32[]{:S(2)}, u32[]{:S(2)}) collective-permute-start(bf16[4,4,16,4096]{3,2,1,0:T(8,128)(2,1)S(1)} %pad_maximum_fusion.own_ref), channel_id=1, source_target_pairs={{0,16},{16,0},{1,17},{17,1},{2,18},{18,2},{3,19},{19,3},{4,20},{20... | collective-permute-start | bytes 6291464 | tf_op jit(solution)/shard_map/ppermute | solution.py:39
  199.4 8.7 %collective-permute-start = (bf16[512,256]{1,0:T(8,128)(2,1)S(1)}, bf16[512,256]{1,0:T(8,128)(2,1)S(1)}, u32[]{:S(2)}, u32[]{:S(2)}) collective-permute-start(bf16[512,256]{1,0:T(8,128)(2,1)S(1)} %get-tuple-element.46), channel_id=1, source_target_pairs={{0,8},{16,24},{1,9},{17,25},{2,10},{18,26},{3,11},{19,27},{4,12},{... | collective-permute-start | bytes 786440 | tf_op jit(solution)/shard_map/ppermute | solution.py:39
  208.2 19.6 %copy-start.5 = (bf16[512,256]{1,0:T(8,128)(2,1)}, bf16[512,256]{1,0:T(8,128)(2,1)S(1)}, u32[]{:S(2)}) copy-start(bf16[512,256]{1,0:T(8,128)(2,1)S(1)} %collective-permute-done.residual_ref) | copy-start | bytes 786436
  233.0 8.7 %collective-permute-start.35 = (bf16[512,256]{1,0:T(8,128)(2,1)}, bf16[512,256]{1,0:T(8,128)(2,1)S(1)}, u32[]{:S(2)}, u32[]{:S(2)}) collective-permute-start(bf16[512,256]{1,0:T(8,128)(2,1)} %output.2), channel_id=1, source_target_pairs={{0,8},{16,24},{1,9},{17,25},{2,10},{18,26},{3,11},{19,27},{4,12},{... | collective-permute-start | bytes 786440 | tf_op jit(solution)/shard_map/ppermute | solution.py:39
Sparse Core Ops, SparseCore 0:
  18.0 57.2 all-gather.5
  172.4 55.4 all-gather.3

commit v2 on v1

--- a/solution.py
+++ b/solution.py
@@ -85,16 +85,17 @@
     out_ref, x_scratch, s_scratch, w_scratch, total, x_sems, s_sems, w_sems = refs[8:]
     x, y, core, y_low = place_ref[0], place_ref[1], place_ref[2], place_ref[3]
 
-    def copies(i):
+    def row_copies(i):
         made = []
-        z, group = i // 2, lax.rem(i, 2)
+        group, z = i // 8, lax.rem(i, 8)
         source = z * 2 + lax.rem(core + group, 2)
         rows = pl.ds(pl.multiple_of(group * HALF, HALF), HALF)
         for p in range(2):
             lanes = pl.ds(pl.multiple_of((z * 2 + p) * PIECE, PIECE), PIECE)
             made.append(
                 pltpu.make_async_copy(
-                    line_ref.at[source, p, pl.ds(0, HALF)], x_scratch.at[rows, lanes], x_sems.at[p, i]
+                    line_ref.at[source, p, pl.ds(0, HALF)], x_scratch.at[rows, lanes],
+                    x_sems.at[p, i],
                 )
             )
             made.append(
@@ -105,64 +106,65 @@
             )
         return made
 
-    def start(i, carry):
-        for copy in copies(i):
-            copy.start()
-        return carry
-
-    def finish(i, carry):
-        for copy in copies(i):
-            copy.wait()
-        return carry
-
-    started = []
-    for other in range(2):
-        for a in range(4):
-            for b in range(4):
+    def weight_copies(i):
+        made = []
+        branch, b = i // 4, lax.rem(i, 4)
+        for other in range(2):
+            for a in range(4):
                 dx, dy = (b, a) if other == 0 else (a, b)
                 to_x, to_y = lax.rem(x + dx, 4), lax.rem(y + dy, 4)
                 owner = to_x * 4 + (to_y // 2) * 2 + lax.rem(core + other, 2)
                 turn = lax.rem(owner, 8) * 2 + lax.rem(owner // 8 + y_low, 2)
                 rows = pl.ds(pl.multiple_of(turn * PIECE, PIECE), PIECE)
                 lanes = pl.ds(pl.multiple_of(lax.rem(to_y, 2) * LANES, LANES), LANES)
-                started.append(
+                made.append(
                     pltpu.make_async_copy(
-                        weights[other * 4 + a].at[b],
-                        w_scratch.at[:, rows, lanes],
-                        w_sems.at[other, a, b],
+                        weights[other * 4 + a].at[b, branch],
+                        w_scratch.at[branch, rows, lanes],
+                        w_sems.at[other * 4 + a, i],
                     )
                 )
-    for copy in started:
-        copy.start()
-    lax.fori_loop(0, 16, start, 0)
-    for copy in started:
-        copy.wait()
-
-    def quarter(part, carry):
-        lax.fori_loop(part * 4, part * 4 + 4, finish, 0)
-        depth = pl.ds(pl.multiple_of(part * 1024, 1024), 1024)
-
-        def step(i, carry):
-            branch, group = i // 2, lax.rem(i, 2)
-            rows = pl.ds(pl.multiple_of(group * HALF, HALF), HALF)
-            product = jnp.dot(
-                x_scratch[rows, depth], w_scratch[branch, depth, :],
-                preferred_element_type=jnp.float32,
-            )
-
-            @pl.when(part == 0)
-            def _():
-                total[branch, rows, :] = product
-
-            @pl.when(part > 0)
-            def _():
-                total[branch, rows, :] += product
-
+        return made
+
+    def start(copies, first, last):
+        def one(i, carry):
+            for copy in copies(i):
+                copy.start()
             return carry
 
-        return lax.fori_loop(0, 6, step, carry)
-
-    lax.fori_loop(0, 4, quarter, 0)
+        lax.fori_loop(first, last, one, 0)
+
+    def finish(copies, first, last):
+        def one(i, carry):
+            for copy in copies(i):
+                copy.wait()
+            return carry
+
+        lax.fori_loop(first, last, one, 0)
+
+    start(row_copies, 0, 8)
+    start(weight_copies, 0, 4)
+    start(row_copies, 8, 16)
+    start(weight_copies, 4, 12)
+
+    def step(i, carry):
+        branch, group = i // 2, lax.rem(i, 2)
+
+        @pl.when(i < 2)
+        def _():
+            finish(row_copies, i * 8, i * 8 + 8)
+
+        @pl.when(group == 0)
+        def _():
+            finish(weight_copies, branch * 4, branch * 4 + 4)
+
+        rows = pl.ds(pl.multiple_of(group * HALF, HALF), HALF)
+        total[branch, rows, :] = jnp.dot(
+            x_scratch[rows, :], w_scratch[branch], preferred_element_type=jnp.float32
+        )
+        return carry
+
+    lax.fori_loop(0, 6, step, 0)
     for group in range(2):
         square = jnp.sum(s_scratch[group].astype(jnp.float32), axis=0)
         for i in range(2):
@@ -193,7 +195,7 @@
             pltpu.VMEM((3, 2 * HALF, 2 * LANES), jnp.float32),
             pltpu.SemaphoreType.DMA((2, 16)),
             pltpu.SemaphoreType.DMA((2, 16)),
-            pltpu.SemaphoreType.DMA((2, 4, 4)),
+            pltpu.SemaphoreType.DMA((8, 12)),
         ],
         cost_estimate=pl.CostEstimate(
             flops=2 * 1024 * D * 768, bytes_accessed=16 << 20, transcendentals=0
@@ -523,18 +525,19 @@
 
 
 def output_kernel(
-    side, place_ref, residual_ref, w_ref, gated_ref, out_ref, scratch, weights, total, sems, w_sems
+    side, place_ref, residual_ref, w_ref, gated_ref, out_ref, scratch, weights, sems, w_sem
 ):
     core, y_low = place_ref[2], place_ref[3]
-    column = lax.rem(y_low + side, 2)
+    load = pltpu.make_async_copy(w_ref.at[lax.rem(y_low + side, 2)], weights, w_sem)
+    load.start()
 
     def copies(i):
-        lanes = pl.ds(pl.multiple_of(i * 1024, 1024), 1024)
-        made = [pltpu.make_async_copy(w_ref.at[column, :, lanes], weights.at[:, lanes], w_sems.at[i])]
-        for k in range(4):
-            lanes = pl.ds(pl.multiple_of((i * 4 + k) * PIECE, PIECE), PIECE)
-            source = gated_ref.at[i * 4 + k, lax.rem(core + k, 2)]
-            made.append(pltpu.make_async_copy(source, scratch.at[:, lanes], sems.at[i, k]))
+        made = []
+        rows = pl.ds(pl.multiple_of(i * BLK, BLK), BLK)
+        for k in range(16):
+            source = gated_ref.at[k, lax.rem(core + k, 2), rows]
+            target = scratch.at[rows, pl.ds(k * PIECE, PIECE)]
+            made.append(pltpu.make_async_copy(source, target, sems.at[i, k]))
         return made
 
     def start(i, carry):
@@ -542,21 +545,20 @@
             copy.start()
         return carry
 
-    lax.fori_loop(0, 4, start, 0)
-    total[...] = residual_ref[...].astype(jnp.float32)
-
     def step(i, carry):
         for copy in copies(i):
             copy.wait()
-        lanes = pl.ds(pl.multiple_of(i * 1024, 1024), 1024)
-        total[...] += lax.dot_general(
-            scratch[:, lanes], weights[:, lanes], (((1,), (1,)), ((), ())),
+        rows = pl.ds(pl.multiple_of(i * BLK, BLK), BLK)
+        summed = lax.dot_general(
+            scratch[rows, :], weights[...], (((1,), (1,)), ((), ())),
             preferred_element_type=jnp.float32,
         )
+        out_ref[rows, :] = (residual_ref[rows, :].astype(jnp.float32) + summed).astype(jnp.bfloat16)
         return carry
 
-    lax.fori_loop(0, 4, step, 0)
-    out_ref[...] = total[...].astype(jnp.bfloat16)
+    lax.fori_loop(0, 2, start, 0)
+    load.wait()
+    lax.fori_loop(0, 2, step, 0)
 
 
 def output(side, place, residual, weights, gated):
@@ -568,9 +570,8 @@
         scratch_shapes=[
             pltpu.VMEM((HALF, D), jnp.bfloat16),
             pltpu.VMEM((PIECE, D), jnp.bfloat16),
-            pltpu.VMEM((HALF, PIECE), jnp.float32),
-            pltpu.SemaphoreType.DMA((4, 4)),
-            pltpu.SemaphoreType.DMA((4,)),
+            pltpu.SemaphoreType.DMA((2, 16)),
+            pltpu.SemaphoreType.DMA,
         ],
         cost_estimate=pl.CostEstimate(
             flops=2 * HALF * D * PIECE, bytes_accessed=6 << 20, transcendentals=0
@@ -619,9 +620,6 @@
 
     place = jnp.stack([x, y, core, y_low, z]).astype(jnp.int32)
 
-    columns = out_weight.reshape(2, 8, 2, LANES, 16).transpose(4, 1, 2, 0, 3).reshape(16, D)
-    columns = axis_of(columns, along_x)
-    columns = jnp.stack(columns)
     proj = project(place, line, weights)
 
     both = jnp.concatenate([short_filter.reshape(SHORT * 3, PIECE), medium_filter], axis=0)
@@ -656,7 +654,6 @@
     starts = (ids[:4] * BLK).astype(jnp.int32)
     ends = jnp.cumsum(genome_lengths).astype(jnp.int32)
 
-    starts, columns = lax.optimization_barrier((starts, columns))
     product, low, high = products(starts, ends, proj, taps)
     rows_x, rows_y = axis_of(low, along_x), axis_of(high, along_y)
     partials = [inner(i, starts, ends, product, medium) for i in range(2)]
@@ -669,7 +666,9 @@
     residual = send(jnp.where(y_low == 0, rows[1], rows[0]), swap_y)
     mine = jnp.where(y_low == 0, rows[0], rows[1])
     gated = edges(starts, ends, picks, proj, partials, taps, medium, halos)
+    columns = out_weight.reshape(2, 8, 2, LANES, 16).transpose(4, 1, 2, 0, 3).reshape(16, D)
     columns = lax.optimization_barrier((columns, gated))[0]
+    columns = jnp.stack(axis_of(columns, along_x))
     gathered = gather_line(gated.reshape(2, HALF, 2 * LANES))
     columns = jnp.stack(axis_of(columns, along_y))
     columns = assemble(place, columns, send(columns, swap_core))

time: 253 us -> 248 us (0.980)
  waiting for transfers between devices: 116 us -> 103 us
  starting transfers between devices: 42.6 us -> 54.4 us
  Pallas kernels: 62.4 us -> 59.1 us
    ppermute x36, starting transfers between devices: 42.5 us -> 54.4 us  [send(): return lax.ppermute(value, AXES, permutation(move))]
    all_gather x2, waiting for transfers between devices: 19.6 us -> 12.6 us  [gather_line(): return lax.all_gather(value, AXES, axis=0, axis_index_groups=groups)]
    ppermute x36, waiting for transfers between devices: 96.5 us -> 90 us  [send(): return lax.ppermute(value, AXES, permutation(move))]
    pallas_call x1, Pallas kernels: 18.8 us -> 14.6 us  [project(): pl.pallas_call(project_kernel, out_shape=jax.ShapeDtypeStruct((3, 4, BLK,...]
  transfers between devices with their start and end apart: 38 -> 38, of which waited for: 16 -> 18; matrix products, arithmetic and copies ran while one was open for 3% -> 3% of each run, Pallas kernels for 9% -> 10%
where the time goes in v2:
time: 248 us; the launch traced here: 245 us
  waiting for transfers between devices  103 us (42%)
  Pallas kernels  59.1 us (24%)
  starting transfers between devices  54.4 us (22%)
  between operations  13.9 us (6%)
  other arithmetic  9.09 us (4%)
  local copies, waits for them, and re-layouts  6.17 us (2%)
    ppermute x36, waiting for transfers between devices, send(): return lax.ppermute(value, AXES, permutation(move))  90 us
    ppermute x36, starting transfers between devices, send(): return lax.ppermute(value, AXES, permutation(move))  54.4 us
    pallas_call x1, Pallas kernels, project(): pl.pallas_call(project_kernel, out_shape=jax.ShapeDtypeStruct((3, 4, BLK,...  14.6 us
    pallas_call x2, Pallas kernels, inner(): pl.pallas_call(functools.partial(inner_kernel, index), grid_spec=pltpu.Pr...  12.8 us
    all_gather x2, waiting for transfers between devices, gather_line(): return lax.all_gather(value, AXES, axis=0, axis_index_groups=groups)  12.6 us
    pallas_call x2, Pallas kernels, output(): pl.pallas_call(functools.partial(output_kernel, side), out_shape=jax.Shap...  11.2 us
    pallas_call x1, Pallas kernels, edges(): pl.pallas_call(edge_kernel, grid_spec=pltpu.PrefetchScalarGridSpec(num_sc...  8.05 us
    pallas_call x1, Pallas kernels, assemble(): pl.pallas_call(assemble_kernel, out_shape=jax.ShapeDtypeStruct((2, PIECE,...  5.36 us
  transfers between devices with their start and end apart: 38, of which 18 were waited for; matrix products, arithmetic and copies ran while one was open for 3% of the time, Pallas kernels for 10%

profile of v2, /device:TPU:32, one launch (start us, length us, event | category | flops | bytes accessed | tf_op | source)
XLA Modules:
  0.0 245.3 jit_solution(17189100664588996697)
XLA Ops:
  6.5 0.7 reshape.315
  7.3 1.3 fusion.1
  8.8 1.7 collective-permute-start.1
  10.5 6.6 %collective-permute-done.1 = bf16[520,256]{1,0:T(8,128)(2,1)S(1)} collective-permute-done((bf16[520,256]{1,0:T(8,128)(2,1)S(1)}, bf16[520,256]{1,0:T(8,128)(2,1)S(1)}, u32[]{:S(2)}, u32[]{:S(2)}) %collective-permute-start.1) | collective-permute-done | bytes 266272 | tf_op jit(solution)/shard_map/ppermute | solution.py:39
  17.0 0.9 pad_maximum_fusion.3
  18.6 2.8 %collective-permute-start.2 = (bf16[3,256,128]{2,1,0:T(8,128)(2,1)S(1)}, bf16[3,256,128]{2,1,0:T(8,128)(2,1)S(1)}, u32[]{:S(2)}, u32[]{:S(2)}) collective-permute-start(bf16[3,256,128]{2,1,0:T(8,128)(2,1)S(1)} %get-tuple-element.48), channel_id=1, source_target_pairs={{0,192},{16,208},{1,193},{17,209},{2,194},{18,210},{3,195},{19,211... | collective-permute-start | bytes 589832 | tf_op jit(solution)/shard_map/ppermute | solution.py:39
  21.5 0.8 collective-permute-start.3
  22.3 0.9 collective-permute-start.4
  23.2 1.7 collective-permute-start.15
  25.1 3.9 %collective-permute-done.2 = bf16[3,256,128]{2,1,0:T(8,128)(2,1)S(1)} collective-permute-done((bf16[3,256,128]{2,1,0:T(8,128)(2,1)S(1)}, bf16[3,256,128]{2,1,0:T(8,128)(2,1)S(1)}, u32[]{:S(2)}, u32[]{:S(2)}) %collective-permute-start.2) | collective-permute-done | bytes 196640 | tf_op jit(solution)/shard_map/ppermute | solution.py:39
  29.0 1.6 collective-permute-done.3
  30.6 2.1 collective-permute-done.4
  32.8 3.1 %collective-permute-start.5 = (bf16[4,3,256,128]{3,2,1,0:T(8,128)(2,1)S(1)}, bf16[4,3,256,128]{3,2,1,0:T(8,128)(2,1)S(1)}, u32[]{:S(2)}, u32[]{:S(2)}) collective-permute-start(bf16[4,3,256,128]{3,2,1,0:T(8,128)(2,1)S(1)} %pad_maximum_fusion.1.refs_0_), channel_id=1, source_target_pairs={{0,40},{16,56},{1,41},{17,57},{2,42},{18,58},{3,43},{19,59},{4,44}... | collective-permute-start | bytes 2359304 | tf_op jit(solution)/shard_map/ppermute | solution.py:39
  36.3 0.8 collective-permute-start.9
  37.4 1.0 collective-permute-start.11
  38.4 0.7 reduce-window.9
  39.4 0.7 stack.96.place_ref
  40.1 20.9 %collective-permute-done.9 = bf16[3,256,128]{2,1,0:T(8,128)(2,1)S(1)} collective-permute-done((bf16[3,256,128]{2,1,0:T(8,128)(2,1)S(1)}, bf16[3,256,128]{2,1,0:T(8,128)(2,1)S(1)}, u32[]{:S(2)}, u32[]{:S(2)}) %collective-permute-start.9) | collective-permute-done | bytes 196640 | tf_op jit(solution)/shard_map/ppermute | solution.py:39
  61.0 4.5 %collective-permute-start.7 = (bf16[4,3,256,128]{3,2,1,0:T(8,128)(2,1)S(1)}, bf16[4,3,256,128]{3,2,1,0:T(8,128)(2,1)}, u32[]{:S(2)}, u32[]{:S(2)}) collective-permute-start(bf16[4,3,256,128]{3,2,1,0:T(8,128)(2,1)S(1)} %pad_maximum_fusion.1.refs_0_), channel_id=1, source_target_pairs={{0,8},{16,24},{1,9},{17,25},{2,10},{18,26},{3,11},{19,27},{4,12},{... | collective-permute-start | bytes 2359304 | tf_op jit(solution)/shard_map/ppermute | solution.py:39
  65.6 8.0 %collective-permute-start.12 = (bf16[4,3,256,128]{3,2,1,0:T(8,128)(2,1)S(1)}, bf16[4,3,256,128]{3,2,1,0:T(8,128)(2,1)}, u32[]{:S(2)}, u32[]{:S(2)}) collective-permute-start(bf16[4,3,256,128]{3,2,1,0:T(8,128)(2,1)S(1)} %pad_maximum_fusion.2.refs_4_), channel_id=1, source_target_pairs={{0,192},{16,208},{1,193},{17,209},{2,194},{18,210},{3,195},{19,211... | collective-permute-start | bytes 2359304 | tf_op jit(solution)/shard_map/ppermute | solution.py:39
  75.8 7.2 %collective-permute-done.6.refs_2_ = bf16[4,3,256,128]{3,2,1,0:T(8,128)(2,1)} collective-permute-done((bf16[4,3,256,128]{3,2,1,0:T(8,128)(2,1)S(1)}, bf16[4,3,256,128]{3,2,1,0:T(8,128)(2,1)}, u32[]{:S(2)}, u32[]{:S(2)}) %collective-permute-start.6) | collective-permute-done | bytes 786464 | tf_op jit(solution)/shard_map/ppermute | solution.py:39
  83.0 11.5 %collective-permute-done.7.refs_3_ = bf16[4,3,256,128]{3,2,1,0:T(8,128)(2,1)} collective-permute-done((bf16[4,3,256,128]{3,2,1,0:T(8,128)(2,1)S(1)}, bf16[4,3,256,128]{3,2,1,0:T(8,128)(2,1)}, u32[]{:S(2)}, u32[]{:S(2)}) %collective-permute-start.7) | collective-permute-done | bytes 786464 | tf_op jit(solution)/shard_map/ppermute | solution.py:39
  94.6 5.5 %collective-permute-done.12.refs_5_ = bf16[4,3,256,128]{3,2,1,0:T(8,128)(2,1)} collective-permute-done((bf16[4,3,256,128]{3,2,1,0:T(8,128)(2,1)S(1)}, bf16[4,3,256,128]{3,2,1,0:T(8,128)(2,1)}, u32[]{:S(2)}, u32[]{:S(2)}) %collective-permute-start.12) | collective-permute-done | bytes 786464 | tf_op jit(solution)/shard_map/ppermute | solution.py:39
  100.1 1.9 collective-permute-done.14.refs_7_
  102.0 14.6 %project.1.proj_ref = bf16[3,4,256,256]{3,2,1,0:T(8,128)(2,1)} custom-call(s32[5]{0:T(128)} %stack.96.place_ref, bf16[16,2,520,256]{3,2,1,0:T(8,128)(2,1)} %bitcast.70, bf16[4,3,256,128]{3,2,1,0:T(8,128)(2,1)} %copy-done.2, bf16[4,3,256,128]{3,2,1,0:T(8,128)(2,1)} %copy-done.21, bf16[4,3,256,128]{3,2,1,0:T(8,128)(2,1)} %collective-permute-done.6.refs_2_, ...), custom_call_target="tpu_custom_call" | custom-call | flops 6442450944 | bytes 16777216 | tf_op jit(solution)/shard_map/project/pallas_call | solution.py:186
  116.6 4.7 %products.1 = (bf16[4,256,256]{2,1,0:T(8,128)(2,1)}, bf16[4,152,128]{2,1,0:T(8,128)(2,1)}, bf16[4,152,128]{2,1,0:T(8,128)(2,1)}) custom-call(s32[4]{0:T(128)} %slice_multiply_fusion.2.start_ref, s32[4]{0:T(128)} %bitcast.65, bf16[3,4,256,256]{3,2,1,0:T(8,128)(2,1)} %project.1.proj_ref, bf16[7,3,256]{2,1,0:T(4,128)(2,1)} %reshape.319.taps_ref), custom_call_target="tpu_custom_call" | custom-call | flops 62914560 | bytes 4194304 | tf_op jit(solution)/shard_map/products/pallas_call | solution.py:266
  121.3 1.9 collective-permute-start.16
  123.2 0.9 collective-permute-start.18
  124.1 2.1 collective-permute-start.20
  126.2 0.8 collective-permute-done.16.refs_1_
  128.2 0.7 fusion.4.medium_ref
  128.8 6.4 %inner.2.early_ref = f32[2,256,256]{2,1,0:T(8,128)} custom-call(s32[4]{0:T(128)} %slice_multiply_fusion.2.start_ref, s32[4]{0:T(128)} %bitcast.66, bf16[4,256,256]{2,1,0:T(8,128)(2,1)} %get-tuple-element.21.product_ref, f32[128,256]{1,0:T(8,128)} %fusion.4.medium_ref), custom_call_target="tpu_custom_call" | custom-call | flops 33554432 | bytes 1048576 | tf_op jit(solution)/shard_map/inner/pallas_call | solution.py:346
  136.1 0.7 copy-done.17
  136.7 2.5 %route.1 = (bf16[4,152,128]{2,1,0:T(8,128)(2,1)}, bf16[4,152,128]{2,1,0:T(8,128)(2,1)}, bf16[4,152,128]{2,1,0:T(8,128)(2,1)}, bf16[4,152,128]{2,1,0:T(8,128)(2,1...) custom-call(s32[2,4,4]{2,1,0:T(4,128)} %pad_add_fusion.table_ref, ...), custom_call_target="tpu_custom_call" | custom-call | flops 1024 | bytes 4194304 | tf_op jit(solution)/shard_map/route/pallas_call | solution.py:377
  139.2 2.7 %collective-permute-start.22 = (bf16[4,152,128]{2,1,0:T(8,128)(2,1)}, bf16[4,152,128]{2,1,0:T(8,128)(2,1)S(1)}, u32[]{:S(2)}, u32[]{:S(2)}) collective-permute-start(bf16[4,152,128]{2,1,0:T(8,128)(2,1)} %get-tuple-element.27), channel_id=1, source_target_pairs={{0,40},{16,56},{1,41},{17,57},{2,42},{18,58},{3,43},{19,59},{4,44}... | collective-permute-start | bytes 466952 | tf_op jit(solution)/shard_map/ppermute | solution.py:39
  141.9 2.0 collective-permute-start.23
  143.9 1.3 collective-permute-start.24
  145.2 2.2 collective-permute-start.25
  147.4 1.1 collective-permute-start.26
  148.5 1.7 collective-permute-start.27
  150.9 6.4 %inner.3.late_ref = f32[2,256,256]{2,1,0:T(8,128)} custom-call(s32[4]{0:T(128)} %slice_multiply_fusion.2.start_ref, s32[4]{0:T(128)} %bitcast.67, bf16[4,256,256]{2,1,0:T(8,128)(2,1)} %get-tuple-element.21.product_ref, f32[128,256]{1,0:T(8,128)} %fusion.4.medium_ref), custom_call_target="tpu_custom_call" | custom-call | flops 33554432 | bytes 1048576 | tf_op jit(solution)/shard_map/inner/pallas_call | solution.py:346
  158.2 8.1 %edges.1 = bf16[4,256,256]{2,1,0:T(8,128)(2,1)} custom-call(s32[4]{0:T(128)} %slice_multiply_fusion.2.start_ref, s32[4]{0:T(128)} %bitcast.68, s32[2,4]{1,0:T(2,128)} %pad_add_fusion.1.pick_ref, bf16[3,4,256,256]{3,2,1,0:T(8,128)(2,1)} %project.1.proj_ref, f32[2,256,256]{2,1,0:T(8,128)} %inner.2.early_ref, f32[2,256,256]{2,1,0:T(8,128)} %inner.3.late_ref, ...), custom_call_target="tpu_custom_call" | custom-call | flops 16777216 | bytes 3145728 | tf_op jit(solution)/shard_map/edges/pallas_call | solution.py:464
  166.5 1.6 collective-permute-start.28
  168.1 1.2 collective-permute-start.29
  169.3 1.1 collective-permute-start.30
  170.4 1.2 collective-permute-done.28
  171.6 3.0 %collective-permute-done.29 = bf16[16,4096]{1,0:T(8,128)(2,1)S(1)} collective-permute-done((bf16[16,4096]{1,0:T(8,128)(2,1)S(1)}, bf16[16,4096]{1,0:T(8,128)(2,1)S(1)}, u32[]{:S(2)}, u32[]{:S(2)}) %collective-permute-start.29) | collective-permute-done | bytes 131104 | tf_op jit(solution)/shard_map/ppermute | solution.py:39
  174.6 1.3 collective-permute-done.30
  176.0 3.1 %collective-permute-start.31 = (bf16[4,16,4096]{2,1,0:T(8,128)(2,1)S(1)}, bf16[4,16,4096]{2,1,0:T(8,128)(2,1)S(1)}, u32[]{:S(2)}, u32[]{:S(2)}) collective-permute-start(bf16[4,16,4096]{2,1,0:T(8,128)(2,1)S(1)} %get-tuple-element.44), channel_id=1, source_target_pairs={{0,40},{16,56},{1,41},{17,57},{2,42},{18,58},{3,43},{19,59},{4,44}... | collective-permute-start | bytes 1572872 | tf_op jit(solution)/shard_map/ppermute | solution.py:39
  179.2 1.5 collective-permute-start.32
  180.7 1.0 collective-permute-start.33
  181.7 14.0 %collective-permute-done.31 = bf16[4,16,4096]{2,1,0:T(8,128)(2,1)S(1)} collective-permute-done((bf16[4,16,4096]{2,1,0:T(8,128)(2,1)S(1)}, bf16[4,16,4096]{2,1,0:T(8,128)(2,1)S(1)}, u32[]{:S(2)}, u32[]{:S(2)}) %collective-permute-start.31) | collective-permute-done | bytes 524320 | tf_op jit(solution)/shard_map/ppermute | solution.py:39
  195.8 3.4 %collective-permute-done.33 = bf16[4,16,4096]{2,1,0:T(8,128)(2,1)S(1)} collective-permute-done((bf16[4,16,4096]{2,1,0:T(8,128)(2,1)S(1)}, bf16[4,16,4096]{2,1,0:T(8,128)(2,1)S(1)}, u32[]{:S(2)}, u32[]{:S(2)}) %collective-permute-start.33) | collective-permute-done | bytes 524320 | tf_op jit(solution)/shard_map/ppermute | solution.py:39
  199.5 0.7 copy-done.1
  200.2 0.7 broadcast_select_fusion.3
  201.0 3.3 %collective-permute-done.34.other_ref = bf16[4,4,16,4096]{3,2,1,0:T(8,128)(2,1)} collective-permute-done((bf16[4,4,16,4096]{3,2,1,0:T(8,128)(2,1)S(1)}, bf16[4,4,16,4096]{3,2,1,0:T(8,128)(2,1)}, u32[]{:S(2)}, u32[]{:S(2)}) %collective-permute-start.34) | collective-permute-done | bytes 2097184 | tf_op jit(solution)/shard_map/ppermute | solution.py:39
  204.3 5.4 %assemble.1.w_ref = bf16[2,256,4096]{2,1,0:T(8,128)(2,1)} custom-call(s32[5]{0:T(128)} %stack.96.place_ref, bf16[4,4,16,4096]{3,2,1,0:T(8,128)(2,1)} %copy-done, bf16[4,4,16,4096]{3,2,1,0:T(8,128)(2,1)} %collective-permute-done.34.other_ref), custom_call_target="tpu_custom_call" | custom-call | flops 1024 | bytes 8388608 | tf_op jit(solution)/shard_map/assemble/pallas_call | solution.py:516
  209.7 12.6 %all-gather.4.cloned.1.call-done.gated_ref = bf16[16,2,512,256]{3,2,1,0:T(8,128)(2,1)} async-done(((bf16[1,2,512,256]{3,2,1,0:T(8,128)(2,1)}), bf16[16,2,512,256]{3,2,1,0:T(8,128)(2,1)}) %all-gather.4.cloned.1.call-update) | async-done | bytes 8388624 | tf_op jit(solution)/shard_map/all_gather | solution.py:64
  222.3 5.6 %output.2 = bf16[512,256]{1,0:T(8,128)(2,1)} custom-call(s32[5]{0:T(128)} %stack.96.place_ref, bf16[512,256]{1,0:T(8,128)(2,1)} %copy-done.5, bf16[2,256,4096]{2,1,0:T(8,128)(2,1)} %assemble.1.w_ref, bf16[16,2,512,256]{3,2,1,0:T(8,128)(2,1)} %all-gather.4.cloned.1.call-done.gated_ref), custom_call_target="tpu_custom_call" | custom-call | flops 1073741824 | bytes 6291456 | tf_op jit(solution)/shard_map/output/pallas_call | solution.py:565
  227.9 1.6 collective-permute-start.35
  229.4 5.6 %output.3 = bf16[512,256]{1,0:T(8,128)(2,1)} custom-call(s32[5]{0:T(128)} %stack.96.place_ref, bf16[512,256]{1,0:T(8,128)(2,1)} %get-tuple-element.41.residual_ref, bf16[2,256,4096]{2,1,0:T(8,128)(2,1)} %assemble.1.w_ref, bf16[16,2,512,256]{3,2,1,0:T(8,128)(2,1)} %all-gather.4.cloned.1.call-done.gated_ref), custom_call_target="tpu_custom_call" | custom-call | flops 1073741824 | bytes 6291456 | tf_op jit(solution)/shard_map/output/pallas_call | solution.py:565
  235.0 1.6 collective-permute-done.35
  236.6 1.0 broadcast_select_fusion.2
  237.6 0.8 pad_maximum_fusion.5
  (120 shorter events, 8.6 us)
Async XLA Ops:
  6.5 95.5 %all-gather.6.cloned.1.call-start = ((), (), s32[]{:S(2)}) async-start(), calls=%async_computation.1 | async-start | bytes 9052160 | tf_op jit(solution)/shard_map/all_gather | solution.py:64
  8.5 9.5 %copy-start.4 = (bf16[3,256,256]{2,1,0:T(8,128)(2,1)S(1)}, bf16[3,256,256]{2,1,0:T(8,128)(2,1)}, u32[]{:S(2)}) copy-start(bf16[3,256,256]{2,1,0:T(8,128)(2,1)} %param.10) | copy-start | bytes 1179652
  8.8 8.2 %collective-permute-start.1 = (bf16[520,256]{1,0:T(8,128)(2,1)S(1)}, bf16[520,256]{1,0:T(8,128)(2,1)S(1)}, u32[]{:S(2)}, u32[]{:S(2)}) collective-permute-start(bf16[520,256]{1,0:T(8,128)(2,1)S(1)} %get-tuple-element.38), channel_id=1, source_target_pairs={{0,8},{16,24},{1,9},{17,25},{2,10},{18,26},{3,11},{19,27},{4,12},{... | collective-permute-start | bytes 798728 | tf_op jit(solution)/shard_map/ppermute | solution.py:39
  17.9 5.3 %copy-start.20 = (bf16[7,3,256]{2,0,1:T(8,128)(2,1)S(1)}, bf16[7,3,256]{2,0,1:T(8,128)(2,1)}, u32[]{:S(2)}) copy-start(bf16[7,3,256]{2,0,1:T(8,128)(2,1)} %param.11) | copy-start | bytes 32260
  17.9 5.3 %copy-start.19 = (bf16[128,256]{1,0:T(8,128)(2,1)S(1)}, bf16[128,256]{1,0:T(8,128)(2,1)}, u32[]{:S(2)}) copy-start(bf16[128,256]{1,0:T(8,128)(2,1)} %param.12) | copy-start | bytes 196612
  17.9 204.3 %all-gather.4.cloned.1.call-start = ((), (), s32[]{:S(2)}) async-start(), calls=%async_computation | async-start | bytes 8912896 | tf_op jit(solution)/shard_map/all_gather | solution.py:64
  18.2 17.9 %copy-start.23 = (s32[64]{0:T(128)S(1)}, s32[64]{0:T(128)}, u32[]{:S(2)}) copy-start(s32[64]{0:T(128)} %param.15) | copy-start | bytes 772
  18.2 20.2 %copy-start.22 = (s32[4]{0:T(128)S(1)}, s32[4]{0:T(128)}, u32[]{:S(2)}) copy-start(s32[4]{0:T(128)} %param.14) | copy-start | bytes 52
  18.6 10.4 %collective-permute-start.2 = (bf16[3,256,128]{2,1,0:T(8,128)(2,1)S(1)}, bf16[3,256,128]{2,1,0:T(8,128)(2,1)S(1)}, u32[]{:S(2)}, u32[]{:S(2)}) collective-permute-start(bf16[3,256,128]{2,1,0:T(8,128)(2,1)S(1)} %get-tuple-element.48), channel_id=1, source_target_pairs={{0,192},{16,208},{1,193},{17,209},{2,194},{18,210},{3,195},{19,211... | collective-permute-start | bytes 589832 | tf_op jit(solution)/shard_map/ppermute | solution.py:39
  21.5 9.2 %collective-permute-start.3 = (bf16[3,256,128]{2,1,0:T(8,128)(2,1)S(1)}, bf16[3,256,128]{2,1,0:T(8,128)(2,1)S(1)}, u32[]{:S(2)}, u32[]{:S(2)}) collective-permute-start(bf16[3,256,128]{2,1,0:T(8,128)(2,1)S(1)} %get-tuple-element.48), channel_id=1, source_target_pairs={{0,128},{16,144},{1,129},{17,145},{2,130},{18,146},{3,131},{19,147... | collective-permute-start | bytes 589832 | tf_op jit(solution)/shard_map/ppermute | solution.py:39
  22.3 10.4 %collective-permute-start.4 = (bf16[3,256,128]{2,1,0:T(8,128)(2,1)S(1)}, bf16[3,256,128]{2,1,0:T(8,128)(2,1)S(1)}, u32[]{:S(2)}, u32[]{:S(2)}) collective-permute-start(bf16[3,256,128]{2,1,0:T(8,128)(2,1)S(1)} %get-tuple-element.48), channel_id=1, source_target_pairs={{0,64},{16,80},{1,65},{17,81},{2,66},{18,82},{3,67},{19,83},{4,68}... | collective-permute-start | bytes 589832 | tf_op jit(solution)/shard_map/ppermute | solution.py:39
  23.1 13.1 %collective-permute-start.8 = (bf16[3,256,128]{2,1,0:T(8,128)(2,1)S(1)}, bf16[3,256,128]{2,1,0:T(8,128)(2,1)S(1)}, u32[]{:S(2)}, u32[]{:S(2)}) collective-permute-start(bf16[3,256,128]{2,1,0:T(8,128)(2,1)S(1)} %get-tuple-element.47), channel_id=1, source_target_pairs={{0,16},{16,0},{1,17},{17,1},{2,18},{18,2},{3,19},{19,3},{4,20},{20... | collective-permute-start | bytes 589832 | tf_op jit(solution)/shard_map/ppermute | solution.py:39
  23.2 50.5 %collective-permute-start.15 = (bf16[149,128]{1,0:T(8,128)(2,1)S(1)}, bf16[149,128]{1,0:T(8,128)(2,1)S(1)}, u32[]{:S(2)}, u32[]{:S(2)}) collective-permute-start(bf16[149,128]{1,0:T(8,128)(2,1)S(1)} %fusion.6), channel_id=1, source_target_pairs={{0,8},{16,24},{1,9},{17,25},{2,10},{18,26},{3,11},{19,27},{4,12},{... | collective-permute-start | bytes 114440 | tf_op jit(solution)/shard_map/ppermute | solution.py:39
  32.8 69.2 %copy-start.2 = (bf16[4,3,256,128]{3,2,1,0:T(8,128)(2,1)}, bf16[4,3,256,128]{3,2,1,0:T(8,128)(2,1)S(1)}, u32[]{:S(2)}) copy-start(bf16[4,3,256,128]{3,2,1,0:T(8,128)(2,1)S(1)} %pad_maximum_fusion.1.refs_0_) | copy-start | bytes 2359300
  32.8 41.3 %collective-permute-start.5 = (bf16[4,3,256,128]{3,2,1,0:T(8,128)(2,1)S(1)}, bf16[4,3,256,128]{3,2,1,0:T(8,128)(2,1)S(1)}, u32[]{:S(2)}, u32[]{:S(2)}) collective-permute-start(bf16[4,3,256,128]{3,2,1,0:T(8,128)(2,1)S(1)} %pad_maximum_fusion.1.refs_0_), channel_id=1, source_target_pairs={{0,40},{16,56},{1,41},{17,57},{2,42},{18,58},{3,43},{19,59},{4,44}... | collective-permute-start | bytes 2359304 | tf_op jit(solution)/shard_map/ppermute | solution.py:39
  36.3 24.7 %collective-permute-start.9 = (bf16[3,256,128]{2,1,0:T(8,128)(2,1)S(1)}, bf16[3,256,128]{2,1,0:T(8,128)(2,1)S(1)}, u32[]{:S(2)}, u32[]{:S(2)}) collective-permute-start(bf16[3,256,128]{2,1,0:T(8,128)(2,1)S(1)} %collective-permute-done.8), channel_id=1, source_target_pairs={{0,40},{16,56},{1,41},{17,57},{2,42},{18,58},{3,43},{19,59},{4,44}... | collective-permute-start | bytes 589832 | tf_op jit(solution)/shard_map/ppermute | solution.py:39
  37.1 23.9 %collective-permute-start.10 = (bf16[3,256,128]{2,1,0:T(8,128)(2,1)S(1)}, bf16[3,256,128]{2,1,0:T(8,128)(2,1)S(1)}, u32[]{:S(2)}, u32[]{:S(2)}) collective-permute-start(bf16[3,256,128]{2,1,0:T(8,128)(2,1)S(1)} %collective-permute-done.8), channel_id=1, source_target_pairs={{0,32},{16,48},{1,33},{17,49},{2,34},{18,50},{3,35},{19,51},{4,36}... | collective-permute-start | bytes 589832 | tf_op jit(solution)/shard_map/ppermute | solution.py:39
  37.4 28.1 %collective-permute-start.11 = (bf16[3,256,128]{2,1,0:T(8,128)(2,1)S(1)}, bf16[3,256,128]{2,1,0:T(8,128)(2,1)S(1)}, u32[]{:S(2)}, u32[]{:S(2)}) collective-permute-start(bf16[3,256,128]{2,1,0:T(8,128)(2,1)S(1)} %collective-permute-done.8), channel_id=1, source_target_pairs={{0,8},{16,24},{1,9},{17,25},{2,10},{18,26},{3,11},{19,27},{4,12},{... | collective-permute-start | bytes 589832 | tf_op jit(solution)/shard_map/ppermute | solution.py:39
  61.0 22.0 %collective-permute-start.6 = (bf16[4,3,256,128]{3,2,1,0:T(8,128)(2,1)S(1)}, bf16[4,3,256,128]{3,2,1,0:T(8,128)(2,1)}, u32[]{:S(2)}, u32[]{:S(2)}) collective-permute-start(bf16[4,3,256,128]{3,2,1,0:T(8,128)(2,1)S(1)} %pad_maximum_fusion.1.refs_0_), channel_id=1, source_target_pairs={{0,32},{16,48},{1,33},{17,49},{2,34},{18,50},{3,35},{19,51},{4,36}... | collective-permute-start | bytes 2359304 | tf_op jit(solution)/shard_map/ppermute | solution.py:39
  61.0 33.6 %collective-permute-start.7 = (bf16[4,3,256,128]{3,2,1,0:T(8,128)(2,1)S(1)}, bf16[4,3,256,128]{3,2,1,0:T(8,128)(2,1)}, u32[]{:S(2)}, u32[]{:S(2)}) collective-permute-start(bf16[4,3,256,128]{3,2,1,0:T(8,128)(2,1)S(1)} %pad_maximum_fusion.1.refs_0_), channel_id=1, source_target_pairs={{0,8},{16,24},{1,9},{17,25},{2,10},{18,26},{3,11},{19,27},{4,12},{... | collective-permute-start | bytes 2359304 | tf_op jit(solution)/shard_map/ppermute | solution.py:39
  65.6 36.4 %copy-start.3 = (bf16[4,3,256,128]{3,2,1,0:T(8,128)(2,1)}, bf16[4,3,256,128]{3,2,1,0:T(8,128)(2,1)S(1)}, u32[]{:S(2)}) copy-start(bf16[4,3,256,128]{3,2,1,0:T(8,128)(2,1)S(1)} %pad_maximum_fusion.2.refs_4_) | copy-start | bytes 2359300
  65.6 34.4 %collective-permute-start.12 = (bf16[4,3,256,128]{3,2,1,0:T(8,128)(2,1)S(1)}, bf16[4,3,256,128]{3,2,1,0:T(8,128)(2,1)}, u32[]{:S(2)}, u32[]{:S(2)}) collective-permute-start(bf16[4,3,256,128]{3,2,1,0:T(8,128)(2,1)S(1)} %pad_maximum_fusion.2.refs_4_), channel_id=1, source_target_pairs={{0,192},{16,208},{1,193},{17,209},{2,194},{18,210},{3,195},{19,211... | collective-permute-start | bytes 2359304 | tf_op jit(solution)/shard_map/ppermute | solution.py:39
  73.7 26.4 %collective-permute-start.13 = (bf16[4,3,256,128]{3,2,1,0:T(8,128)(2,1)S(1)}, bf16[4,3,256,128]{3,2,1,0:T(8,128)(2,1)}, u32[]{:S(2)}, u32[]{:S(2)}) collective-permute-start(bf16[4,3,256,128]{3,2,1,0:T(8,128)(2,1)S(1)} %pad_maximum_fusion.2.refs_4_), channel_id=1, source_target_pairs={{0,128},{16,144},{1,129},{17,145},{2,130},{18,146},{3,131},{19,147... | collective-permute-start | bytes 2359304 | tf_op jit(solution)/shard_map/ppermute | solution.py:39
  74.1 27.9 %copy-start.21 = (bf16[4,3,256,128]{3,2,1,0:T(8,128)(2,1)}, bf16[4,3,256,128]{3,2,1,0:T(8,128)(2,1)S(1)}, u32[]{:S(2)}) copy-start(bf16[4,3,256,128]{3,2,1,0:T(8,128)(2,1)S(1)} %collective-permute-done.5.refs_1_) | copy-start | bytes 2359300
  74.1 27.9 %collective-permute-start.14 = (bf16[4,3,256,128]{3,2,1,0:T(8,128)(2,1)S(1)}, bf16[4,3,256,128]{3,2,1,0:T(8,128)(2,1)}, u32[]{:S(2)}, u32[]{:S(2)}) collective-permute-start(bf16[4,3,256,128]{3,2,1,0:T(8,128)(2,1)S(1)} %pad_maximum_fusion.2.refs_4_), channel_id=1, source_target_pairs={{0,64},{16,80},{1,65},{17,81},{2,66},{18,82},{3,67},{19,83},{4,68}... | collective-permute-start | bytes 2359304 | tf_op jit(solution)/shard_map/ppermute | solution.py:39
  121.3 5.7 %collective-permute-start.16 = (bf16[4,152,128]{2,1,0:T(8,128)(2,1)}, bf16[4,152,128]{2,1,0:T(8,128)(2,1)S(1)}, u32[]{:S(2)}, u32[]{:S(2)}) collective-permute-start(bf16[4,152,128]{2,1,0:T(8,128)(2,1)} %get-tuple-element.24.refs_0_), channel_id=1, source_target_pairs={{0,192},{16,208},{1,193},{17,209},{2,194},{18,210},{3,195},{19,211... | collective-permute-start | bytes 466952 | tf_op jit(solution)/shard_map/ppermute | solution.py:39
  123.2 12.1 %collective-permute-start.17 = (bf16[4,152,128]{2,1,0:T(8,128)(2,1)}, bf16[4,152,128]{2,1,0:T(8,128)(2,1)S(1)}, u32[]{:S(2)}, u32[]{:S(2)}) collective-permute-start(bf16[4,152,128]{2,1,0:T(8,128)(2,1)} %get-tuple-element.24.refs_0_), channel_id=1, source_target_pairs={{0,128},{16,144},{1,129},{17,145},{2,130},{18,146},{3,131},{19,147... | collective-permute-start | bytes 466952 | tf_op jit(solution)/shard_map/ppermute | solution.py:39
  123.2 12.1 %collective-permute-start.18 = (bf16[4,152,128]{2,1,0:T(8,128)(2,1)}, bf16[4,152,128]{2,1,0:T(8,128)(2,1)S(1)}, u32[]{:S(2)}, u32[]{:S(2)}) collective-permute-start(bf16[4,152,128]{2,1,0:T(8,128)(2,1)} %get-tuple-element.24.refs_0_), channel_id=1, source_target_pairs={{0,64},{16,80},{1,65},{17,81},{2,66},{18,82},{3,67},{19,83},{4,68}... | collective-permute-start | bytes 466952 | tf_op jit(solution)/shard_map/ppermute | solution.py:39
  124.1 11.1 %collective-permute-start.19 = (bf16[4,152,128]{2,1,0:T(8,128)(2,1)}, bf16[4,152,128]{2,1,0:T(8,128)(2,1)S(1)}, u32[]{:S(2)}, u32[]{:S(2)}) collective-permute-start(bf16[4,152,128]{2,1,0:T(8,128)(2,1)} %get-tuple-element.25.refs_4_), channel_id=1, source_target_pairs={{0,40},{16,56},{1,41},{17,57},{2,42},{18,58},{3,43},{19,59},{4,44}... | collective-permute-start | bytes 466952 | tf_op jit(solution)/shard_map/ppermute | solution.py:39
  124.1 11.1 %collective-permute-start.20 = (bf16[4,152,128]{2,1,0:T(8,128)(2,1)}, bf16[4,152,128]{2,1,0:T(8,128)(2,1)S(1)}, u32[]{:S(2)}, u32[]{:S(2)}) collective-permute-start(bf16[4,152,128]{2,1,0:T(8,128)(2,1)} %get-tuple-element.25.refs_4_), channel_id=1, source_target_pairs={{0,32},{16,48},{1,33},{17,49},{2,34},{18,50},{3,35},{19,51},{4,36}... | collective-permute-start | bytes 466952 | tf_op jit(solution)/shard_map/ppermute | solution.py:39
  127.0 8.3 %copy-start.12 = (bf16[4,152,128]{2,1,0:T(8,128)(2,1)}, bf16[4,152,128]{2,1,0:T(8,128)(2,1)S(1)}, u32[]{:S(2)}) copy-start(bf16[4,152,128]{2,1,0:T(8,128)(2,1)S(1)} %collective-permute-done.16.refs_1_) | copy-start | bytes 466948
  127.0 8.3 %collective-permute-start.21 = (bf16[4,152,128]{2,1,0:T(8,128)(2,1)}, bf16[4,152,128]{2,1,0:T(8,128)(2,1)S(1)}, u32[]{:S(2)}, u32[]{:S(2)}) collective-permute-start(bf16[4,152,128]{2,1,0:T(8,128)(2,1)} %get-tuple-element.25.refs_4_), channel_id=1, source_target_pairs={{0,8},{16,24},{1,9},{17,25},{2,10},{18,26},{3,11},{19,27},{4,12},{... | collective-permute-start | bytes 466952 | tf_op jit(solution)/shard_map/ppermute | solution.py:39
  135.2 0.6 copy-start.13
  135.2 0.7 copy-start.14
  135.3 0.8 copy-start.15
  135.3 0.8 copy-start.16
  136.1 0.7 copy-start.17
  139.2 9.3 %collective-permute-start.22 = (bf16[4,152,128]{2,1,0:T(8,128)(2,1)}, bf16[4,152,128]{2,1,0:T(8,128)(2,1)S(1)}, u32[]{:S(2)}, u32[]{:S(2)}) collective-permute-start(bf16[4,152,128]{2,1,0:T(8,128)(2,1)} %get-tuple-element.27), channel_id=1, source_target_pairs={{0,40},{16,56},{1,41},{17,57},{2,42},{18,58},{3,43},{19,59},{4,44}... | collective-permute-start | bytes 466952 | tf_op jit(solution)/shard_map/ppermute | solution.py:39
  141.9 15.4 %collective-permute-start.23 = (bf16[4,152,128]{2,1,0:T(8,128)(2,1)}, bf16[4,152,128]{2,1,0:T(8,128)(2,1)S(1)}, u32[]{:S(2)}, u32[]{:S(2)}) collective-permute-start(bf16[4,152,128]{2,1,0:T(8,128)(2,1)} %get-tuple-element.28), channel_id=1, source_target_pairs={{0,32},{16,48},{1,33},{17,49},{2,34},{18,50},{3,35},{19,51},{4,36}... | collective-permute-start | bytes 466952 | tf_op jit(solution)/shard_map/ppermute | solution.py:39
  143.9 13.4 %collective-permute-start.24 = (bf16[4,152,128]{2,1,0:T(8,128)(2,1)}, bf16[4,152,128]{2,1,0:T(8,128)(2,1)S(1)}, u32[]{:S(2)}, u32[]{:S(2)}) collective-permute-start(bf16[4,152,128]{2,1,0:T(8,128)(2,1)} %get-tuple-element.29), channel_id=1, source_target_pairs={{0,8},{16,24},{1,9},{17,25},{2,10},{18,26},{3,11},{19,27},{4,12},{... | collective-permute-start | bytes 466952 | tf_op jit(solution)/shard_map/ppermute | solution.py:39
  145.2 12.1 %collective-permute-start.25 = (bf16[4,152,128]{2,1,0:T(8,128)(2,1)}, bf16[4,152,128]{2,1,0:T(8,128)(2,1)S(1)}, u32[]{:S(2)}, u32[]{:S(2)}) collective-permute-start(bf16[4,152,128]{2,1,0:T(8,128)(2,1)} %get-tuple-element.31), channel_id=1, source_target_pairs={{0,192},{16,208},{1,193},{17,209},{2,194},{18,210},{3,195},{19,211... | collective-permute-start | bytes 466952 | tf_op jit(solution)/shard_map/ppermute | solution.py:39
  147.4 9.9 %collective-permute-start.26 = (bf16[4,152,128]{2,1,0:T(8,128)(2,1)}, bf16[4,152,128]{2,1,0:T(8,128)(2,1)S(1)}, u32[]{:S(2)}, u32[]{:S(2)}) collective-permute-start(bf16[4,152,128]{2,1,0:T(8,128)(2,1)} %get-tuple-element.32), channel_id=1, source_target_pairs={{0,128},{16,144},{1,129},{17,145},{2,130},{18,146},{3,131},{19,147... | collective-permute-start | bytes 466952 | tf_op jit(solution)/shard_map/ppermute | solution.py:39
  148.5 8.8 %copy-start.6 = (bf16[4,152,128]{2,1,0:T(8,128)(2,1)}, bf16[4,152,128]{2,1,0:T(8,128)(2,1)S(1)}, u32[]{:S(2)}) copy-start(bf16[4,152,128]{2,1,0:T(8,128)(2,1)S(1)} %collective-permute-done.22.refs_1_) | copy-start | bytes 466948
  148.5 8.8 %collective-permute-start.27 = (bf16[4,152,128]{2,1,0:T(8,128)(2,1)}, bf16[4,152,128]{2,1,0:T(8,128)(2,1)S(1)}, u32[]{:S(2)}, u32[]{:S(2)}) collective-permute-start(bf16[4,152,128]{2,1,0:T(8,128)(2,1)} %get-tuple-element.33), channel_id=1, source_target_pairs={{0,64},{16,80},{1,65},{17,81},{2,66},{18,82},{3,67},{19,83},{4,68}... | collective-permute-start | bytes 466952 | tf_op jit(solution)/shard_map/ppermute | solution.py:39
  157.3 0.7 copy-start.7
  157.3 0.7 copy-start.8
  157.3 0.8 copy-start.9
  157.3 0.8 copy-start.10
  157.3 0.8 copy-start.11
  158.2 8.1 %copy-start.18 = (bf16[4096,16]{0,1:T(8,128)(2,1)S(1)}, bf16[4096,16]{0,1:T(8,128)(2,1)}, u32[]{:S(2)}) copy-start(bf16[4096,16]{0,1:T(8,128)(2,1)} %param.13) | copy-start | bytes 393220
  166.5 5.0 %collective-permute-start.28 = (bf16[16,4096]{1,0:T(8,128)(2,1)S(1)}, bf16[16,4096]{1,0:T(8,128)(2,1)S(1)}, u32[]{:S(2)}, u32[]{:S(2)}) collective-permute-start(bf16[16,4096]{1,0:T(8,128)(2,1)S(1)} %reshape.311), channel_id=1, source_target_pairs={{0,192},{16,208},{1,193},{17,209},{2,194},{18,210},{3,195},{19,211... | collective-permute-start | bytes 393224 | tf_op jit(solution)/shard_map/ppermute | solution.py:39
  168.1 6.5 %collective-permute-start.29 = (bf16[16,4096]{1,0:T(8,128)(2,1)S(1)}, bf16[16,4096]{1,0:T(8,128)(2,1)S(1)}, u32[]{:S(2)}, u32[]{:S(2)}) collective-permute-start(bf16[16,4096]{1,0:T(8,128)(2,1)S(1)} %reshape.311), channel_id=1, source_target_pairs={{0,128},{16,144},{1,129},{17,145},{2,130},{18,146},{3,131},{19,147... | collective-permute-start | bytes 393224 | tf_op jit(solution)/shard_map/ppermute | solution.py:39
  169.3 6.7 %collective-permute-start.30 = (bf16[16,4096]{1,0:T(8,128)(2,1)S(1)}, bf16[16,4096]{1,0:T(8,128)(2,1)S(1)}, u32[]{:S(2)}, u32[]{:S(2)}) collective-permute-start(bf16[16,4096]{1,0:T(8,128)(2,1)S(1)} %reshape.311), channel_id=1, source_target_pairs={{0,64},{16,80},{1,65},{17,81},{2,66},{18,82},{3,67},{19,83},{4,68}... | collective-permute-start | bytes 393224 | tf_op jit(solution)/shard_map/ppermute | solution.py:39
  176.0 19.7 %collective-permute-start.31 = (bf16[4,16,4096]{2,1,0:T(8,128)(2,1)S(1)}, bf16[4,16,4096]{2,1,0:T(8,128)(2,1)S(1)}, u32[]{:S(2)}, u32[]{:S(2)}) collective-permute-start(bf16[4,16,4096]{2,1,0:T(8,128)(2,1)S(1)} %get-tuple-element.44), channel_id=1, source_target_pairs={{0,40},{16,56},{1,41},{17,57},{2,42},{18,58},{3,43},{19,59},{4,44}... | collective-permute-start | bytes 1572872 | tf_op jit(solution)/shard_map/ppermute | solution.py:39
  179.2 16.6 %collective-permute-start.32 = (bf16[4,16,4096]{2,1,0:T(8,128)(2,1)S(1)}, bf16[4,16,4096]{2,1,0:T(8,128)(2,1)S(1)}, u32[]{:S(2)}, u32[]{:S(2)}) collective-permute-start(bf16[4,16,4096]{2,1,0:T(8,128)(2,1)S(1)} %get-tuple-element.44), channel_id=1, source_target_pairs={{0,32},{16,48},{1,33},{17,49},{2,34},{18,50},{3,35},{19,51},{4,36}... | collective-permute-start | bytes 1572872 | tf_op jit(solution)/shard_map/ppermute | solution.py:39
  180.7 18.4 %collective-permute-start.33 = (bf16[4,16,4096]{2,1,0:T(8,128)(2,1)S(1)}, bf16[4,16,4096]{2,1,0:T(8,128)(2,1)S(1)}, u32[]{:S(2)}, u32[]{:S(2)}) collective-permute-start(bf16[4,16,4096]{2,1,0:T(8,128)(2,1)S(1)} %get-tuple-element.44), channel_id=1, source_target_pairs={{0,8},{16,24},{1,9},{17,25},{2,10},{18,26},{3,11},{19,27},{4,12},{... | collective-permute-start | bytes 1572872 | tf_op jit(solution)/shard_map/ppermute | solution.py:39
  199.2 1.1 copy-start.1
  199.4 4.9 %copy-start = (bf16[4,4,16,4096]{3,2,1,0:T(8,128)(2,1)}, bf16[4,4,16,4096]{3,2,1,0:T(8,128)(2,1)S(1)}, u32[]{:S(2)}) copy-start(bf16[4,4,16,4096]{3,2,1,0:T(8,128)(2,1)S(1)} %pad_maximum_fusion.own_ref) | copy-start | bytes 6291460
  199.4 4.8 %collective-permute-start.34 = (bf16[4,4,16,4096]{3,2,1,0:T(8,128)(2,1)S(1)}, bf16[4,4,16,4096]{3,2,1,0:T(8,128)(2,1)}, u32[]{:S(2)}, u32[]{:S(2)}) collective-permute-start(bf16[4,4,16,4096]{3,2,1,0:T(8,128)(2,1)S(1)} %pad_maximum_fusion.own_ref), channel_id=1, source_target_pairs={{0,16},{16,0},{1,17},{17,1},{2,18},{18,2},{3,19},{19,3},{4,20},{20... | collective-permute-start | bytes 6291464 | tf_op jit(solution)/shard_map/ppermute | solution.py:39
  200.9 8.7 %collective-permute-start = (bf16[512,256]{1,0:T(8,128)(2,1)S(1)}, bf16[512,256]{1,0:T(8,128)(2,1)S(1)}, u32[]{:S(2)}, u32[]{:S(2)}) collective-permute-start(bf16[512,256]{1,0:T(8,128)(2,1)S(1)} %get-tuple-element.42), channel_id=1, source_target_pairs={{0,8},{16,24},{1,9},{17,25},{2,10},{18,26},{3,11},{19,27},{4,12},{... | collective-permute-start | bytes 786440 | tf_op jit(solution)/shard_map/ppermute | solution.py:39
  209.7 12.6 %copy-start.5 = (bf16[512,256]{1,0:T(8,128)(2,1)}, bf16[512,256]{1,0:T(8,128)(2,1)S(1)}, u32[]{:S(2)}) copy-start(bf16[512,256]{1,0:T(8,128)(2,1)S(1)} %collective-permute-done.residual_ref) | copy-start | bytes 786436
  227.9 8.7 %collective-permute-start.35 = (bf16[512,256]{1,0:T(8,128)(2,1)}, bf16[512,256]{1,0:T(8,128)(2,1)S(1)}, u32[]{:S(2)}, u32[]{:S(2)}) collective-permute-start(bf16[512,256]{1,0:T(8,128)(2,1)} %output.2), channel_id=1, source_target_pairs={{0,8},{16,24},{1,9},{17,25},{2,10},{18,26},{3,11},{19,27},{4,12},{... | collective-permute-start | bytes 786440 | tf_op jit(solution)/shard_map/ppermute | solution.py:39
Sparse Core Ops, SparseCore 0:
  18.0 57.2 all-gather.5
  166.3 55.8 all-gather.3

commit v3 on v2

--- a/solution.py
+++ b/solution.py
@@ -492,7 +492,7 @@
     )(starts, ends, picks, proj, *partials, taps, medium, *halos)
 
 
-def assemble_kernel(place_ref, own_ref, other_ref, out_ref, sems):
+def assemble_kernel(place_ref, own_ref, other_ref, out_ref, scratch, sems):
     x, y, core = place_ref[0], place_ref[1], place_ref[2]
     started = []
     for other, ref in enumerate((own_ref, other_ref)):
@@ -503,7 +503,7 @@
                 rows = pl.ds(pl.multiple_of(owner * 16, 16), 16)
                 started.append(
                     pltpu.make_async_copy(
-                        ref.at[dy, dx], out_ref.at[lax.rem(to_y, 2), rows], sems.at[other, dy, dx]
+                        ref.at[dy, dx], scratch.at[lax.rem(to_y, 2), rows], sems.at[other, dy, dx]
                     )
                 )
     for copy in started:
@@ -511,14 +511,25 @@
     for copy in started:
         copy.wait()
 
+    def turn(i, carry):
+        lanes = pl.ds(pl.multiple_of(i * PIECE, PIECE), PIECE)
+        for column in range(2):
+            value = scratch[column, :, lanes].astype(jnp.float32)
+            out_ref[column, lanes, :] = jnp.transpose(value).astype(jnp.bfloat16)
+        return carry
+
+    lax.fori_loop(0, D // PIECE, turn, 0)
+
 
 def assemble(place, own, other):
     return pl.pallas_call(
         assemble_kernel,
-        out_shape=jax.ShapeDtypeStruct((2, PIECE, D), jnp.bfloat16),
+        out_shape=jax.ShapeDtypeStruct((2, D, PIECE), jnp.bfloat16),
         in_specs=[scalars()] + [anywhere()] * 2,
         out_specs=full(),
-        scratch_shapes=[pltpu.SemaphoreType.DMA((2, 4, 4))],
+        scratch_shapes=[
+            pltpu.VMEM((2, PIECE, D), jnp.bfloat16), pltpu.SemaphoreType.DMA((2, 4, 4)),
+        ],
         cost_estimate=pl.CostEstimate(flops=1 << 10, bytes_accessed=8 << 20, transcendentals=0),
         name="assemble",
     )(place, own, other)
@@ -549,11 +560,12 @@
         for copy in copies(i):
             copy.wait()
         rows = pl.ds(pl.multiple_of(i * BLK, BLK), BLK)
-        summed = lax.dot_general(
-            scratch[rows, :], weights[...], (((1,), (1,)), ((), ())),
-            preferred_element_type=jnp.float32,
-        )
-        out_ref[rows, :] = (residual_ref[rows, :].astype(jnp.float32) + summed).astype(jnp.bfloat16)
+        summed = jnp.dot(scratch[rows, :], weights[...], preferred_element_type=jnp.float32)
+        value = (residual_ref[rows, :].astype(jnp.float32) + summed).astype(jnp.bfloat16)
+        if side == 0:
+            out_ref[y_low, rows, :] = value
+        else:
+            out_ref[rows, :] = value
         return carry
 
     lax.fori_loop(0, 2, start, 0)
@@ -564,12 +576,14 @@
 def output(side, place, residual, weights, gated):
     return pl.pallas_call(
         functools.partial(output_kernel, side),
-        out_shape=jax.ShapeDtypeStruct((HALF, PIECE), jnp.bfloat16),
+        out_shape=jax.ShapeDtypeStruct(
+            (2, HALF, PIECE) if side == 0 else (HALF, PIECE), jnp.bfloat16
+        ),
         in_specs=[scalars(), full()] + [anywhere()] * 2,
         out_specs=full(),
         scratch_shapes=[
             pltpu.VMEM((HALF, D), jnp.bfloat16),
-            pltpu.VMEM((PIECE, D), jnp.bfloat16),
+            pltpu.VMEM((D, PIECE), jnp.bfloat16),
             pltpu.SemaphoreType.DMA((2, 16)),
             pltpu.SemaphoreType.DMA,
         ],
@@ -676,9 +690,8 @@
     place, theirs = lax.optimization_barrier((place, theirs))
     theirs = send(theirs, swap_y)
     ours = output(0, place, mine, columns, gathered)
-    first = jnp.where(y_low == 0, ours, theirs)
-    second = jnp.where(y_low == 0, theirs, ours)
-    return jnp.concatenate([first, second], axis=0)
+    ours = lax.dynamic_update_index_in_dim(ours, theirs, 1 - y_low, 0)
+    return ours.reshape(2 * HALF, PIECE)
 
 
 def solution(mesh):

time: 248 us -> 247 us (level)
  waiting for transfers between devices: 103 us -> 100 us
  transfers between devices with their start and end apart: 38 -> 38, of which waited for: 18 -> 18; matrix products, arithmetic and copies ran while one was open for 3% -> 3% of each run, Pallas kernels for 10% -> 11%
where the time goes in v3:
time: 247 us; the launch traced here: 244 us
  waiting for transfers between devices  100 us (40%)
  Pallas kernels  61.3 us (25%)
  starting transfers between devices  54.4 us (22%)
  between operations  13.9 us (6%)
  other arithmetic  7.3 us (3%)
  local copies, waits for them, and re-layouts  6.89 us (3%)
    ppermute x36, waiting for transfers between devices, send(): return lax.ppermute(value, AXES, permutation(move))  90 us
    ppermute x36, starting transfers between devices, send(): return lax.ppermute(value, AXES, permutation(move))  54.4 us
    pallas_call x1, Pallas kernels, project(): pl.pallas_call(project_kernel, out_shape=jax.ShapeDtypeStruct((3, 4, BLK,...  14.6 us
    pallas_call x2, Pallas kernels, inner(): pl.pallas_call(functools.partial(inner_kernel, index), grid_spec=pltpu.Pr...  12.8 us
    pallas_call x2, Pallas kernels, output(): pl.pallas_call(functools.partial(output_kernel, side), out_shape=jax.Shap...  11.1 us
    all_gather x2, waiting for transfers between devices, gather_line(): return lax.all_gather(value, AXES, axis=0, axis_index_groups=groups)  10.4 us
    pallas_call x1, Pallas kernels, edges(): pl.pallas_call(edge_kernel, grid_spec=pltpu.PrefetchScalarGridSpec(num_sc...  8.05 us
    pallas_call x1, Pallas kernels, assemble(): pl.pallas_call(assemble_kernel, out_shape=jax.ShapeDtypeStruct((2, D, PIE...  7.58 us
  transfers between devices with their start and end apart: 38, of which 18 were waited for; matrix products, arithmetic and copies ran while one was open for 3% of the time, Pallas kernels for 11%

profile of v3, /device:TPU:32, one launch (start us, length us, event | category | flops | bytes accessed | tf_op | source)
XLA Modules:
  0.0 244.1 jit_solution(3716668761963971562)
XLA Ops:
  6.5 0.7 reshape.318
  7.3 1.3 fusion.1
  8.8 1.7 collective-permute-start.1
  10.5 6.6 %collective-permute-done.1 = bf16[520,256]{1,0:T(8,128)(2,1)S(1)} collective-permute-done((bf16[520,256]{1,0:T(8,128)(2,1)S(1)}, bf16[520,256]{1,0:T(8,128)(2,1)S(1)}, u32[]{:S(2)}, u32[]{:S(2)}) %collective-permute-start.1) | collective-permute-done | bytes 266272 | tf_op jit(solution)/shard_map/ppermute | solution.py:39
  17.0 0.9 pad_maximum_fusion.3
  18.6 2.8 %collective-permute-start.2 = (bf16[3,256,128]{2,1,0:T(8,128)(2,1)S(1)}, bf16[3,256,128]{2,1,0:T(8,128)(2,1)S(1)}, u32[]{:S(2)}, u32[]{:S(2)}) collective-permute-start(bf16[3,256,128]{2,1,0:T(8,128)(2,1)S(1)} %get-tuple-element.46), channel_id=1, source_target_pairs={{0,192},{16,208},{1,193},{17,209},{2,194},{18,210},{3,195},{19,211... | collective-permute-start | bytes 589832 | tf_op jit(solution)/shard_map/ppermute | solution.py:39
  21.5 0.8 collective-permute-start.3
  22.3 0.9 collective-permute-start.4
  23.2 1.7 collective-permute-start.15
  25.1 3.9 %collective-permute-done.2 = bf16[3,256,128]{2,1,0:T(8,128)(2,1)S(1)} collective-permute-done((bf16[3,256,128]{2,1,0:T(8,128)(2,1)S(1)}, bf16[3,256,128]{2,1,0:T(8,128)(2,1)S(1)}, u32[]{:S(2)}, u32[]{:S(2)}) %collective-permute-start.2) | collective-permute-done | bytes 196640 | tf_op jit(solution)/shard_map/ppermute | solution.py:39
  29.0 1.6 collective-permute-done.3
  30.6 2.1 collective-permute-done.4
  32.8 3.1 %collective-permute-start.5 = (bf16[4,3,256,128]{3,2,1,0:T(8,128)(2,1)S(1)}, bf16[4,3,256,128]{3,2,1,0:T(8,128)(2,1)S(1)}, u32[]{:S(2)}, u32[]{:S(2)}) collective-permute-start(bf16[4,3,256,128]{3,2,1,0:T(8,128)(2,1)S(1)} %pad_maximum_fusion.1.refs_0_), channel_id=1, source_target_pairs={{0,40},{16,56},{1,41},{17,57},{2,42},{18,58},{3,43},{19,59},{4,44}... | collective-permute-start | bytes 2359304 | tf_op jit(solution)/shard_map/ppermute | solution.py:39
  36.3 0.8 collective-permute-start.9
  37.4 1.0 collective-permute-start.11
  38.4 0.7 reduce-window.9
  39.3 0.7 stack.96.place_ref
  40.0 21.0 %collective-permute-done.9 = bf16[3,256,128]{2,1,0:T(8,128)(2,1)S(1)} collective-permute-done((bf16[3,256,128]{2,1,0:T(8,128)(2,1)S(1)}, bf16[3,256,128]{2,1,0:T(8,128)(2,1)S(1)}, u32[]{:S(2)}, u32[]{:S(2)}) %collective-permute-start.9) | collective-permute-done | bytes 196640 | tf_op jit(solution)/shard_map/ppermute | solution.py:39
  61.0 4.5 %collective-permute-start.7 = (bf16[4,3,256,128]{3,2,1,0:T(8,128)(2,1)S(1)}, bf16[4,3,256,128]{3,2,1,0:T(8,128)(2,1)}, u32[]{:S(2)}, u32[]{:S(2)}) collective-permute-start(bf16[4,3,256,128]{3,2,1,0:T(8,128)(2,1)S(1)} %pad_maximum_fusion.1.refs_0_), channel_id=1, source_target_pairs={{0,8},{16,24},{1,9},{17,25},{2,10},{18,26},{3,11},{19,27},{4,12},{... | collective-permute-start | bytes 2359304 | tf_op jit(solution)/shard_map/ppermute | solution.py:39
  65.6 8.0 %collective-permute-start.12 = (bf16[4,3,256,128]{3,2,1,0:T(8,128)(2,1)S(1)}, bf16[4,3,256,128]{3,2,1,0:T(8,128)(2,1)}, u32[]{:S(2)}, u32[]{:S(2)}) collective-permute-start(bf16[4,3,256,128]{3,2,1,0:T(8,128)(2,1)S(1)} %pad_maximum_fusion.2.refs_4_), channel_id=1, source_target_pairs={{0,192},{16,208},{1,193},{17,209},{2,194},{18,210},{3,195},{19,211... | collective-permute-start | bytes 2359304 | tf_op jit(solution)/shard_map/ppermute | solution.py:39
  75.3 0.6 reshape.322.taps_ref
  75.9 7.1 %collective-permute-done.6.refs_2_ = bf16[4,3,256,128]{3,2,1,0:T(8,128)(2,1)} collective-permute-done((bf16[4,3,256,128]{3,2,1,0:T(8,128)(2,1)S(1)}, bf16[4,3,256,128]{3,2,1,0:T(8,128)(2,1)}, u32[]{:S(2)}, u32[]{:S(2)}) %collective-permute-start.6) | collective-permute-done | bytes 786464 | tf_op jit(solution)/shard_map/ppermute | solution.py:39
  83.0 11.5 %collective-permute-done.7.refs_3_ = bf16[4,3,256,128]{3,2,1,0:T(8,128)(2,1)} collective-permute-done((bf16[4,3,256,128]{3,2,1,0:T(8,128)(2,1)S(1)}, bf16[4,3,256,128]{3,2,1,0:T(8,128)(2,1)}, u32[]{:S(2)}, u32[]{:S(2)}) %collective-permute-start.7) | collective-permute-done | bytes 786464 | tf_op jit(solution)/shard_map/ppermute | solution.py:39
  94.6 5.5 %collective-permute-done.12.refs_5_ = bf16[4,3,256,128]{3,2,1,0:T(8,128)(2,1)} collective-permute-done((bf16[4,3,256,128]{3,2,1,0:T(8,128)(2,1)S(1)}, bf16[4,3,256,128]{3,2,1,0:T(8,128)(2,1)}, u32[]{:S(2)}, u32[]{:S(2)}) %collective-permute-start.12) | collective-permute-done | bytes 786464 | tf_op jit(solution)/shard_map/ppermute | solution.py:39
  100.1 1.9 collective-permute-done.14.refs_7_
  102.0 14.6 %project.1.proj_ref = bf16[3,4,256,256]{3,2,1,0:T(8,128)(2,1)} custom-call(s32[5]{0:T(128)} %stack.96.place_ref, bf16[16,2,520,256]{3,2,1,0:T(8,128)(2,1)} %bitcast.73, bf16[4,3,256,128]{3,2,1,0:T(8,128)(2,1)} %copy-done.2, bf16[4,3,256,128]{3,2,1,0:T(8,128)(2,1)} %copy-done.21, bf16[4,3,256,128]{3,2,1,0:T(8,128)(2,1)} %collective-permute-done.6.refs_2_, ...), custom_call_target="tpu_custom_call" | custom-call | flops 6442450944 | bytes 16777216 | tf_op jit(solution)/shard_map/project/pallas_call | solution.py:186
  116.6 4.7 %products.1 = (bf16[4,256,256]{2,1,0:T(8,128)(2,1)}, bf16[4,152,128]{2,1,0:T(8,128)(2,1)}, bf16[4,152,128]{2,1,0:T(8,128)(2,1)}) custom-call(s32[4]{0:T(128)} %slice_multiply_fusion.2.start_ref, s32[4]{0:T(128)} %bitcast.68, bf16[3,4,256,256]{3,2,1,0:T(8,128)(2,1)} %project.1.proj_ref, bf16[7,3,256]{2,1,0:T(4,128)(2,1)} %reshape.322.taps_ref), custom_call_target="tpu_custom_call" | custom-call | flops 62914560 | bytes 4194304 | tf_op jit(solution)/shard_map/products/pallas_call | solution.py:266
  121.3 1.9 collective-permute-start.16
  123.2 1.0 collective-permute-start.18
  124.1 2.1 collective-permute-start.20
  126.2 0.8 collective-permute-done.16.refs_1_
  128.2 0.7 fusion.4.medium_ref
  128.8 6.4 %inner.2.early_ref = f32[2,256,256]{2,1,0:T(8,128)} custom-call(s32[4]{0:T(128)} %slice_multiply_fusion.2.start_ref, s32[4]{0:T(128)} %bitcast.69, bf16[4,256,256]{2,1,0:T(8,128)(2,1)} %get-tuple-element.21.product_ref, f32[128,256]{1,0:T(8,128)} %fusion.4.medium_ref), custom_call_target="tpu_custom_call" | custom-call | flops 33554432 | bytes 1048576 | tf_op jit(solution)/shard_map/inner/pallas_call | solution.py:346
  136.1 0.7 copy-done.17
  136.8 2.5 %route.1 = (bf16[4,152,128]{2,1,0:T(8,128)(2,1)}, bf16[4,152,128]{2,1,0:T(8,128)(2,1)}, bf16[4,152,128]{2,1,0:T(8,128)(2,1)}, bf16[4,152,128]{2,1,0:T(8,128)(2,1...) custom-call(s32[2,4,4]{2,1,0:T(4,128)} %pad_add_fusion.table_ref, ...), custom_call_target="tpu_custom_call" | custom-call | flops 1024 | bytes 4194304 | tf_op jit(solution)/shard_map/route/pallas_call | solution.py:377
  139.2 2.7 %collective-permute-start.22 = (bf16[4,152,128]{2,1,0:T(8,128)(2,1)}, bf16[4,152,128]{2,1,0:T(8,128)(2,1)S(1)}, u32[]{:S(2)}, u32[]{:S(2)}) collective-permute-start(bf16[4,152,128]{2,1,0:T(8,128)(2,1)} %get-tuple-element.27), channel_id=1, source_target_pairs={{0,40},{16,56},{1,41},{17,57},{2,42},{18,58},{3,43},{19,59},{4,44}... | collective-permute-start | bytes 466952 | tf_op jit(solution)/shard_map/ppermute | solution.py:39
  141.9 2.0 collective-permute-start.23
  143.9 1.3 collective-permute-start.24
  145.2 2.2 collective-permute-start.25
  147.4 1.1 collective-permute-start.26
  148.5 1.7 collective-permute-start.27
  150.9 6.4 %inner.3.late_ref = f32[2,256,256]{2,1,0:T(8,128)} custom-call(s32[4]{0:T(128)} %slice_multiply_fusion.2.start_ref, s32[4]{0:T(128)} %bitcast.70, bf16[4,256,256]{2,1,0:T(8,128)(2,1)} %get-tuple-element.21.product_ref, f32[128,256]{1,0:T(8,128)} %fusion.4.medium_ref), custom_call_target="tpu_custom_call" | custom-call | flops 33554432 | bytes 1048576 | tf_op jit(solution)/shard_map/inner/pallas_call | solution.py:346
  158.2 8.1 %edges.1 = bf16[4,256,256]{2,1,0:T(8,128)(2,1)} custom-call(s32[4]{0:T(128)} %slice_multiply_fusion.2.start_ref, s32[4]{0:T(128)} %bitcast.71, s32[2,4]{1,0:T(2,128)} %pad_add_fusion.1.pick_ref, bf16[3,4,256,256]{3,2,1,0:T(8,128)(2,1)} %project.1.proj_ref, f32[2,256,256]{2,1,0:T(8,128)} %inner.2.early_ref, f32[2,256,256]{2,1,0:T(8,128)} %inner.3.late_ref, ...), custom_call_target="tpu_custom_call" | custom-call | flops 16777216 | bytes 3145728 | tf_op jit(solution)/shard_map/edges/pallas_call | solution.py:464
  166.5 1.6 collective-permute-start.28
  168.1 1.2 collective-permute-start.29
  169.3 1.1 collective-permute-start.30
  170.4 1.2 collective-permute-done.28
  171.6 3.0 %collective-permute-done.29 = bf16[16,4096]{1,0:T(8,128)(2,1)S(1)} collective-permute-done((bf16[16,4096]{1,0:T(8,128)(2,1)S(1)}, bf16[16,4096]{1,0:T(8,128)(2,1)S(1)}, u32[]{:S(2)}, u32[]{:S(2)}) %collective-permute-start.29) | collective-permute-done | bytes 131104 | tf_op jit(solution)/shard_map/ppermute | solution.py:39
  174.6 1.3 collective-permute-done.30
  176.1 3.1 %collective-permute-start.31 = (bf16[4,16,4096]{2,1,0:T(8,128)(2,1)S(1)}, bf16[4,16,4096]{2,1,0:T(8,128)(2,1)S(1)}, u32[]{:S(2)}, u32[]{:S(2)}) collective-permute-start(bf16[4,16,4096]{2,1,0:T(8,128)(2,1)S(1)} %get-tuple-element.42), channel_id=1, source_target_pairs={{0,40},{16,56},{1,41},{17,57},{2,42},{18,58},{3,43},{19,59},{4,44}... | collective-permute-start | bytes 1572872 | tf_op jit(solution)/shard_map/ppermute | solution.py:39
  179.2 1.6 collective-permute-start.32
  180.7 1.0 collective-permute-start.33
  181.7 14.0 %collective-permute-done.31 = bf16[4,16,4096]{2,1,0:T(8,128)(2,1)S(1)} collective-permute-done((bf16[4,16,4096]{2,1,0:T(8,128)(2,1)S(1)}, bf16[4,16,4096]{2,1,0:T(8,128)(2,1)S(1)}, u32[]{:S(2)}, u32[]{:S(2)}) %collective-permute-start.31) | collective-permute-done | bytes 524320 | tf_op jit(solution)/shard_map/ppermute | solution.py:39
  195.8 3.4 %collective-permute-done.33 = bf16[4,16,4096]{2,1,0:T(8,128)(2,1)S(1)} collective-permute-done((bf16[4,16,4096]{2,1,0:T(8,128)(2,1)S(1)}, bf16[4,16,4096]{2,1,0:T(8,128)(2,1)S(1)}, u32[]{:S(2)}, u32[]{:S(2)}) %collective-permute-start.33) | collective-permute-done | bytes 524320 | tf_op jit(solution)/shard_map/ppermute | solution.py:39
  199.6 0.7 copy-done.1
  200.2 0.7 broadcast_select_fusion.1
  201.0 3.3 %collective-permute-done.34.other_ref = bf16[4,4,16,4096]{3,2,1,0:T(8,128)(2,1)} collective-permute-done((bf16[4,4,16,4096]{3,2,1,0:T(8,128)(2,1)S(1)}, bf16[4,4,16,4096]{3,2,1,0:T(8,128)(2,1)}, u32[]{:S(2)}, u32[]{:S(2)}) %collective-permute-start.34) | collective-permute-done | bytes 2097184 | tf_op jit(solution)/shard_map/ppermute | solution.py:39
  204.3 7.6 %assemble.1.w_ref = bf16[2,4096,256]{2,1,0:T(8,128)(2,1)} custom-call(s32[5]{0:T(128)} %stack.96.place_ref, bf16[4,4,16,4096]{3,2,1,0:T(8,128)(2,1)} %copy-done, bf16[4,4,16,4096]{3,2,1,0:T(8,128)(2,1)} %collective-permute-done.34.other_ref), custom_call_target="tpu_custom_call" | custom-call | flops 1024 | bytes 8388608 | tf_op jit(solution)/shard_map/assemble/pallas_call | solution.py:525
  211.9 10.4 %all-gather.4.cloned.1.call-done.gated_ref = bf16[16,2,512,256]{3,2,1,0:T(8,128)(2,1)} async-done(((bf16[1,2,512,256]{3,2,1,0:T(8,128)(2,1)}), bf16[16,2,512,256]{3,2,1,0:T(8,128)(2,1)}) %all-gather.4.cloned.1.call-update) | async-done | bytes 8388624 | tf_op jit(solution)/shard_map/all_gather | solution.py:64
  222.3 5.5 %output.2 = bf16[512,256]{1,0:T(8,128)(2,1)} custom-call(s32[5]{0:T(128)} %stack.96.place_ref, bf16[512,256]{1,0:T(8,128)(2,1)} %copy-done.5, bf16[2,4096,256]{2,1,0:T(8,128)(2,1)} %assemble.1.w_ref, bf16[16,2,512,256]{3,2,1,0:T(8,128)(2,1)} %all-gather.4.cloned.1.call-done.gated_ref), custom_call_target="tpu_custom_call" | custom-call | flops 1073741824 | bytes 6291456 | tf_op jit(solution)/shard_map/output/pallas_call | solution.py:577
  227.8 1.6 collective-permute-start.35
  229.4 5.6 %output.3 = bf16[2,512,256]{2,1,0:T(8,128)(2,1)} custom-call(s32[5]{0:T(128)} %stack.96.place_ref, bf16[512,256]{1,0:T(8,128)(2,1)} %get-tuple-element.39.residual_ref, bf16[2,4096,256]{2,1,0:T(8,128)(2,1)} %assemble.1.w_ref, bf16[16,2,512,256]{3,2,1,0:T(8,128)(2,1)} %all-gather.4.cloned.1.call-done.gated_ref), custom_call_target="tpu_custom_call" | custom-call | flops 1073741824 | bytes 6291456 | tf_op jit(solution)/shard_map/output/pallas_call | solution.py:577
  235.0 1.5 collective-permute-done.35
  236.6 0.7 bitcast_dynamic-update-slice_fusion
  (119 shorter events, 8.1 us)
Async XLA Ops:
  6.5 95.5 %all-gather.6.cloned.1.call-start = ((), (), s32[]{:S(2)}) async-start(), calls=%async_computation.1 | async-start | bytes 9052160 | tf_op jit(solution)/shard_map/all_gather | solution.py:64
  8.5 9.5 %copy-start.4 = (bf16[3,256,256]{2,1,0:T(8,128)(2,1)S(1)}, bf16[3,256,256]{2,1,0:T(8,128)(2,1)}, u32[]{:S(2)}) copy-start(bf16[3,256,256]{2,1,0:T(8,128)(2,1)} %param.10) | copy-start | bytes 1179652
  8.8 8.2 %collective-permute-start.1 = (bf16[520,256]{1,0:T(8,128)(2,1)S(1)}, bf16[520,256]{1,0:T(8,128)(2,1)S(1)}, u32[]{:S(2)}, u32[]{:S(2)}) collective-permute-start(bf16[520,256]{1,0:T(8,128)(2,1)S(1)} %get-tuple-element.38), channel_id=1, source_target_pairs={{0,8},{16,24},{1,9},{17,25},{2,10},{18,26},{3,11},{19,27},{4,12},{... | collective-permute-start | bytes 798728 | tf_op jit(solution)/shard_map/ppermute | solution.py:39
  17.9 5.3 %copy-start.20 = (bf16[7,3,256]{2,0,1:T(8,128)(2,1)S(1)}, bf16[7,3,256]{2,0,1:T(8,128)(2,1)}, u32[]{:S(2)}) copy-start(bf16[7,3,256]{2,0,1:T(8,128)(2,1)} %param.11) | copy-start | bytes 32260
  17.9 5.3 %copy-start.19 = (bf16[128,256]{1,0:T(8,128)(2,1)S(1)}, bf16[128,256]{1,0:T(8,128)(2,1)}, u32[]{:S(2)}) copy-start(bf16[128,256]{1,0:T(8,128)(2,1)} %param.12) | copy-start | bytes 196612
  17.9 204.4 %all-gather.4.cloned.1.call-start = ((), (), s32[]{:S(2)}) async-start(), calls=%async_computation | async-start | bytes 8912896 | tf_op jit(solution)/shard_map/all_gather | solution.py:64
  18.2 17.9 %copy-start.23 = (s32[64]{0:T(128)S(1)}, s32[64]{0:T(128)}, u32[]{:S(2)}) copy-start(s32[64]{0:T(128)} %param.15) | copy-start | bytes 772
  18.2 20.2 %copy-start.22 = (s32[4]{0:T(128)S(1)}, s32[4]{0:T(128)}, u32[]{:S(2)}) copy-start(s32[4]{0:T(128)} %param.14) | copy-start | bytes 52
  18.6 10.4 %collective-permute-start.2 = (bf16[3,256,128]{2,1,0:T(8,128)(2,1)S(1)}, bf16[3,256,128]{2,1,0:T(8,128)(2,1)S(1)}, u32[]{:S(2)}, u32[]{:S(2)}) collective-permute-start(bf16[3,256,128]{2,1,0:T(8,128)(2,1)S(1)} %get-tuple-element.46), channel_id=1, source_target_pairs={{0,192},{16,208},{1,193},{17,209},{2,194},{18,210},{3,195},{19,211... | collective-permute-start | bytes 589832 | tf_op jit(solution)/shard_map/ppermute | solution.py:39
  21.5 9.2 %collective-permute-start.3 = (bf16[3,256,128]{2,1,0:T(8,128)(2,1)S(1)}, bf16[3,256,128]{2,1,0:T(8,128)(2,1)S(1)}, u32[]{:S(2)}, u32[]{:S(2)}) collective-permute-start(bf16[3,256,128]{2,1,0:T(8,128)(2,1)S(1)} %get-tuple-element.46), channel_id=1, source_target_pairs={{0,128},{16,144},{1,129},{17,145},{2,130},{18,146},{3,131},{19,147... | collective-permute-start | bytes 589832 | tf_op jit(solution)/shard_map/ppermute | solution.py:39
  22.3 10.4 %collective-permute-start.4 = (bf16[3,256,128]{2,1,0:T(8,128)(2,1)S(1)}, bf16[3,256,128]{2,1,0:T(8,128)(2,1)S(1)}, u32[]{:S(2)}, u32[]{:S(2)}) collective-permute-start(bf16[3,256,128]{2,1,0:T(8,128)(2,1)S(1)} %get-tuple-element.46), channel_id=1, source_target_pairs={{0,64},{16,80},{1,65},{17,81},{2,66},{18,82},{3,67},{19,83},{4,68}... | collective-permute-start | bytes 589832 | tf_op jit(solution)/shard_map/ppermute | solution.py:39
  23.1 13.1 %collective-permute-start.8 = (bf16[3,256,128]{2,1,0:T(8,128)(2,1)S(1)}, bf16[3,256,128]{2,1,0:T(8,128)(2,1)S(1)}, u32[]{:S(2)}, u32[]{:S(2)}) collective-permute-start(bf16[3,256,128]{2,1,0:T(8,128)(2,1)S(1)} %get-tuple-element.45), channel_id=1, source_target_pairs={{0,16},{16,0},{1,17},{17,1},{2,18},{18,2},{3,19},{19,3},{4,20},{20... | collective-permute-start | bytes 589832 | tf_op jit(solution)/shard_map/ppermute | solution.py:39
  23.2 50.5 %collective-permute-start.15 = (bf16[149,128]{1,0:T(8,128)(2,1)S(1)}, bf16[149,128]{1,0:T(8,128)(2,1)S(1)}, u32[]{:S(2)}, u32[]{:S(2)}) collective-permute-start(bf16[149,128]{1,0:T(8,128)(2,1)S(1)} %fusion.6), channel_id=1, source_target_pairs={{0,8},{16,24},{1,9},{17,25},{2,10},{18,26},{3,11},{19,27},{4,12},{... | collective-permute-start | bytes 114440 | tf_op jit(solution)/shard_map/ppermute | solution.py:39
  32.8 69.2 %copy-start.2 = (bf16[4,3,256,128]{3,2,1,0:T(8,128)(2,1)}, bf16[4,3,256,128]{3,2,1,0:T(8,128)(2,1)S(1)}, u32[]{:S(2)}) copy-start(bf16[4,3,256,128]{3,2,1,0:T(8,128)(2,1)S(1)} %pad_maximum_fusion.1.refs_0_) | copy-start | bytes 2359300
  32.8 41.3 %collective-permute-start.5 = (bf16[4,3,256,128]{3,2,1,0:T(8,128)(2,1)S(1)}, bf16[4,3,256,128]{3,2,1,0:T(8,128)(2,1)S(1)}, u32[]{:S(2)}, u32[]{:S(2)}) collective-permute-start(bf16[4,3,256,128]{3,2,1,0:T(8,128)(2,1)S(1)} %pad_maximum_fusion.1.refs_0_), channel_id=1, source_target_pairs={{0,40},{16,56},{1,41},{17,57},{2,42},{18,58},{3,43},{19,59},{4,44}... | collective-permute-start | bytes 2359304 | tf_op jit(solution)/shard_map/ppermute | solution.py:39
  36.3 24.7 %collective-permute-start.9 = (bf16[3,256,128]{2,1,0:T(8,128)(2,1)S(1)}, bf16[3,256,128]{2,1,0:T(8,128)(2,1)S(1)}, u32[]{:S(2)}, u32[]{:S(2)}) collective-permute-start(bf16[3,256,128]{2,1,0:T(8,128)(2,1)S(1)} %collective-permute-done.8), channel_id=1, source_target_pairs={{0,40},{16,56},{1,41},{17,57},{2,42},{18,58},{3,43},{19,59},{4,44}... | collective-permute-start | bytes 589832 | tf_op jit(solution)/shard_map/ppermute | solution.py:39
  37.1 23.9 %collective-permute-start.10 = (bf16[3,256,128]{2,1,0:T(8,128)(2,1)S(1)}, bf16[3,256,128]{2,1,0:T(8,128)(2,1)S(1)}, u32[]{:S(2)}, u32[]{:S(2)}) collective-permute-start(bf16[3,256,128]{2,1,0:T(8,128)(2,1)S(1)} %collective-permute-done.8), channel_id=1, source_target_pairs={{0,32},{16,48},{1,33},{17,49},{2,34},{18,50},{3,35},{19,51},{4,36}... | collective-permute-start | bytes 589832 | tf_op jit(solution)/shard_map/ppermute | solution.py:39
  37.4 28.1 %collective-permute-start.11 = (bf16[3,256,128]{2,1,0:T(8,128)(2,1)S(1)}, bf16[3,256,128]{2,1,0:T(8,128)(2,1)S(1)}, u32[]{:S(2)}, u32[]{:S(2)}) collective-permute-start(bf16[3,256,128]{2,1,0:T(8,128)(2,1)S(1)} %collective-permute-done.8), channel_id=1, source_target_pairs={{0,8},{16,24},{1,9},{17,25},{2,10},{18,26},{3,11},{19,27},{4,12},{... | collective-permute-start | bytes 589832 | tf_op jit(solution)/shard_map/ppermute | solution.py:39
  61.0 22.0 %collective-permute-start.6 = (bf16[4,3,256,128]{3,2,1,0:T(8,128)(2,1)S(1)}, bf16[4,3,256,128]{3,2,1,0:T(8,128)(2,1)}, u32[]{:S(2)}, u32[]{:S(2)}) collective-permute-start(bf16[4,3,256,128]{3,2,1,0:T(8,128)(2,1)S(1)} %pad_maximum_fusion.1.refs_0_), channel_id=1, source_target_pairs={{0,32},{16,48},{1,33},{17,49},{2,34},{18,50},{3,35},{19,51},{4,36}... | collective-permute-start | bytes 2359304 | tf_op jit(solution)/shard_map/ppermute | solution.py:39
  61.0 33.6 %collective-permute-start.7 = (bf16[4,3,256,128]{3,2,1,0:T(8,128)(2,1)S(1)}, bf16[4,3,256,128]{3,2,1,0:T(8,128)(2,1)}, u32[]{:S(2)}, u32[]{:S(2)}) collective-permute-start(bf16[4,3,256,128]{3,2,1,0:T(8,128)(2,1)S(1)} %pad_maximum_fusion.1.refs_0_), channel_id=1, source_target_pairs={{0,8},{16,24},{1,9},{17,25},{2,10},{18,26},{3,11},{19,27},{4,12},{... | collective-permute-start | bytes 2359304 | tf_op jit(solution)/shard_map/ppermute | solution.py:39
  65.6 36.4 %copy-start.3 = (bf16[4,3,256,128]{3,2,1,0:T(8,128)(2,1)}, bf16[4,3,256,128]{3,2,1,0:T(8,128)(2,1)S(1)}, u32[]{:S(2)}) copy-start(bf16[4,3,256,128]{3,2,1,0:T(8,128)(2,1)S(1)} %pad_maximum_fusion.2.refs_4_) | copy-start | bytes 2359300
  65.6 34.4 %collective-permute-start.12 = (bf16[4,3,256,128]{3,2,1,0:T(8,128)(2,1)S(1)}, bf16[4,3,256,128]{3,2,1,0:T(8,128)(2,1)}, u32[]{:S(2)}, u32[]{:S(2)}) collective-permute-start(bf16[4,3,256,128]{3,2,1,0:T(8,128)(2,1)S(1)} %pad_maximum_fusion.2.refs_4_), channel_id=1, source_target_pairs={{0,192},{16,208},{1,193},{17,209},{2,194},{18,210},{3,195},{19,211... | collective-permute-start | bytes 2359304 | tf_op jit(solution)/shard_map/ppermute | solution.py:39
  73.7 26.4 %collective-permute-start.13 = (bf16[4,3,256,128]{3,2,1,0:T(8,128)(2,1)S(1)}, bf16[4,3,256,128]{3,2,1,0:T(8,128)(2,1)}, u32[]{:S(2)}, u32[]{:S(2)}) collective-permute-start(bf16[4,3,256,128]{3,2,1,0:T(8,128)(2,1)S(1)} %pad_maximum_fusion.2.refs_4_), channel_id=1, source_target_pairs={{0,128},{16,144},{1,129},{17,145},{2,130},{18,146},{3,131},{19,147... | collective-permute-start | bytes 2359304 | tf_op jit(solution)/shard_map/ppermute | solution.py:39
  74.1 27.9 %copy-start.21 = (bf16[4,3,256,128]{3,2,1,0:T(8,128)(2,1)}, bf16[4,3,256,128]{3,2,1,0:T(8,128)(2,1)S(1)}, u32[]{:S(2)}) copy-start(bf16[4,3,256,128]{3,2,1,0:T(8,128)(2,1)S(1)} %collective-permute-done.5.refs_1_) | copy-start | bytes 2359300
  74.1 27.9 %collective-permute-start.14 = (bf16[4,3,256,128]{3,2,1,0:T(8,128)(2,1)S(1)}, bf16[4,3,256,128]{3,2,1,0:T(8,128)(2,1)}, u32[]{:S(2)}, u32[]{:S(2)}) collective-permute-start(bf16[4,3,256,128]{3,2,1,0:T(8,128)(2,1)S(1)} %pad_maximum_fusion.2.refs_4_), channel_id=1, source_target_pairs={{0,64},{16,80},{1,65},{17,81},{2,66},{18,82},{3,67},{19,83},{4,68}... | collective-permute-start | bytes 2359304 | tf_op jit(solution)/shard_map/ppermute | solution.py:39
  121.3 5.7 %collective-permute-start.16 = (bf16[4,152,128]{2,1,0:T(8,128)(2,1)}, bf16[4,152,128]{2,1,0:T(8,128)(2,1)S(1)}, u32[]{:S(2)}, u32[]{:S(2)}) collective-permute-start(bf16[4,152,128]{2,1,0:T(8,128)(2,1)} %get-tuple-element.24.refs_0_), channel_id=1, source_target_pairs={{0,192},{16,208},{1,193},{17,209},{2,194},{18,210},{3,195},{19,211... | collective-permute-start | bytes 466952 | tf_op jit(solution)/shard_map/ppermute | solution.py:39
  123.2 12.1 %collective-permute-start.17 = (bf16[4,152,128]{2,1,0:T(8,128)(2,1)}, bf16[4,152,128]{2,1,0:T(8,128)(2,1)S(1)}, u32[]{:S(2)}, u32[]{:S(2)}) collective-permute-start(bf16[4,152,128]{2,1,0:T(8,128)(2,1)} %get-tuple-element.24.refs_0_), channel_id=1, source_target_pairs={{0,128},{16,144},{1,129},{17,145},{2,130},{18,146},{3,131},{19,147... | collective-permute-start | bytes 466952 | tf_op jit(solution)/shard_map/ppermute | solution.py:39
  123.2 12.1 %collective-permute-start.18 = (bf16[4,152,128]{2,1,0:T(8,128)(2,1)}, bf16[4,152,128]{2,1,0:T(8,128)(2,1)S(1)}, u32[]{:S(2)}, u32[]{:S(2)}) collective-permute-start(bf16[4,152,128]{2,1,0:T(8,128)(2,1)} %get-tuple-element.24.refs_0_), channel_id=1, source_target_pairs={{0,64},{16,80},{1,65},{17,81},{2,66},{18,82},{3,67},{19,83},{4,68}... | collective-permute-start | bytes 466952 | tf_op jit(solution)/shard_map/ppermute | solution.py:39
  124.1 11.1 %collective-permute-start.19 = (bf16[4,152,128]{2,1,0:T(8,128)(2,1)}, bf16[4,152,128]{2,1,0:T(8,128)(2,1)S(1)}, u32[]{:S(2)}, u32[]{:S(2)}) collective-permute-start(bf16[4,152,128]{2,1,0:T(8,128)(2,1)} %get-tuple-element.25.refs_4_), channel_id=1, source_target_pairs={{0,40},{16,56},{1,41},{17,57},{2,42},{18,58},{3,43},{19,59},{4,44}... | collective-permute-start | bytes 466952 | tf_op jit(solution)/shard_map/ppermute | solution.py:39
  124.1 11.2 %collective-permute-start.20 = (bf16[4,152,128]{2,1,0:T(8,128)(2,1)}, bf16[4,152,128]{2,1,0:T(8,128)(2,1)S(1)}, u32[]{:S(2)}, u32[]{:S(2)}) collective-permute-start(bf16[4,152,128]{2,1,0:T(8,128)(2,1)} %get-tuple-element.25.refs_4_), channel_id=1, source_target_pairs={{0,32},{16,48},{1,33},{17,49},{2,34},{18,50},{3,35},{19,51},{4,36}... | collective-permute-start | bytes 466952 | tf_op jit(solution)/shard_map/ppermute | solution.py:39
  127.0 8.3 %copy-start.12 = (bf16[4,152,128]{2,1,0:T(8,128)(2,1)}, bf16[4,152,128]{2,1,0:T(8,128)(2,1)S(1)}, u32[]{:S(2)}) copy-start(bf16[4,152,128]{2,1,0:T(8,128)(2,1)S(1)} %collective-permute-done.16.refs_1_) | copy-start | bytes 466948
  127.0 8.3 %collective-permute-start.21 = (bf16[4,152,128]{2,1,0:T(8,128)(2,1)}, bf16[4,152,128]{2,1,0:T(8,128)(2,1)S(1)}, u32[]{:S(2)}, u32[]{:S(2)}) collective-permute-start(bf16[4,152,128]{2,1,0:T(8,128)(2,1)} %get-tuple-element.25.refs_4_), channel_id=1, source_target_pairs={{0,8},{16,24},{1,9},{17,25},{2,10},{18,26},{3,11},{19,27},{4,12},{... | collective-permute-start | bytes 466952 | tf_op jit(solution)/shard_map/ppermute | solution.py:39
  135.3 0.7 copy-start.13
  135.3 0.7 copy-start.14
  135.3 0.8 copy-start.15
  135.3 0.8 copy-start.16
  136.1 0.7 copy-start.17
  139.2 9.3 %collective-permute-start.22 = (bf16[4,152,128]{2,1,0:T(8,128)(2,1)}, bf16[4,152,128]{2,1,0:T(8,128)(2,1)S(1)}, u32[]{:S(2)}, u32[]{:S(2)}) collective-permute-start(bf16[4,152,128]{2,1,0:T(8,128)(2,1)} %get-tuple-element.27), channel_id=1, source_target_pairs={{0,40},{16,56},{1,41},{17,57},{2,42},{18,58},{3,43},{19,59},{4,44}... | collective-permute-start | bytes 466952 | tf_op jit(solution)/shard_map/ppermute | solution.py:39
  141.9 15.4 %collective-permute-start.23 = (bf16[4,152,128]{2,1,0:T(8,128)(2,1)}, bf16[4,152,128]{2,1,0:T(8,128)(2,1)S(1)}, u32[]{:S(2)}, u32[]{:S(2)}) collective-permute-start(bf16[4,152,128]{2,1,0:T(8,128)(2,1)} %get-tuple-element.28), channel_id=1, source_target_pairs={{0,32},{16,48},{1,33},{17,49},{2,34},{18,50},{3,35},{19,51},{4,36}... | collective-permute-start | bytes 466952 | tf_op jit(solution)/shard_map/ppermute | solution.py:39
  143.9 13.4 %collective-permute-start.24 = (bf16[4,152,128]{2,1,0:T(8,128)(2,1)}, bf16[4,152,128]{2,1,0:T(8,128)(2,1)S(1)}, u32[]{:S(2)}, u32[]{:S(2)}) collective-permute-start(bf16[4,152,128]{2,1,0:T(8,128)(2,1)} %get-tuple-element.29), channel_id=1, source_target_pairs={{0,8},{16,24},{1,9},{17,25},{2,10},{18,26},{3,11},{19,27},{4,12},{... | collective-permute-start | bytes 466952 | tf_op jit(solution)/shard_map/ppermute | solution.py:39
  145.2 12.1 %collective-permute-start.25 = (bf16[4,152,128]{2,1,0:T(8,128)(2,1)}, bf16[4,152,128]{2,1,0:T(8,128)(2,1)S(1)}, u32[]{:S(2)}, u32[]{:S(2)}) collective-permute-start(bf16[4,152,128]{2,1,0:T(8,128)(2,1)} %get-tuple-element.31), channel_id=1, source_target_pairs={{0,192},{16,208},{1,193},{17,209},{2,194},{18,210},{3,195},{19,211... | collective-permute-start | bytes 466952 | tf_op jit(solution)/shard_map/ppermute | solution.py:39
  147.4 9.9 %collective-permute-start.26 = (bf16[4,152,128]{2,1,0:T(8,128)(2,1)}, bf16[4,152,128]{2,1,0:T(8,128)(2,1)S(1)}, u32[]{:S(2)}, u32[]{:S(2)}) collective-permute-start(bf16[4,152,128]{2,1,0:T(8,128)(2,1)} %get-tuple-element.32), channel_id=1, source_target_pairs={{0,128},{16,144},{1,129},{17,145},{2,130},{18,146},{3,131},{19,147... | collective-permute-start | bytes 466952 | tf_op jit(solution)/shard_map/ppermute | solution.py:39
  148.5 8.8 %copy-start.6 = (bf16[4,152,128]{2,1,0:T(8,128)(2,1)}, bf16[4,152,128]{2,1,0:T(8,128)(2,1)S(1)}, u32[]{:S(2)}) copy-start(bf16[4,152,128]{2,1,0:T(8,128)(2,1)S(1)} %collective-permute-done.22.refs_1_) | copy-start | bytes 466948
  148.5 8.8 %collective-permute-start.27 = (bf16[4,152,128]{2,1,0:T(8,128)(2,1)}, bf16[4,152,128]{2,1,0:T(8,128)(2,1)S(1)}, u32[]{:S(2)}, u32[]{:S(2)}) collective-permute-start(bf16[4,152,128]{2,1,0:T(8,128)(2,1)} %get-tuple-element.33), channel_id=1, source_target_pairs={{0,64},{16,80},{1,65},{17,81},{2,66},{18,82},{3,67},{19,83},{4,68}... | collective-permute-start | bytes 466952 | tf_op jit(solution)/shard_map/ppermute | solution.py:39
  157.3 0.7 copy-start.7
  157.3 0.7 copy-start.8
  157.3 0.8 copy-start.9
  157.3 0.8 copy-start.10
  157.3 0.8 copy-start.11
  158.2 8.1 %copy-start.18 = (bf16[4096,16]{0,1:T(8,128)(2,1)S(1)}, bf16[4096,16]{0,1:T(8,128)(2,1)}, u32[]{:S(2)}) copy-start(bf16[4096,16]{0,1:T(8,128)(2,1)} %param.13) | copy-start | bytes 393220
  166.5 5.0 %collective-permute-start.28 = (bf16[16,4096]{1,0:T(8,128)(2,1)S(1)}, bf16[16,4096]{1,0:T(8,128)(2,1)S(1)}, u32[]{:S(2)}, u32[]{:S(2)}) collective-permute-start(bf16[16,4096]{1,0:T(8,128)(2,1)S(1)} %reshape.314), channel_id=1, source_target_pairs={{0,192},{16,208},{1,193},{17,209},{2,194},{18,210},{3,195},{19,211... | collective-permute-start | bytes 393224 | tf_op jit(solution)/shard_map/ppermute | solution.py:39
  168.1 6.5 %collective-permute-start.29 = (bf16[16,4096]{1,0:T(8,128)(2,1)S(1)}, bf16[16,4096]{1,0:T(8,128)(2,1)S(1)}, u32[]{:S(2)}, u32[]{:S(2)}) collective-permute-start(bf16[16,4096]{1,0:T(8,128)(2,1)S(1)} %reshape.314), channel_id=1, source_target_pairs={{0,128},{16,144},{1,129},{17,145},{2,130},{18,146},{3,131},{19,147... | collective-permute-start | bytes 393224 | tf_op jit(solution)/shard_map/ppermute | solution.py:39
  169.3 6.7 %collective-permute-start.30 = (bf16[16,4096]{1,0:T(8,128)(2,1)S(1)}, bf16[16,4096]{1,0:T(8,128)(2,1)S(1)}, u32[]{:S(2)}, u32[]{:S(2)}) collective-permute-start(bf16[16,4096]{1,0:T(8,128)(2,1)S(1)} %reshape.314), channel_id=1, source_target_pairs={{0,64},{16,80},{1,65},{17,81},{2,66},{18,82},{3,67},{19,83},{4,68}... | collective-permute-start | bytes 393224 | tf_op jit(solution)/shard_map/ppermute | solution.py:39
  176.1 19.7 %collective-permute-start.31 = (bf16[4,16,4096]{2,1,0:T(8,128)(2,1)S(1)}, bf16[4,16,4096]{2,1,0:T(8,128)(2,1)S(1)}, u32[]{:S(2)}, u32[]{:S(2)}) collective-permute-start(bf16[4,16,4096]{2,1,0:T(8,128)(2,1)S(1)} %get-tuple-element.42), channel_id=1, source_target_pairs={{0,40},{16,56},{1,41},{17,57},{2,42},{18,58},{3,43},{19,59},{4,44}... | collective-permute-start | bytes 1572872 | tf_op jit(solution)/shard_map/ppermute | solution.py:39
  179.2 16.6 %collective-permute-start.32 = (bf16[4,16,4096]{2,1,0:T(8,128)(2,1)S(1)}, bf16[4,16,4096]{2,1,0:T(8,128)(2,1)S(1)}, u32[]{:S(2)}, u32[]{:S(2)}) collective-permute-start(bf16[4,16,4096]{2,1,0:T(8,128)(2,1)S(1)} %get-tuple-element.42), channel_id=1, source_target_pairs={{0,32},{16,48},{1,33},{17,49},{2,34},{18,50},{3,35},{19,51},{4,36}... | collective-permute-start | bytes 1572872 | tf_op jit(solution)/shard_map/ppermute | solution.py:39
  180.7 18.4 %collective-permute-start.33 = (bf16[4,16,4096]{2,1,0:T(8,128)(2,1)S(1)}, bf16[4,16,4096]{2,1,0:T(8,128)(2,1)S(1)}, u32[]{:S(2)}, u32[]{:S(2)}) collective-permute-start(bf16[4,16,4096]{2,1,0:T(8,128)(2,1)S(1)} %get-tuple-element.42), channel_id=1, source_target_pairs={{0,8},{16,24},{1,9},{17,25},{2,10},{18,26},{3,11},{19,27},{4,12},{... | collective-permute-start | bytes 1572872 | tf_op jit(solution)/shard_map/ppermute | solution.py:39
  199.2 1.1 copy-start.1
  199.5 4.9 %copy-start = (bf16[4,4,16,4096]{3,2,1,0:T(8,128)(2,1)}, bf16[4,4,16,4096]{3,2,1,0:T(8,128)(2,1)S(1)}, u32[]{:S(2)}) copy-start(bf16[4,4,16,4096]{3,2,1,0:T(8,128)(2,1)S(1)} %pad_maximum_fusion.own_ref) | copy-start | bytes 6291460
  199.5 4.8 %collective-permute-start.34 = (bf16[4,4,16,4096]{3,2,1,0:T(8,128)(2,1)S(1)}, bf16[4,4,16,4096]{3,2,1,0:T(8,128)(2,1)}, u32[]{:S(2)}, u32[]{:S(2)}) collective-permute-start(bf16[4,4,16,4096]{3,2,1,0:T(8,128)(2,1)S(1)} %pad_maximum_fusion.own_ref), channel_id=1, source_target_pairs={{0,16},{16,0},{1,17},{17,1},{2,18},{18,2},{3,19},{19,3},{4,20},{20... | collective-permute-start | bytes 6291464 | tf_op jit(solution)/shard_map/ppermute | solution.py:39
  201.0 10.9 %collective-permute-start = (bf16[512,256]{1,0:T(8,128)(2,1)S(1)}, bf16[512,256]{1,0:T(8,128)(2,1)S(1)}, u32[]{:S(2)}, u32[]{:S(2)}) collective-permute-start(bf16[512,256]{1,0:T(8,128)(2,1)S(1)} %get-tuple-element.40), channel_id=1, source_target_pairs={{0,8},{16,24},{1,9},{17,25},{2,10},{18,26},{3,11},{19,27},{4,12},{... | collective-permute-start | bytes 786440 | tf_op jit(solution)/shard_map/ppermute | solution.py:39
  211.9 10.4 %copy-start.5 = (bf16[512,256]{1,0:T(8,128)(2,1)}, bf16[512,256]{1,0:T(8,128)(2,1)S(1)}, u32[]{:S(2)}) copy-start(bf16[512,256]{1,0:T(8,128)(2,1)S(1)} %collective-permute-done.residual_ref) | copy-start | bytes 786436
  227.8 8.7 %collective-permute-start.35 = (bf16[512,256]{1,0:T(8,128)(2,1)}, bf16[512,256]{1,0:T(8,128)(2,1)S(1)}, u32[]{:S(2)}, u32[]{:S(2)}) collective-permute-start(bf16[512,256]{1,0:T(8,128)(2,1)} %output.2), channel_id=1, source_target_pairs={{0,8},{16,24},{1,9},{17,25},{2,10},{18,26},{3,11},{19,27},{4,12},{... | collective-permute-start | bytes 786440 | tf_op jit(solution)/shard_map/ppermute | solution.py:39
Sparse Core Ops, SparseCore 0:
  18.1 57.2 all-gather.5
  166.4 55.8 all-gather.3
